TPU v7x, 256 devices: a whole 4x4x8 slice. The times are simulated.
256 devices in a mesh: blk: 2 (over y_hi), theta: 32 (over x, z), radial: 4 (over y_lo, core).
Axes of the slice: x: 4, y: 4 (y_hi: 2, y_lo: 2; y = y_hi * 2 + y_lo), z: 8, core: 2. Of those that a mesh axis runs over, the one named last changes fastest.
Arguments:
- base_state: float32 [5, 12, 32, 32768], P(None, 'blk', 'radial', 'theta'), may hold values from -4 to 12, as said below
- section_state: float32 [5, 12, 32, 32768], P(None, 'blk', 'radial', 'theta'), may hold values from -4 to 12, as said below
- rotor_step: int32 [1], replicated, may hold values from 4096 to 131071
Outputs:
- next_state: float32 [5, 12, 32, 32768], P(None, 'blk', 'radial', 'theta')
Inputs may be any that keep to these rules, and one draw needn't show every extreme that they name: `base_state`: density between 0.5 and 2, pressure between 0.5 and 2, every velocity component under 2 in magnitude. `section_state`: density between 0.5 and 2, pressure between 0.5 and 2, every velocity component under 2 in magnitude.
All inputs are finite; a program needn't handle non-finite values.
Results may differ from a plain program's by a relative error of at most 0.0003.
Values sent between devices are 32-bit elements; how exact they have to be, the bound alone decides.
A program may use at most 64 MiB of HBM per device.

v0:
```python
import jax
import jax.numpy as jnp
from jax import lax
from jax.sharding import PartitionSpec as P
from jax.experimental import pallas as pl

gamma_ratio = 1.4
weno_epsilon = 1e-06
step_ratio = 0.12


def padded_2(cells, sides, width, closed):
    for axis, dim in sides:
        count = lax.axis_size(axis)
        ends = count if closed else count - 1
        head = lax.slice_in_dim(cells, 0, width, axis=dim)
        tail = lax.slice_in_dim(cells, cells.shape[dim] - width, cells.shape[dim], axis=dim)
        cells = jnp.concatenate(
            [
                lax.ppermute(tail, axis, [(i, (i + 1) % count) for i in range(ends)]),
                cells,
                lax.ppermute(head, axis, [((i + 1) % count, i) for i in range(ends)]),
            ],
            axis=dim,
        )
    return cells


def partner(block, axis, distance):
    count = lax.axis_size(axis)
    route = []
    for low in range(count):
        high = low | 1 << distance
        if high != low and high < count:
            route += [(low, high), (high, low)]
    return lax.ppermute(block, axis, route)


def pressure_of(state):
    kinetic = 0.5 * (jnp.square(state[1]) + jnp.square(state[2]) + jnp.square(state[3])) / state[0]
    return (gamma_ratio - 1.0) * (state[4] - kinetic)


def euler_flux(state, normal):
    pressure = pressure_of(state)
    velocity = state[normal] / state[0]
    flux = state * velocity[None]
    flux = flux.at[normal].add(pressure)
    flux = flux.at[4].add(pressure * velocity)
    return flux


def wave_speed(state, normal):
    pressure = pressure_of(state)
    return jnp.abs(state[normal] / state[0]) + jnp.sqrt(gamma_ratio * pressure / state[0])


def weno_side(far_left, left_cell, centre, right_cell, far_right):
    smooth_low = 13.0 / 12.0 * jnp.square(far_left - 2.0 * left_cell + centre) + 0.25 * jnp.square(
        far_left - 4.0 * left_cell + 3.0 * centre
    )
    smooth_mid = 13.0 / 12.0 * jnp.square(
        left_cell - 2.0 * centre + right_cell
    ) + 0.25 * jnp.square(left_cell - right_cell)
    smooth_high = 13.0 / 12.0 * jnp.square(
        centre - 2.0 * right_cell + far_right
    ) + 0.25 * jnp.square(3.0 * centre - 4.0 * right_cell + far_right)
    weight_low = 0.1 / jnp.square(weno_epsilon + smooth_low)
    weight_mid = 0.6 / jnp.square(weno_epsilon + smooth_mid)
    weight_high = 0.3 / jnp.square(weno_epsilon + smooth_high)
    guess_low = (2.0 * far_left - 7.0 * left_cell + 11.0 * centre) / 6.0
    guess_mid = (-left_cell + 5.0 * centre + 2.0 * right_cell) / 6.0
    guess_high = (2.0 * centre + 5.0 * right_cell - far_right) / 6.0
    return (weight_low * guess_low + weight_mid * guess_mid + weight_high * guess_high) / (
        weight_low + weight_mid + weight_high
    )


def face_flux(padded, fluxes, axis, count, normal, first, second):
    states = [
        lax.slice_in_dim(padded, shift_index, shift_index + count + 1, axis=axis)
        for shift_index in range(6)
    ]
    physical = [
        lax.slice_in_dim(fluxes, shift_index, shift_index + count + 1, axis=axis)
        for shift_index in range(6)
    ]
    mean = 0.5 * (states[2] + states[3])
    density = mean[0]
    normal_speed = mean[normal] / density
    speed_first = mean[first] / density
    speed_second = mean[second] / density
    kinetic = 0.5 * (jnp.square(normal_speed) + jnp.square(speed_first) + jnp.square(speed_second))
    pressure = pressure_of(mean)
    sound = jnp.sqrt(gamma_ratio * pressure / density)
    enthalpy = (mean[4] + pressure) / density
    inv_sound = 1.0 / sound
    factor_one = (gamma_ratio - 1.0) * jnp.square(inv_sound)
    factor_two = factor_one * kinetic
    dissipation = jnp.maximum(wave_speed(states[2], normal), wave_speed(states[3], normal))

    def project(vector):
        dens_part = vector[0]
        norm_part = vector[normal]
        first_part = vector[first]
        second_part = vector[second]
        energy_part = vector[4]
        tangent_sum = factor_one * (
            speed_first * first_part + speed_second * second_part - energy_part
        )
        wave_minus = 0.5 * (
            (factor_two + normal_speed * inv_sound) * dens_part
            - (factor_one * normal_speed + inv_sound) * norm_part
            - tangent_sum
        )
        entropy = (
            (1.0 - factor_two) * dens_part + factor_one * normal_speed * norm_part + tangent_sum
        )
        shear_first = first_part - speed_first * dens_part
        shear_second = second_part - speed_second * dens_part
        wave_plus = 0.5 * (
            (factor_two - normal_speed * inv_sound) * dens_part
            - (factor_one * normal_speed - inv_sound) * norm_part
            - tangent_sum
        )
        return (wave_minus, entropy, shear_first, shear_second, wave_plus)

    state_chars = [project(cell_state) for cell_state in states]
    flux_chars = [project(cell_flux) for cell_flux in physical]
    recon = []
    for field_index in range(5):
        plus_vals = [
            0.5 * (flux_chars[cell][field_index] + dissipation * state_chars[cell][field_index])
            for cell in range(6)
        ]
        minus_vals = [
            0.5 * (flux_chars[cell][field_index] - dissipation * state_chars[cell][field_index])
            for cell in range(6)
        ]
        recon.append(
            weno_side(plus_vals[0], plus_vals[1], plus_vals[2], plus_vals[3], plus_vals[4])
            + weno_side(minus_vals[5], minus_vals[4], minus_vals[3], minus_vals[2], minus_vals[1])
        )
    wave_minus, entropy, shear_first, shear_second, wave_plus = recon
    acoustic = wave_minus + entropy + wave_plus
    parts = {}
    parts[0] = acoustic
    parts[normal] = (
        (normal_speed - sound) * wave_minus
        + normal_speed * entropy
        + (normal_speed + sound) * wave_plus
    )
    parts[first] = speed_first * acoustic + shear_first
    parts[second] = speed_second * acoustic + shear_second
    parts[4] = (
        (enthalpy - normal_speed * sound) * wave_minus
        + kinetic * entropy
        + speed_first * shear_first
        + speed_second * shear_second
        + (enthalpy + normal_speed * sound) * wave_plus
    )
    return jnp.stack([parts[index_part] for index_part in range(5)])


def divergence(padded, axis, count, normal, first, second):
    faces = face_flux(padded, euler_flux(padded, normal), axis, count, normal, first, second)
    return lax.slice_in_dim(faces, 1, count + 1, axis=axis) - lax.slice_in_dim(
        faces, 0, count, axis=axis
    )


def flip_radial(cells):
    turned = cells[:, :, ::-1]
    return jnp.concatenate([turned[:3], -turned[3:4], turned[4:]], axis=0)


def flip_theta(cells):
    return jnp.concatenate([cells[:2], -cells[2:3], cells[3:]], axis=0)


def hold(cells, value):
    return jnp.where(jnp.isnan(value.reshape(-1)[0]), jnp.zeros((), cells.dtype), cells)


def after(value, index):
    return index + jnp.isnan(value.reshape(-1)[0]).astype(jnp.int32)


def route_parts(rotor_step, width):
    rows = lax.axis_size("tx")
    columns = lax.axis_size("tz")
    turns = rotor_step[0] // 4 // width
    centre = (turns - 1) % (rows * columns)
    return rows, columns, centre // columns, centre % columns


def pick_column(slab, rotor_step, before):
    rows, columns, centre_row, centre_column = route_parts(rotor_step, slab.shape[3])
    source_column = (centre_column - lax.axis_index("tz")) % columns
    gathered = lax.all_gather(slab, "tz")
    return lax.dynamic_index_in_dim(gathered, after(before, source_column), 0, keepdims=False)


def pick_row(slab, rotor_step, before):
    rows, columns, centre_row, centre_column = route_parts(rotor_step, slab.shape[3])
    borrow = (lax.axis_index("tz") > centre_column).astype(jnp.int32)
    source_row = (centre_row - lax.axis_index("tx") - borrow) % rows
    gathered = lax.all_gather(slab, "tx")
    return lax.dynamic_index_in_dim(gathered, after(before, source_row), 0, keepdims=False)


def cross_blocks(slab):
    block_count = lax.axis_size("blk")
    slab_count = lax.axis_size("tx") * lax.axis_size("tz")
    this_route = []
    next_route = []
    for blk_from in range(block_count):
        blk_to = (blk_from + 1) % block_count
        for slab_from in range(slab_count):
            source = blk_from * slab_count + slab_from
            this_route.append((source, blk_to * slab_count + slab_from))
            next_route.append((source, blk_to * slab_count + (slab_from + 1) % slab_count))
    axes = ("blk", "tx", "tz")
    return lax.ppermute(slab, axes, this_route), lax.ppermute(slab, axes, next_route)


def window_of(this_slab, next_slab, rotor_step, before):
    width = this_slab.shape[3]
    remainder = after(before, rotor_step[0] // 4 % width)
    doubled = jnp.concatenate([next_slab, this_slab], axis=3)
    return lax.dynamic_slice_in_dim(doubled, width - 1 - remainder, width + 1, 3)


def axial_kernel(padded_ref, out_ref):
    padded = padded_ref[...]
    count = padded.shape[1] - 6
    pressure = pressure_of(padded)
    velocity = padded[1] / padded[0]
    parts = [padded[index_part] * velocity for index_part in range(5)]
    parts[1] = parts[1] + pressure
    parts[4] = parts[4] + pressure * velocity
    faces = face_flux(padded, jnp.stack(parts), 1, count, 1, 2, 3)
    out_ref[...] = faces


def axial_faces(padded):
    components, planes, bands, width = padded.shape
    lanes = 128
    block = (components, planes, bands, lanes)
    out_block = (components, planes - 5, bands, lanes)
    return pl.pallas_call(
        axial_kernel,
        grid=(width // lanes,),
        in_specs=[pl.BlockSpec(block, lambda i: (0, 0, 0, i))],
        out_specs=pl.BlockSpec(out_block, lambda i: (0, 0, 0, i)),
        out_shape=jax.ShapeDtypeStruct((components, planes - 5, bands, width), padded.dtype),
    )(padded)


def shards(base_state, section_state, rotor_step):
    planes = section_state.shape[1]
    bands = section_state.shape[2]
    width = section_state.shape[3]
    fraction = (rotor_step[0] % 4).astype(jnp.float32) / 4.0
    theta_padded = padded_2(section_state, ((("tx", "tz"), 3),), 3, True)
    radial_raw = padded_2(section_state, (("radial", 2),), 3, False)
    band_index = lax.axis_index("radial")
    band_count = lax.axis_size("radial")
    lower_wall = jnp.where(
        band_index == 0, flip_radial(section_state[:, :, :3]), radial_raw[:, :, :3]
    )
    upper_wall = jnp.where(
        band_index == band_count - 1, flip_radial(section_state[:, :, -3:]), radial_raw[:, :, -3:]
    )
    radial_padded = jnp.concatenate([lower_wall, section_state, upper_wall], axis=2)
    block_index = lax.axis_index("blk")
    front = block_index == 0
    outgoing = jnp.where(front, section_state[:, -3:], section_state[:, :3])[..., ::-1]
    radial = divergence(radial_padded, 2, bands, 3, 1, 2)
    chosen = pick_column(outgoing, rotor_step, radial)
    theta_padded = hold(theta_padded, chosen)
    azimuthal = divergence(theta_padded, 3, width, 2, 1, 3)
    chosen = pick_row(chosen, rotor_step, azimuthal)
    this_slab, next_slab = cross_blocks(chosen)
    edge_low = jnp.concatenate(
        [section_state[:, :1], section_state[:, :1], section_state[:, :1]], axis=1
    )
    edge_high = jnp.concatenate(
        [section_state[:, -1:], section_state[:, -1:], section_state[:, -1:]], axis=1
    )
    local_window = jnp.where(
        front,
        jnp.concatenate([edge_low, section_state], axis=1),
        jnp.concatenate([section_state, edge_high], axis=1),
    )
    local_window = hold(local_window, chosen)
    local_faces = axial_faces(local_window)
    window = window_of(this_slab, next_slab, rotor_step, local_faces)
    ghost = flip_theta(
        (1.0 - fraction) * window[..., 1 : width + 1] + fraction * window[..., :width]
    )
    mortar_window = jnp.where(
        front,
        jnp.concatenate([section_state[:, 1:], ghost], axis=1),
        jnp.concatenate([ghost, section_state[:, :-1]], axis=1),
    )
    mortar_faces = axial_faces(mortar_window)
    faces = jnp.where(
        front,
        jnp.concatenate([local_faces, mortar_faces], axis=1),
        jnp.concatenate([mortar_faces, local_faces], axis=1),
    )
    axial = lax.slice_in_dim(faces, 1, planes + 1, axis=1) - lax.slice_in_dim(
        faces, 0, planes, axis=1
    )
    change = -step_ratio * (axial + radial + azimuthal)
    return 0.75 * base_state + 0.25 * (section_state + change)


def solution(mesh):
    blocks, slabs, bands = (mesh.shape[name] for name in ("blk", "theta", "radial"))
    rows = 4 if slabs % 4 == 0 else 1
    grid = jax.sharding.Mesh(
        mesh.devices.reshape(blocks, rows, slabs // rows, bands), ("blk", "tx", "tz", "radial")
    )
    in_specs = (P(None, "blk", "radial", ("tx", "tz")), P(None, "blk", "radial", ("tx", "tz")), P())
    out_specs = P(None, "blk", "radial", ("tx", "tz"))
    inner = jax.shard_map(shards, mesh=grid, in_specs=in_specs, out_specs=out_specs, check_vma=False)
    sharded = jax.sharding.NamedSharding(mesh, P(None, "blk", "radial", "theta"))

    def run(base_state, section_state, rotor_step):
        return jax.lax.with_sharding_constraint(
            inner(base_state, section_state, rotor_step), sharded
        )

    return run
```

profile of v0, /device:TPU:1, one launch (start us, length us, event | category | flops | bytes accessed | tf_op | source)
XLA Modules:
  0.0 160.9 jit_solution(13041949293229279393)
XLA Ops:
  6.5 2.6 %fusion.238 = (f32[5,6,3,1024]{3,2,1,0:T(4,128)}, f32[5,6,3,1024]{3,2,1,0:T(4,128)S(1)}) fusion(f32[5,6,8,1024]{3,2,1,0:T(8,128)} %param.12), kind=kLoop, calls=%fused_computation.447 | loop fusion | bytes 1474560 | tf_op jit(solution)/shard_map/slice | solution.py:17
  9.1 4.6 %collective-permute-start = (f32[5,6,3,1024]{3,2,1,0:T(4,128)}, f32[5,6,3,1024]{3,2,1,0:T(4,128)}, u32[]{:S(2)}, u32[]{:S(2)}) collective-permute-start(f32[5,6,3,1024]{3,2,1,0:T(4,128)} %get-tuple-element.135), channel_id=1, source_target_pairs={{0,1},{1,2},{2,3},{4,5},{5,6},{6,7},{8,9},{9,10},{10,11},{12,13},{... | collective-permute-start | bytes 1105928 | tf_op jit(solution)/shard_map/ppermute | solution.py:20
  13.7 2.7 %collective-permute-start.1 = (f32[5,6,3,1024]{3,2,1,0:T(4,128)S(1)}, f32[5,6,3,1024]{3,2,1,0:T(4,128)}, u32[]{:S(2)}, u32[]{:S(2)}) collective-permute-start(f32[5,6,3,1024]{3,2,1,0:T(4,128)S(1)} %get-tuple-element.136), channel_id=1, source_target_pairs={{1,0},{2,1},{3,2},{5,4},{6,5},{7,6},{9,8},{10,9},{11,10},{13,12},{... | collective-permute-start | bytes 1105928 | tf_op jit(solution)/shard_map/ppermute | solution.py:22
  16.5 3.0 %rev.2 = f32[5,3,8,1024]{3,2,1,0:T(8,128)} reverse(f32[5,3,8,1024]{3,2,1,0:T(8,128)S(1)} %slice_select_fusion), dimensions={3} | reverse | bytes 983040 | tf_op jit(solution)/shard_map/rev | solution.py:278
  19.6 0.1 fusion.239
  19.7 1.0 collective-permute-start.2
  20.6 6.2 %collective-permute-start.3 = (f32[5,6,8,3]{3,2,1,0:T(8,128)S(1)}, f32[5,6,8,3]{3,2,1,0:T(8,128)}, u32[]{:S(2)}, u32[]{:S(2)}) collective-permute-start(f32[5,6,8,3]{3,2,1,0:T(8,128)S(1)} %get-tuple-element.137), channel_id=1, source_target_pairs={{4,0},{8,4},{12,8},{16,12},{20,16},{24,20},{28,24},{32,28},{36,32}... | collective-permute-start | bytes 8648 | tf_op jit(solution)/shard_map/ppermute | solution.py:22
  26.9 1.4 fusion.234
  28.3 0.1 fusion.236
  29.3 0.3 slice.887
  29.6 2.6 %slice.889 = f32[1,6,3,1024]{3,2,1,0:T(4,128)} reverse(f32[1,6,3,1024]{3,2,1,0:T(4,128)S(1)} %get-tuple-element.134), dimensions={2} | reverse | bytes 147456 | tf_op jit(solution)/shard_map/slice | solution.py:174
  32.2 0.5 slice.885
  32.8 0.3 slice.895
  33.1 0.3 slice.897
  33.5 0.5 slice.893
  34.1 1.5 concatenate.59
  35.7 1.2 maximum_select_fusion.3
  36.9 1.2 maximum_select_fusion.4
  38.1 0.4 pad_maximum_fusion
  38.5 0.4 fusion.2
  39.0 0.4 broadcast_multiply_fusion
  39.5 0.2 slice_add_fusion.2
  39.7 0.1 slice_add_fusion.1
  39.8 12.4 %constant_dynamic-update-slice_fusion = (f32[5,6,9,1024]{3,2,1,0:T(8,128)S(1)}, f32[1,6,9,1024]{3,2,1,0:T(8,128)S(1)}, f32[1,6,9,1024]{3,2,1,0:T(8,128)S(1)}, f3...) fusion(f32[1,6,14,1024]{3,2,1,0:T(8,128)S(1)} %get-tuple-elemen, ...), kind=kLoop, calls=%fused_computation.413 | loop fusion | flops 42190848 | bytes 22044672
  52.2 2.8 %add_dynamic-update-slice_fusion.3 = (f32[5,6,9,1024]{3,2,1,0:T(8,128)S(1)}, f32[1,6,9,1024]{3,2,1,0:T(8,128)S(1)}) fusion(f32[5,6,9,1024]{3,2,1,0:T(8,128)S(1)} %get-tuple-element.91, f32[1,6,9,1024]{3,2,1,0:T(8,128)S(1)} %get-tuple-element.108, f32[1,6,9,1024]{3,2,1,0:T(8,128)S(1)} %get-tuple-element.92, f32[1,6,9,1024]{3,2,1,0:T(8,128)S(1)} %get-tuple-element.118, ...), kind=kLoop, calls=%fused_computation.174 | loop fusion | flops 9897984 | bytes 11010048
  55.1 2.8 %add_dynamic-update-slice_fusion.2 = (f32[5,6,9,1024]{3,2,1,0:T(8,128)S(1)}, f32[1,6,9,1024]{3,2,1,0:T(8,128)S(1)}) fusion(f32[5,6,9,1024]{3,2,1,0:T(8,128)S(1)} %get-tuple-element.89, f32[1,6,9,1024]{3,2,1,0:T(8,128)S(1)} %get-tuple-element.109, f32[1,6,9,1024]{3,2,1,0:T(8,128)S(1)} %get-tuple-element.92, f32[1,6,9,1024]{3,2,1,0:T(8,128)S(1)} %get-tuple-element.118, ...), kind=kLoop, calls=%fused_computation.166 | loop fusion | flops 9897984 | bytes 11010048
  57.9 9.8 %add_dynamic-update-slice_fusion.1 = (f32[5,6,9,1024]{3,2,1,0:T(8,128)S(1)}, f32[1,6,9,1024]{3,2,1,0:T(8,128)S(1)}, f32[1,6,9,1024]{3,2,1,0:T(8,128)S(1)}, f32[1,6,9,1024]{3,2,1,0:T(8,128)S(1)}) fusion(f32[5,6,9,1024]{3,2,1,0:T(8,128)S(1)} %get-tuple-element.87, f32[1,6,9,1024]{3,2,1,0:T(8,128)S(1)} %get-tuple-element.95, ...), kind=kLoop, calls=%fused_computation.143 | loop fusion | flops 35665920 | bytes 17694720
  67.7 0.5 add_dynamic-update-slice_fusion
  68.3 0.2 slice_subtract_fusion.2
  68.4 0.2 copy.4
  68.6 0.9 copy-done.1
  69.5 0.5 slice.1172
  71.2 2.8 %all-gather.6.cloned.1.call-done = f32[40,3,8,1024]{3,2,1,0:T(8,128)} async-done(((f32[5,3,8,1024]{3,2,1,0:T(8,128)}), f32[40,3,8,1024]{3,2,1,0:T(8,128)}) %all-gather.6.cloned.1.call-update) | async-done | bytes 3932176 | tf_op jit(solution)/shard_map/all_gather | solution.py:200
  74.0 1.1 constant_dynamic-slice_fusion.1
  75.1 0.6 slice.1173
  77.1 1.6 %fusion.5 = f32[5,6,8,1025]{3,2,1,0:T(8,128)} fusion(f32[5,6,8,1030]{3,2,1,0:T(8,128)S(1)} %broadcast_select_fusion), kind=kLoop, calls=%fused_computation.70 | loop fusion | flops 492000 | bytes 2952000 | tf_op jit(solution)/shard_map/mul | solution.py:88
  78.9 0.1 slice_add_fusion.4
  79.0 1.1 copy-done.3
  80.1 6.4 %constant_dynamic-update-slice_fusion.1 = (f32[5,6,8,1025]{3,2,1,0:T(8,128)S(1)}, f32[1,6,8,1025]{3,2,1,0:T(8,128)S(1)}, f32[1,6,8,1025]{3,2,1,0:T(8,128)S(1)}, ...) fusion(f32[5,6,8,1030]{3,2,1,0:T(8,128)S(1)} %broadcast_select_, ...), kind=kLoop, calls=%fused_computation.414 | loop fusion | flops 35768400 | bytes 17215680
  86.5 1.5 add_dynamic-update-slice_fusion.7
  88.0 5.7 %add_dynamic-update-slice_fusion.6 = (f32[5,6,8,1025]{3,2,1,0:T(8,128)S(1)}, f32[1,6,8,1025]{3,2,1,0:T(8,128)S(1)}, f32[1,6,8,1025]{3,2,1,0:T(8,128)S(1)}, f32[1,6,8,1025]{3,2,1,0:T(8,128)S(1)}) fusion(f32[5,6,8,1025]{3,2,1,0:T(8,128)S(1)} %get-tuple-element.59, f32[1,6,8,1025]{3,2,1,0:T(8,128)S(1)} %get-tuple-element.65, ...), kind=kLoop, calls=%fused_computation.296 | loop fusion | flops 31734000 | bytes 9953280
  93.7 1.5 add_dynamic-update-slice_fusion.5
  95.3 0.3 add_dynamic-update-slice_fusion.4
  95.5 0.3 slice_subtract_fusion.1
  95.9 0.2 copy.6
  96.1 0.5 slice.1250
  97.7 12.1 %all-gather.4.cloned.1.call-done = f32[4,5,3,8,1024]{4,3,2,1,0:T(8,128)} async-done(((f32[1,5,3,8,1024]{4,3,2,1,0:T(8,128)}), f32[4,5,3,8,1024]{4,3,2,1,0:T(8,128)}) %all-gather.4.cloned.1.call-update) | async-done | bytes 1966096 | tf_op jit(solution)/shard_map/all_gather | solution.py:208
  109.8 1.1 fusion.241
  110.9 3.8 %collective-permute-start.4 = (f32[5,3,8,1024]{3,2,1,0:T(8,128)S(1)}, f32[5,3,8,1024]{3,2,1,0:T(8,128)S(1)}, u32[]{:S(2)}, u32[]{:S(2)}) collective-permute-start(f32[5,3,8,1024]{3,2,1,0:T(8,128)S(1)} %fusion.241), channel_id=1, source_target_pairs={{0,132},{4,136},{8,140},{12,144},{16,148},{20,152},{24,156},{28,16... | collective-permute-start | bytes 1474568 | tf_op jit(solution)/shard_map/ppermute | solution.py:224
  114.7 0.2 collective-permute-start.5
  114.9 1.1 constant_dynamic-slice_fusion
  116.1 0.5 slice.1251
  117.9 1.4 fusion.4.padded_ref
  119.3 7.9 %shard_map.37 = f32[5,4,8,1024]{3,2,1,0:T(8,128)} custom-call(f32[5,9,8,1024]{3,2,1,0:T(8,128)} %fusion.4.padded_ref), custom_call_target="tpu_custom_call" | custom-call | tf_op jit(solution)/shard_map/pallas_call | solution.py:251
  127.2 1.2 copy.8
  128.4 0.6 slice.1252
  130.4 9.1 %collective-permute-done.5 = f32[5,3,8,1024]{3,2,1,0:T(8,128)} collective-permute-done((f32[5,3,8,1024]{3,2,1,0:T(8,128)S(1)}, f32[5,3,8,1024]{3,2,1,0:T(8,128)}, u32[]{:S(2)}, u32[]{:S(2)}) %collective-permute-start.5) | collective-permute-done | bytes 491552 | tf_op jit(solution)/shard_map/ppermute | solution.py:224
  139.4 1.2 fusion.12
  140.7 0.2 fusion.13
  141.0 1.2 maximum_select_fusion.1.padded_ref
  142.2 7.1 %shard_map.38 = f32[5,3,8,1024]{3,2,1,0:T(8,128)} custom-call(f32[5,8,8,1024]{3,2,1,0:T(8,128)} %maximum_select_fusion.1.padded_ref), custom_call_target="tpu_custom_call" | custom-call | tf_op jit(solution)/shard_map/pallas_call | solution.py:251
  149.3 1.5 maximum_select_fusion.2
  150.7 0.4 copy-done.2
  151.1 2.9 %fusion.11 = f32[5,6,8,1024]{3,2,1,0:T(8,128)} fusion(f32[5,6,8,1024]{3,2,1,0:T(8,128)S(1)} %copy-done, f32[5,7,8,1024]{3,2,1,0:T(8,128)S(1)} %maximum_select_fusion.2, f32[5,6,8,1024]{3,2,1,0:T(8,128)} %param.11, f32[5,6,8,1025]{3,2,1,0:T(8,128)S(1)} %add_dynamic-update-slice_fusion.4, f32[5,6,9,1024]{3,2,1,0:T(8,128)S(1)} %copy-done.2), kind=kLoop, calls=%fused_computation.77 | loop fusion | flops 2457600 | bytes 8847360 | tf_op jit(solution)/shard_map/add | solution.py:317
  (36 shorter events, 0.8 us)
Async XLA Ops:
  6.5 9.9 %copy-start = (f32[5,6,8,1024]{3,2,1,0:T(8,128)S(1)}, f32[5,6,8,1024]{3,2,1,0:T(8,128)}, u32[]{:S(2)}) copy-start(f32[5,6,8,1024]{3,2,1,0:T(8,128)} %param.12) | copy-start | bytes 2949124
  6.5 67.4 %all-gather.6.cloned.1.call-start = ((), (), s32[]{:S(2)}) async-start(), calls=%async_computation.1 | async-start | bytes 4423680 | tf_op jit(solution)/shard_map/all_gather | solution.py:200
  9.1 26.5 %collective-permute-start = (f32[5,6,3,1024]{3,2,1,0:T(4,128)}, f32[5,6,3,1024]{3,2,1,0:T(4,128)}, u32[]{:S(2)}, u32[]{:S(2)}) collective-permute-start(f32[5,6,3,1024]{3,2,1,0:T(4,128)} %get-tuple-element.135), channel_id=1, source_target_pairs={{0,1},{1,2},{2,3},{4,5},{5,6},{6,7},{8,9},{9,10},{10,11},{12,13},{... | collective-permute-start | bytes 1105928 | tf_op jit(solution)/shard_map/ppermute | solution.py:20
  13.7 23.2 %collective-permute-start.1 = (f32[5,6,3,1024]{3,2,1,0:T(4,128)S(1)}, f32[5,6,3,1024]{3,2,1,0:T(4,128)}, u32[]{:S(2)}, u32[]{:S(2)}) collective-permute-start(f32[5,6,3,1024]{3,2,1,0:T(4,128)S(1)} %get-tuple-element.136), channel_id=1, source_target_pairs={{1,0},{2,1},{3,2},{5,4},{6,5},{7,6},{9,8},{10,9},{11,10},{13,12},{... | collective-permute-start | bytes 1105928 | tf_op jit(solution)/shard_map/ppermute | solution.py:22
  19.5 90.3 %all-gather.4.cloned.1.call-start = ((), (), s32[]{:S(2)}) async-start(), calls=%async_computation | async-start | bytes 2457600 | tf_op jit(solution)/shard_map/all_gather | solution.py:208
  19.7 14.4 %collective-permute-start.2 = (f32[5,6,8,3]{3,2,1,0:T(8,128)S(1)}, f32[5,6,8,3]{3,2,1,0:T(8,128)}, u32[]{:S(2)}, u32[]{:S(2)}) collective-permute-start(f32[5,6,8,3]{3,2,1,0:T(8,128)S(1)} %get-tuple-element.138), channel_id=1, source_target_pairs={{0,4},{4,8},{8,12},{12,16},{16,20},{20,24},{24,28},{28,32},{32,36}... | collective-permute-start | bytes 8648 | tf_op jit(solution)/shard_map/ppermute | solution.py:20
  20.6 13.4 %collective-permute-start.3 = (f32[5,6,8,3]{3,2,1,0:T(8,128)S(1)}, f32[5,6,8,3]{3,2,1,0:T(8,128)}, u32[]{:S(2)}, u32[]{:S(2)}) collective-permute-start(f32[5,6,8,3]{3,2,1,0:T(8,128)S(1)} %get-tuple-element.137), channel_id=1, source_target_pairs={{4,0},{8,4},{12,8},{16,12},{20,16},{24,20},{28,24},{32,28},{36,32}... | collective-permute-start | bytes 8648 | tf_op jit(solution)/shard_map/ppermute | solution.py:22
  68.2 1.3 copy-start.1
  75.0 1.9 %copy-start.5 = (f32[1,5,3,8,1024]{4,3,2,1,0:T(8,128)}, f32[1,5,3,8,1024]{4,3,2,1,0:T(8,128)S(1)}, u32[]{:S(2)}) copy-start(f32[1,5,3,8,1024]{4,3,2,1,0:T(8,128)S(1)} %constant_dynamic-slice_fusion.1) | copy-start | bytes 1474564
  78.9 1.2 copy-start.3
  110.9 19.5 %collective-permute-start.4 = (f32[5,3,8,1024]{3,2,1,0:T(8,128)S(1)}, f32[5,3,8,1024]{3,2,1,0:T(8,128)S(1)}, u32[]{:S(2)}, u32[]{:S(2)}) collective-permute-start(f32[5,3,8,1024]{3,2,1,0:T(8,128)S(1)} %fusion.241), channel_id=1, source_target_pairs={{0,132},{4,136},{8,140},{12,144},{16,148},{20,152},{24,156},{28,16... | collective-permute-start | bytes 1474568 | tf_op jit(solution)/shard_map/ppermute | solution.py:224
  114.7 24.7 %collective-permute-start.5 = (f32[5,3,8,1024]{3,2,1,0:T(8,128)S(1)}, f32[5,3,8,1024]{3,2,1,0:T(8,128)}, u32[]{:S(2)}, u32[]{:S(2)}) collective-permute-start(f32[5,3,8,1024]{3,2,1,0:T(8,128)S(1)} %fusion.241), channel_id=1, source_target_pairs={{0,128},{4,132},{8,136},{12,140},{16,144},{20,148},{24,152},{28,15... | collective-permute-start | bytes 1474568 | tf_op jit(solution)/shard_map/ppermute | solution.py:224
  130.3 10.6 %copy-start.6 = (f32[5,5,8,1024]{3,2,1,0:T(8,128)S(1)}, f32[5,5,8,1024]{3,2,1,0:T(8,128)}, u32[]{:S(2)}) copy-start(f32[5,5,8,1024]{3,2,1,0:T(8,128)} %get-tuple-element.125) | copy-start | bytes 2457604
  130.3 10.6 %copy-start.7 = (f32[5,5,8,1024]{3,2,1,0:T(8,128)S(1)}, f32[5,5,8,1024]{3,2,1,0:T(8,128)}, u32[]{:S(2)}) copy-start(f32[5,5,8,1024]{3,2,1,0:T(8,128)} %get-tuple-element.126) | copy-start | bytes 2457604
  140.9 8.3 %copy-start.4 = (f32[5,4,8,1024]{3,2,1,0:T(8,128)S(1)}, f32[5,4,8,1024]{3,2,1,0:T(8,128)}, u32[]{:S(2)}) copy-start(f32[5,4,8,1024]{3,2,1,0:T(8,128)} %shard_map.37) | copy-start | bytes 1966084
  149.3 1.8 %copy-start.2 = (f32[5,6,9,1024]{3,2,1,0:T(8,128)S(1)}, f32[5,6,9,1024]{3,2,1,0:T(8,128)}, u32[]{:S(2)}) copy-start(f32[5,6,9,1024]{3,2,1,0:T(8,128)} %copy-done.1) | copy-start | bytes 3317764
Sparse Core Ops, SparseCore 0:
  19.6 54.2 all-gather.5
  78.9 30.8 all-gather.3
where the time goes:
time: 162 us; the launch traced here: 161 us
  other arithmetic  59 us (36%)
  waiting for transfers between devices  24 us (15%)
  local copies, waits for them, and re-layouts  23.6 us (15%)
  between operations  20.8 us (13%)
  starting transfers between devices  18.5 us (11%)
  Pallas kernels  15 us (9%)
    unnamed x8, other arithmetic  43 us
    pallas_call x2, Pallas kernels, axial_faces(): pl.pallas_call(axial_kernel, grid=(width // lanes,), in_specs=[pl.BlockSp...  15 us
    all_gather x1, waiting for transfers between devices, pick_row(): gathered = lax.all_gather(slab, 'tx')  12.1 us
    ppermute x1, waiting for transfers between devices, cross_blocks(): lax.ppermute(slab, axes, this_route)  9.07 us
    ppermute x2, starting transfers between devices, padded_2(): lax.ppermute(head, axis, [((i + 1) % count, i) for i in range(ends)])  8.89 us
    ppermute x2, starting transfers between devices, padded_2(): lax.ppermute(tail, axis, [(i, (i + 1) % count) for i in range(ends)])  5.56 us
    slice x8, local copies, waits for them, and re-layouts, flip_radial(): return jnp.concatenate([turned[:3], -turned[3:4], turned[4:]], axis=0)  4.86 us
    unnamed x21, local copies, waits for them, and re-layouts  4.15 us
  transfers between devices with their start and end apart: 8, of which 3 were waited for; matrix products, arithmetic and copies ran while one was open for 41% of the time, Pallas kernels for 5%

commit v1 on v0

--- a/solution.py
+++ b/solution.py
@@ -194,10 +194,9 @@
     return rows, columns, centre // columns, centre % columns
 
 
-def pick_column(slab, rotor_step, before):
-    rows, columns, centre_row, centre_column = route_parts(rotor_step, slab.shape[3])
+def pick_column(gathered, rotor_step, before):
+    rows, columns, centre_row, centre_column = route_parts(rotor_step, gathered.shape[4])
     source_column = (centre_column - lax.axis_index("tz")) % columns
-    gathered = lax.all_gather(slab, "tz")
     return lax.dynamic_index_in_dim(gathered, after(before, source_column), 0, keepdims=False)
 
 
@@ -262,8 +261,12 @@
     bands = section_state.shape[2]
     width = section_state.shape[3]
     fraction = (rotor_step[0] % 4).astype(jnp.float32) / 4.0
-    theta_padded = padded_2(section_state, ((("tx", "tz"), 3),), 3, True)
-    radial_raw = padded_2(section_state, (("radial", 2),), 3, False)
+    front = lax.axis_index("blk") == 0
+    outgoing = jnp.where(front, section_state[:, -3:], section_state[:, :3])[..., ::-1]
+    gathered = lax.all_gather(outgoing, "tz")
+    halo_state = hold(section_state, outgoing)
+    theta_padded = padded_2(halo_state, ((("tx", "tz"), 3),), 3, True)
+    radial_raw = padded_2(halo_state, (("radial", 2),), 3, False)
     band_index = lax.axis_index("radial")
     band_count = lax.axis_size("radial")
     lower_wall = jnp.where(
@@ -275,9 +278,8 @@
     radial_padded = jnp.concatenate([lower_wall, section_state, upper_wall], axis=2)
     block_index = lax.axis_index("blk")
     front = block_index == 0
-    outgoing = jnp.where(front, section_state[:, -3:], section_state[:, :3])[..., ::-1]
     radial = divergence(radial_padded, 2, bands, 3, 1, 2)
-    chosen = pick_column(outgoing, rotor_step, radial)
+    chosen = pick_column(gathered, rotor_step, radial)
     theta_padded = hold(theta_padded, chosen)
     azimuthal = divergence(theta_padded, 3, width, 2, 1, 3)
     chosen = pick_row(chosen, rotor_step, azimuthal)

time: 162 us -> 169 us (1.043)
  local copies, waits for them, and re-layouts: 23.6 us -> 29.7 us
  waiting for transfers between devices: 24 us -> 20.5 us
  other arithmetic: 59 us -> 61.6 us
  between operations: 20.8 us -> 22.5 us
    slice x8, local copies, waits for them, and re-layouts: 4.86 us -> 9.25 us  [flip_radial(): return jnp.concatenate([turned[:3], -turned[3:4], turned[4:]], axis=0)]
    all_gather x1, waiting for transfers between devices: 2.77 us -> 0.02 us  [shards(): gathered = lax.all_gather(outgoing, 'tz')]
    unnamed x21 -> x26, local copies, waits for them, and re-layouts: 4.15 us -> 5.99 us
  transfers between devices with their start and end apart: 8 -> 8, of which waited for: 3 -> 2; matrix products, arithmetic and copies ran while one was open for 41% -> 43% of each run, Pallas kernels for 5% -> 5%
where the time goes in v1:
time: 169 us; the launch traced here: 168 us
  other arithmetic  61.6 us (36%)
  local copies, waits for them, and re-layouts  29.7 us (18%)
  between operations  22.5 us (13%)
  waiting for transfers between devices  20.5 us (12%)
  starting transfers between devices  18.3 us (11%)
  Pallas kernels  15 us (9%)
    unnamed x8, other arithmetic  43 us
    pallas_call x2, Pallas kernels, axial_faces(): pl.pallas_call(axial_kernel, grid=(width // lanes,), in_specs=[pl.BlockSp...  15 us
    all_gather x1, waiting for transfers between devices, pick_row(): gathered = lax.all_gather(slab, 'tx')  11.4 us
    slice x8, local copies, waits for them, and re-layouts, flip_radial(): return jnp.concatenate([turned[:3], -turned[3:4], turned[4:]], axis=0)  9.25 us
    ppermute x1, waiting for transfers between devices, cross_blocks(): lax.ppermute(slab, axes, this_route)  9.06 us
    ppermute x2, starting transfers between devices, padded_2(): lax.ppermute(head, axis, [((i + 1) % count, i) for i in range(ends)])  8.77 us
    unnamed x26, local copies, waits for them, and re-layouts  5.99 us
    ppermute x2, starting transfers between devices, padded_2(): lax.ppermute(tail, axis, [(i, (i + 1) % count) for i in range(ends)])  5.51 us
  transfers between devices with their start and end apart: 8, of which 2 were waited for; matrix products, arithmetic and copies ran while one was open for 43% of the time, Pallas kernels for 5%

profile of v1, /device:TPU:1, one launch (start us, length us, event | category | flops | bytes accessed | tf_op | source)
XLA Modules:
  0.0 167.7 jit_solution(5033145508905354908)
XLA Ops:
  6.5 1.3 slice_select_fusion
  7.9 3.0 %rev.2 = f32[5,3,8,1024]{3,2,1,0:T(8,128)} reverse(f32[5,3,8,1024]{3,2,1,0:T(8,128)S(1)} %slice_select_fusion), dimensions={3} | reverse | bytes 983040 | tf_op jit(solution)/shard_map/rev | solution.py:265
  11.0 1.1 copy.4
  12.1 0.5 slice.1072
  14.0 1.3 fusion.238
  15.3 4.6 %collective-permute-start = (f32[5,6,3,1024]{3,2,1,0:T(4,128)}, f32[5,6,3,1024]{3,2,1,0:T(4,128)}, u32[]{:S(2)}, u32[]{:S(2)}) collective-permute-start(f32[5,6,3,1024]{3,2,1,0:T(4,128)} %get-tuple-element.135), channel_id=1, source_target_pairs={{0,1},{1,2},{2,3},{4,5},{5,6},{6,7},{8,9},{9,10},{10,11},{12,13},{... | collective-permute-start | bytes 1105928 | tf_op jit(solution)/shard_map/ppermute | solution.py:20
  19.9 2.6 %collective-permute-start.1 = (f32[5,6,3,1024]{3,2,1,0:T(4,128)}, f32[5,6,3,1024]{3,2,1,0:T(4,128)}, u32[]{:S(2)}, u32[]{:S(2)}) collective-permute-start(f32[5,6,3,1024]{3,2,1,0:T(4,128)} %get-tuple-element.136), channel_id=1, source_target_pairs={{1,0},{2,1},{3,2},{5,4},{6,5},{7,6},{9,8},{10,9},{11,10},{13,12},{... | collective-permute-start | bytes 1105928 | tf_op jit(solution)/shard_map/ppermute | solution.py:22
  22.5 0.8 fusion.239
  23.2 0.9 collective-permute-start.2
  24.2 6.1 %collective-permute-start.3 = (f32[5,6,8,3]{3,2,1,0:T(8,128)}, f32[5,6,8,3]{3,2,1,0:T(8,128)}, u32[]{:S(2)}, u32[]{:S(2)}) collective-permute-start(f32[5,6,8,3]{3,2,1,0:T(8,128)} %get-tuple-element.137), channel_id=1, source_target_pairs={{4,0},{8,4},{12,8},{16,12},{20,16},{24,20},{28,24},{32,28},{36,32}... | collective-permute-start | bytes 8648 | tf_op jit(solution)/shard_map/ppermute | solution.py:22
  30.3 1.4 fusion.234
  32.7 0.3 slice.890
  33.0 0.7 neg.169
  33.7 2.5 %slice.892 = f32[1,6,3,1024]{3,2,1,0:T(4,128)} reverse(f32[1,6,3,1024]{3,2,1,0:T(4,128)S(1)} %get-tuple-element.134), dimensions={2} | reverse | bytes 147456 | tf_op jit(solution)/shard_map/slice | solution.py:174
  36.2 0.5 slice.888
  36.8 0.3 slice.899
  37.1 0.7 neg.170
  37.8 2.5 %slice.901 = f32[1,6,3,1024]{3,2,1,0:T(4,128)} reverse(f32[1,6,3,1024]{3,2,1,0:T(4,128)S(1)} %get-tuple-element.132), dimensions={2} | reverse | bytes 147456 | tf_op jit(solution)/shard_map/slice | solution.py:174
  40.3 2.8 %slice.897 = f32[3,6,3,1024]{3,2,1,0:T(4,128)} reverse(f32[3,6,3,1024]{3,2,1,0:T(4,128)S(1)} %get-tuple-element.130), dimensions={2} | reverse | bytes 442368 | tf_op jit(solution)/shard_map/slice | solution.py:174
  43.1 0.6 copy-done.9
  43.7 1.4 concatenate.59
  45.2 1.3 maximum_select_fusion.3
  46.5 1.4 maximum_select_fusion.4
  47.9 0.4 pad_maximum_fusion
  48.3 0.4 fusion.2
  48.8 0.4 broadcast_multiply_fusion
  49.2 0.2 slice_add_fusion.2
  49.5 12.4 %constant_dynamic-update-slice_fusion = (f32[5,6,9,1024]{3,2,1,0:T(8,128)S(1)}, f32[1,6,9,1024]{3,2,1,0:T(8,128)S(1)}, f32[1,6,9,1024]{3,2,1,0:T(8,128)S(1)}, f3...) fusion(f32[1,6,14,1024]{3,2,1,0:T(8,128)S(1)} %get-tuple-elemen, ...), kind=kLoop, calls=%fused_computation.414 | loop fusion | flops 42190848 | bytes 22044672
  61.9 2.8 %add_dynamic-update-slice_fusion.3 = (f32[5,6,9,1024]{3,2,1,0:T(8,128)S(1)}, f32[1,6,9,1024]{3,2,1,0:T(8,128)S(1)}) fusion(f32[5,6,9,1024]{3,2,1,0:T(8,128)S(1)} %get-tuple-element.91, f32[1,6,9,1024]{3,2,1,0:T(8,128)S(1)} %get-tuple-element.108, f32[1,6,9,1024]{3,2,1,0:T(8,128)S(1)} %get-tuple-element.92, f32[1,6,9,1024]{3,2,1,0:T(8,128)S(1)} %get-tuple-element.118, ...), kind=kLoop, calls=%fused_computation.175 | loop fusion | flops 9897984 | bytes 11010048
  64.8 2.8 %add_dynamic-update-slice_fusion.2 = (f32[5,6,9,1024]{3,2,1,0:T(8,128)S(1)}, f32[1,6,9,1024]{3,2,1,0:T(8,128)S(1)}) fusion(f32[5,6,9,1024]{3,2,1,0:T(8,128)S(1)} %get-tuple-element.89, f32[1,6,9,1024]{3,2,1,0:T(8,128)S(1)} %get-tuple-element.109, f32[1,6,9,1024]{3,2,1,0:T(8,128)S(1)} %get-tuple-element.92, f32[1,6,9,1024]{3,2,1,0:T(8,128)S(1)} %get-tuple-element.118, ...), kind=kLoop, calls=%fused_computation.167 | loop fusion | flops 9897984 | bytes 11010048
  67.7 9.8 %add_dynamic-update-slice_fusion.1 = (f32[5,6,9,1024]{3,2,1,0:T(8,128)S(1)}, f32[1,6,9,1024]{3,2,1,0:T(8,128)S(1)}, f32[1,6,9,1024]{3,2,1,0:T(8,128)S(1)}, f32[1,6,9,1024]{3,2,1,0:T(8,128)S(1)}) fusion(f32[5,6,9,1024]{3,2,1,0:T(8,128)S(1)} %get-tuple-element.87, f32[1,6,9,1024]{3,2,1,0:T(8,128)S(1)} %get-tuple-element.95, ...), kind=kLoop, calls=%fused_computation.144 | loop fusion | flops 35665920 | bytes 17694720
  77.4 0.5 add_dynamic-update-slice_fusion
  78.2 0.2 copy.5
  78.3 1.0 copy-done.1
  79.3 0.5 slice.1179
  81.2 1.1 constant_dynamic-slice_fusion.1
  82.3 0.6 slice.1180
  84.3 1.6 fusion.5
  86.2 1.1 copy-done.3
  87.3 6.4 %constant_dynamic-update-slice_fusion.1 = (f32[5,6,8,1025]{3,2,1,0:T(8,128)S(1)}, f32[1,6,8,1025]{3,2,1,0:T(8,128)S(1)}, f32[1,6,8,1025]{3,2,1,0:T(8,128)S(1)}, ...) fusion(f32[5,6,8,1030]{3,2,1,0:T(8,128)S(1)} %broadcast_select_, ...), kind=kLoop, calls=%fused_computation.415 | loop fusion | flops 35768400 | bytes 17215680
  93.7 1.5 add_dynamic-update-slice_fusion.7
  95.3 5.7 %add_dynamic-update-slice_fusion.6 = (f32[5,6,8,1025]{3,2,1,0:T(8,128)S(1)}, f32[1,6,8,1025]{3,2,1,0:T(8,128)S(1)}, f32[1,6,8,1025]{3,2,1,0:T(8,128)S(1)}, f32[1,6,8,1025]{3,2,1,0:T(8,128)S(1)}) fusion(f32[5,6,8,1025]{3,2,1,0:T(8,128)S(1)} %get-tuple-element.59, f32[1,6,8,1025]{3,2,1,0:T(8,128)S(1)} %get-tuple-element.65, ...), kind=kLoop, calls=%fused_computation.297 | loop fusion | flops 31734000 | bytes 9953280
  100.9 1.5 add_dynamic-update-slice_fusion.5
  102.5 0.3 add_dynamic-update-slice_fusion.4
  102.8 0.3 slice_subtract_fusion.1
  103.3 0.6 slice.1259
  105.2 11.4 %all-gather.4.cloned.1.call-done = f32[4,5,3,8,1024]{4,3,2,1,0:T(8,128)} async-done(((f32[1,5,3,8,1024]{4,3,2,1,0:T(8,128)}), f32[4,5,3,8,1024]{4,3,2,1,0:T(8,128)}) %all-gather.4.cloned.1.call-update) | async-done | bytes 1966096 | tf_op jit(solution)/shard_map/all_gather | solution.py:207
  116.6 1.1 fusion.241
  117.6 3.8 %collective-permute-start.4 = (f32[5,3,8,1024]{3,2,1,0:T(8,128)S(1)}, f32[5,3,8,1024]{3,2,1,0:T(8,128)S(1)}, u32[]{:S(2)}, u32[]{:S(2)}) collective-permute-start(f32[5,3,8,1024]{3,2,1,0:T(8,128)S(1)} %fusion.241), channel_id=1, source_target_pairs={{0,132},{4,136},{8,140},{12,144},{16,148},{20,152},{24,156},{28,16... | collective-permute-start | bytes 1474568 | tf_op jit(solution)/shard_map/ppermute | solution.py:223
  121.4 0.2 collective-permute-start.5
  121.7 1.1 constant_dynamic-slice_fusion
  122.9 0.5 slice.1260
  124.7 1.3 fusion.4.padded_ref
  126.0 7.9 %shard_map.37 = f32[5,4,8,1024]{3,2,1,0:T(8,128)} custom-call(f32[5,9,8,1024]{3,2,1,0:T(8,128)} %fusion.4.padded_ref), custom_call_target="tpu_custom_call" | custom-call | tf_op jit(solution)/shard_map/pallas_call | solution.py:250
  133.9 1.2 copy.9
  135.1 0.6 slice.1261
  137.1 9.1 %collective-permute-done.5 = f32[5,3,8,1024]{3,2,1,0:T(8,128)} collective-permute-done((f32[5,3,8,1024]{3,2,1,0:T(8,128)S(1)}, f32[5,3,8,1024]{3,2,1,0:T(8,128)}, u32[]{:S(2)}, u32[]{:S(2)}) %collective-permute-start.5) | collective-permute-done | bytes 491552 | tf_op jit(solution)/shard_map/ppermute | solution.py:223
  146.2 1.3 fusion.12
  147.4 0.2 fusion.13
  147.7 1.2 maximum_select_fusion.1.padded_ref
  149.0 7.1 %shard_map.38 = f32[5,3,8,1024]{3,2,1,0:T(8,128)} custom-call(f32[5,8,8,1024]{3,2,1,0:T(8,128)} %maximum_select_fusion.1.padded_ref), custom_call_target="tpu_custom_call" | custom-call | tf_op jit(solution)/shard_map/pallas_call | solution.py:250
  156.0 1.4 maximum_select_fusion.2
  157.5 0.4 copy-done.2
  157.9 2.9 %fusion.11 = f32[5,6,8,1024]{3,2,1,0:T(8,128)} fusion(f32[5,6,8,1024]{3,2,1,0:T(8,128)S(1)} %copy-done, f32[5,7,8,1024]{3,2,1,0:T(8,128)S(1)} %maximum_select_fusion.2, f32[5,6,8,1024]{3,2,1,0:T(8,128)} %param.11, f32[5,6,8,1025]{3,2,1,0:T(8,128)S(1)} %add_dynamic-update-slice_fusion.4, f32[5,6,9,1024]{3,2,1,0:T(8,128)S(1)} %copy-done.2), kind=kLoop, calls=%fused_computation.77 | loop fusion | flops 2457600 | bytes 8847360 | tf_op jit(solution)/shard_map/add | solution.py:319
  (43 shorter events, 1.5 us)
Async XLA Ops:
  6.5 74.6 %all-gather.6.cloned.1.call-start = ((), (), s32[]{:S(2)}) async-start(), calls=%async_computation.1 | async-start | bytes 4423680 | tf_op jit(solution)/shard_map/all_gather | solution.py:266
  6.5 7.4 %copy-start = (f32[5,6,8,1024]{3,2,1,0:T(8,128)S(1)}, f32[5,6,8,1024]{3,2,1,0:T(8,128)}, u32[]{:S(2)}) copy-start(f32[5,6,8,1024]{3,2,1,0:T(8,128)} %param.12) | copy-start | bytes 2949124
  10.9 105.6 %all-gather.4.cloned.1.call-start = ((), (), s32[]{:S(2)}) async-start(), calls=%async_computation | async-start | bytes 2457600 | tf_op jit(solution)/shard_map/all_gather | solution.py:207
  15.3 29.9 %collective-permute-start = (f32[5,6,3,1024]{3,2,1,0:T(4,128)}, f32[5,6,3,1024]{3,2,1,0:T(4,128)}, u32[]{:S(2)}, u32[]{:S(2)}) collective-permute-start(f32[5,6,3,1024]{3,2,1,0:T(4,128)} %get-tuple-element.135), channel_id=1, source_target_pairs={{0,1},{1,2},{2,3},{4,5},{5,6},{6,7},{8,9},{9,10},{10,11},{12,13},{... | collective-permute-start | bytes 1105928 | tf_op jit(solution)/shard_map/ppermute | solution.py:20
  19.9 26.7 %collective-permute-start.1 = (f32[5,6,3,1024]{3,2,1,0:T(4,128)}, f32[5,6,3,1024]{3,2,1,0:T(4,128)}, u32[]{:S(2)}, u32[]{:S(2)}) collective-permute-start(f32[5,6,3,1024]{3,2,1,0:T(4,128)} %get-tuple-element.136), channel_id=1, source_target_pairs={{1,0},{2,1},{3,2},{5,4},{6,5},{7,6},{9,8},{10,9},{11,10},{13,12},{... | collective-permute-start | bytes 1105928 | tf_op jit(solution)/shard_map/ppermute | solution.py:22
  23.2 19.8 %collective-permute-start.2 = (f32[5,6,8,3]{3,2,1,0:T(8,128)}, f32[5,6,8,3]{3,2,1,0:T(8,128)S(1)}, u32[]{:S(2)}, u32[]{:S(2)}) collective-permute-start(f32[5,6,8,3]{3,2,1,0:T(8,128)} %get-tuple-element.138), channel_id=1, source_target_pairs={{0,4},{4,8},{8,12},{12,16},{16,20},{20,24},{24,28},{28,32},{32,36}... | collective-permute-start | bytes 8648 | tf_op jit(solution)/shard_map/ppermute | solution.py:20
  24.2 19.6 %collective-permute-start.3 = (f32[5,6,8,3]{3,2,1,0:T(8,128)}, f32[5,6,8,3]{3,2,1,0:T(8,128)}, u32[]{:S(2)}, u32[]{:S(2)}) collective-permute-start(f32[5,6,8,3]{3,2,1,0:T(8,128)} %get-tuple-element.137), channel_id=1, source_target_pairs={{4,0},{8,4},{12,8},{16,12},{20,16},{24,20},{28,24},{32,28},{36,32}... | collective-permute-start | bytes 8648 | tf_op jit(solution)/shard_map/ppermute | solution.py:22
  43.1 3.4 %copy-start.8 = (f32[1,6,3,1024]{3,2,1,0:T(4,128)S(1)}, f32[1,6,3,1024]{3,2,1,0:T(4,128)}, u32[]{:S(2)}) copy-start(f32[1,6,3,1024]{3,2,1,0:T(4,128)} %neg.170) | copy-start | bytes 221188
  43.1 0.6 copy-start.9
  78.0 1.3 copy-start.1
  82.2 2.0 %copy-start.5 = (f32[1,5,3,8,1024]{4,3,2,1,0:T(8,128)}, f32[1,5,3,8,1024]{4,3,2,1,0:T(8,128)S(1)}, u32[]{:S(2)}) copy-start(f32[1,5,3,8,1024]{4,3,2,1,0:T(8,128)S(1)} %constant_dynamic-slice_fusion.1) | copy-start | bytes 1474564
  86.1 1.2 copy-start.3
  117.6 19.5 %collective-permute-start.4 = (f32[5,3,8,1024]{3,2,1,0:T(8,128)S(1)}, f32[5,3,8,1024]{3,2,1,0:T(8,128)S(1)}, u32[]{:S(2)}, u32[]{:S(2)}) collective-permute-start(f32[5,3,8,1024]{3,2,1,0:T(8,128)S(1)} %fusion.241), channel_id=1, source_target_pairs={{0,132},{4,136},{8,140},{12,144},{16,148},{20,152},{24,156},{28,16... | collective-permute-start | bytes 1474568 | tf_op jit(solution)/shard_map/ppermute | solution.py:223
  121.4 24.7 %collective-permute-start.5 = (f32[5,3,8,1024]{3,2,1,0:T(8,128)S(1)}, f32[5,3,8,1024]{3,2,1,0:T(8,128)}, u32[]{:S(2)}, u32[]{:S(2)}) collective-permute-start(f32[5,3,8,1024]{3,2,1,0:T(8,128)S(1)} %fusion.241), channel_id=1, source_target_pairs={{0,128},{4,132},{8,136},{12,140},{16,144},{20,148},{24,152},{28,15... | collective-permute-start | bytes 1474568 | tf_op jit(solution)/shard_map/ppermute | solution.py:223
  137.1 10.6 %copy-start.6 = (f32[5,5,8,1024]{3,2,1,0:T(8,128)S(1)}, f32[5,5,8,1024]{3,2,1,0:T(8,128)}, u32[]{:S(2)}) copy-start(f32[5,5,8,1024]{3,2,1,0:T(8,128)} %get-tuple-element.125) | copy-start | bytes 2457604
  137.1 10.6 %copy-start.7 = (f32[5,5,8,1024]{3,2,1,0:T(8,128)S(1)}, f32[5,5,8,1024]{3,2,1,0:T(8,128)}, u32[]{:S(2)}) copy-start(f32[5,5,8,1024]{3,2,1,0:T(8,128)} %get-tuple-element.126) | copy-start | bytes 2457604
  147.7 8.3 %copy-start.4 = (f32[5,4,8,1024]{3,2,1,0:T(8,128)S(1)}, f32[5,4,8,1024]{3,2,1,0:T(8,128)}, u32[]{:S(2)}) copy-start(f32[5,4,8,1024]{3,2,1,0:T(8,128)} %shard_map.37) | copy-start | bytes 1966084
  156.0 1.8 %copy-start.2 = (f32[5,6,9,1024]{3,2,1,0:T(8,128)S(1)}, f32[5,6,9,1024]{3,2,1,0:T(8,128)}, u32[]{:S(2)}) copy-start(f32[5,6,9,1024]{3,2,1,0:T(8,128)} %copy-done.1) | copy-start | bytes 3317764
Sparse Core Ops, SparseCore 0:
  11.1 57.5 all-gather.5
  86.1 30.4 all-gather.3

commit v2 on v0

--- a/solution.py
+++ b/solution.py
@@ -295,7 +295,8 @@
     )
     local_window = hold(local_window, chosen)
     local_faces = axial_faces(local_window)
-    window = window_of(this_slab, next_slab, rotor_step, local_faces)
+    settled = 0.75 * base_state + 0.25 * (section_state - step_ratio * (radial + azimuthal))
+    window = window_of(this_slab, next_slab, rotor_step, local_faces + settled[:, :1, :, :1])
     ghost = flip_theta(
         (1.0 - fraction) * window[..., 1 : width + 1] + fraction * window[..., :width]
     )
@@ -313,8 +314,7 @@
     axial = lax.slice_in_dim(faces, 1, planes + 1, axis=1) - lax.slice_in_dim(
         faces, 0, planes, axis=1
     )
-    change = -step_ratio * (axial + radial + azimuthal)
-    return 0.75 * base_state + 0.25 * (section_state + change)
+    return settled - 0.25 * step_ratio * axial
 
 
 def solution(mesh):

time: 162 us -> 160 us (0.988)
  waiting for transfers between devices: 24 us -> 20 us
  local copies, waits for them, and re-layouts: 23.6 us -> 25.6 us
    all_gather x1, waiting for transfers between devices: 2.77 us -> 0.77 us  [pick_column(): gathered = lax.all_gather(slab, 'tz')]
    all_gather x1, waiting for transfers between devices: 12.1 us -> 10.3 us  [pick_row(): gathered = lax.all_gather(slab, 'tx')]
    unnamed x21 -> x29, local copies, waits for them, and re-layouts: 4.15 us -> 4.66 us
  transfers between devices with their start and end apart: 8 -> 8, of which waited for: 3 -> 3; matrix products, arithmetic and copies ran while one was open for 41% -> 43% of each run, Pallas kernels for 5% -> 5%
where the time goes in v2:
time: 160 us; the launch traced here: 159 us
  other arithmetic  58.6 us (37%)
  local copies, waits for them, and re-layouts  25.6 us (16%)
  between operations  21 us (13%)
  waiting for transfers between devices  20 us (12%)
  starting transfers between devices  18.4 us (11%)
  Pallas kernels  15 us (9%)
    unnamed x8, other arithmetic  43 us
    pallas_call x2, Pallas kernels, axial_faces(): pl.pallas_call(axial_kernel, grid=(width // lanes,), in_specs=[pl.BlockSp...  15 us
    all_gather x1, waiting for transfers between devices, pick_row(): gathered = lax.all_gather(slab, 'tx')  10.3 us
    ppermute x1, waiting for transfers between devices, cross_blocks(): lax.ppermute(slab, axes, this_route)  8.95 us
    ppermute x2, starting transfers between devices, padded_2(): lax.ppermute(head, axis, [((i + 1) % count, i) for i in range(ends)])  8.79 us
    ppermute x2, starting transfers between devices, padded_2(): lax.ppermute(tail, axis, [(i, (i + 1) % count) for i in range(ends)])  5.49 us
    slice x8, local copies, waits for them, and re-layouts, flip_radial(): return jnp.concatenate([turned[:3], -turned[3:4], turned[4:]], axis=0)  4.85 us
    unnamed x29, local copies, waits for them, and re-layouts  4.66 us
  transfers between devices with their start and end apart: 8, of which 3 were waited for; matrix products, arithmetic and copies ran while one was open for 43% of the time, Pallas kernels for 5%

profile of v2, /device:TPU:1, one launch (start us, length us, event | category | flops | bytes accessed | tf_op | source)
XLA Modules:
  0.0 158.6 jit_solution(3133786218428639662)
XLA Ops:
  6.5 2.6 %fusion.235 = (f32[5,6,3,1024]{3,2,1,0:T(4,128)}, f32[5,6,3,1024]{3,2,1,0:T(4,128)S(1)}) fusion(f32[5,6,8,1024]{3,2,1,0:T(8,128)} %param.12), kind=kLoop, calls=%fused_computation.447 | loop fusion | bytes 1474560 | tf_op jit(solution)/shard_map/slice | solution.py:17
  9.1 4.6 %collective-permute-start = (f32[5,6,3,1024]{3,2,1,0:T(4,128)}, f32[5,6,3,1024]{3,2,1,0:T(4,128)}, u32[]{:S(2)}, u32[]{:S(2)}) collective-permute-start(f32[5,6,3,1024]{3,2,1,0:T(4,128)} %get-tuple-element.139), channel_id=1, source_target_pairs={{0,1},{1,2},{2,3},{4,5},{5,6},{6,7},{8,9},{9,10},{10,11},{12,13},{... | collective-permute-start | bytes 1105928 | tf_op jit(solution)/shard_map/ppermute | solution.py:20
  13.7 2.6 %collective-permute-start.1 = (f32[5,6,3,1024]{3,2,1,0:T(4,128)S(1)}, f32[5,6,3,1024]{3,2,1,0:T(4,128)}, u32[]{:S(2)}, u32[]{:S(2)}) collective-permute-start(f32[5,6,3,1024]{3,2,1,0:T(4,128)S(1)} %get-tuple-element.140), channel_id=1, source_target_pairs={{1,0},{2,1},{3,2},{5,4},{6,5},{7,6},{9,8},{10,9},{11,10},{13,12},{... | collective-permute-start | bytes 1105928 | tf_op jit(solution)/shard_map/ppermute | solution.py:22
  16.4 3.0 %rev.2 = f32[5,3,8,1024]{3,2,1,0:T(8,128)} reverse(f32[5,3,8,1024]{3,2,1,0:T(8,128)S(1)} %slice_select_fusion), dimensions={3} | reverse | bytes 983040 | tf_op jit(solution)/shard_map/rev | solution.py:278
  19.5 0.7 fusion.232
  20.3 0.9 collective-permute-start.2
  21.2 6.1 %collective-permute-start.3 = (f32[5,6,8,3]{3,2,1,0:T(8,128)S(1)}, f32[5,6,8,3]{3,2,1,0:T(8,128)}, u32[]{:S(2)}, u32[]{:S(2)}) collective-permute-start(f32[5,6,8,3]{3,2,1,0:T(8,128)S(1)} %get-tuple-element.131), channel_id=1, source_target_pairs={{4,0},{8,4},{12,8},{16,12},{20,16},{24,20},{28,24},{32,28},{36,32}... | collective-permute-start | bytes 8648 | tf_op jit(solution)/shard_map/ppermute | solution.py:22
  27.3 0.1 fusion.233
  27.5 1.4 fusion.230
  29.0 0.8 fusion.231
  30.5 0.3 slice.888
  30.9 2.6 %slice.890 = f32[1,6,3,1024]{3,2,1,0:T(4,128)} reverse(f32[1,6,3,1024]{3,2,1,0:T(4,128)S(1)} %get-tuple-element.138), dimensions={2} | reverse | bytes 147456 | tf_op jit(solution)/shard_map/slice | solution.py:174
  33.4 0.5 slice.886
  34.0 0.3 slice.896
  34.3 0.3 slice.898
  34.7 0.5 slice.894
  35.3 0.6 copy-done.11
  35.9 1.5 concatenate.59
  37.5 1.2 maximum_select_fusion.3
  38.7 1.2 maximum_select_fusion.4
  40.0 0.4 pad_maximum_fusion
  40.4 0.4 fusion.2
  40.9 0.4 broadcast_multiply_fusion
  41.3 0.2 slice_add_fusion.2
  41.7 12.4 %constant_dynamic-update-slice_fusion = (f32[5,6,9,1024]{3,2,1,0:T(8,128)S(1)}, f32[1,6,9,1024]{3,2,1,0:T(8,128)S(1)}, f32[1,6,9,1024]{3,2,1,0:T(8,128)S(1)}, f3...) fusion(f32[1,6,14,1024]{3,2,1,0:T(8,128)S(1)} %get-tuple-elemen, ...), kind=kLoop, calls=%fused_computation.411 | loop fusion | flops 42190848 | bytes 22044672
  54.1 2.8 %add_dynamic-update-slice_fusion.3 = (f32[5,6,9,1024]{3,2,1,0:T(8,128)S(1)}, f32[1,6,9,1024]{3,2,1,0:T(8,128)S(1)}) fusion(f32[5,6,9,1024]{3,2,1,0:T(8,128)S(1)} %get-tuple-element.93, f32[1,6,9,1024]{3,2,1,0:T(8,128)S(1)} %get-tuple-element.110, f32[1,6,9,1024]{3,2,1,0:T(8,128)S(1)} %get-tuple-element.94, f32[1,6,9,1024]{3,2,1,0:T(8,128)S(1)} %get-tuple-element.120, ...), kind=kLoop, calls=%fused_computation.171 | loop fusion | flops 9897984 | bytes 11010048
  56.9 2.8 %add_dynamic-update-slice_fusion.2 = (f32[5,6,9,1024]{3,2,1,0:T(8,128)S(1)}, f32[1,6,9,1024]{3,2,1,0:T(8,128)S(1)}) fusion(f32[5,6,9,1024]{3,2,1,0:T(8,128)S(1)} %get-tuple-element.91, f32[1,6,9,1024]{3,2,1,0:T(8,128)S(1)} %get-tuple-element.111, f32[1,6,9,1024]{3,2,1,0:T(8,128)S(1)} %get-tuple-element.94, f32[1,6,9,1024]{3,2,1,0:T(8,128)S(1)} %get-tuple-element.120, ...), kind=kLoop, calls=%fused_computation.163 | loop fusion | flops 9897984 | bytes 11010048
  59.8 9.8 %add_dynamic-update-slice_fusion.1 = (f32[5,6,9,1024]{3,2,1,0:T(8,128)S(1)}, f32[1,6,9,1024]{3,2,1,0:T(8,128)S(1)}, f32[1,6,9,1024]{3,2,1,0:T(8,128)S(1)}, f32[1,6,9,1024]{3,2,1,0:T(8,128)S(1)}) fusion(f32[5,6,9,1024]{3,2,1,0:T(8,128)S(1)} %get-tuple-element.89, f32[1,6,9,1024]{3,2,1,0:T(8,128)S(1)} %get-tuple-element.97, ...), kind=kLoop, calls=%fused_computation.140 | loop fusion | flops 35665920 | bytes 17694720
  69.6 0.5 add_dynamic-update-slice_fusion
  70.1 0.2 slice_subtract_fusion.2
  70.3 0.2 copy.4
  70.5 0.9 copy-done.1
  71.4 0.5 slice.1176
  73.2 0.8 all-gather.6.cloned.1.call-done
  74.0 1.1 constant_dynamic-slice_fusion.1
  75.1 0.6 slice.1177
  77.0 1.7 %fusion.5 = f32[5,6,8,1025]{3,2,1,0:T(8,128)} fusion(f32[5,6,8,1030]{3,2,1,0:T(8,128)S(1)} %broadcast_select_fusion), kind=kLoop, calls=%fused_computation.70 | loop fusion | flops 492000 | bytes 2952000 | tf_op jit(solution)/shard_map/mul | solution.py:88
  78.9 1.1 copy-done.3
  80.0 6.4 %constant_dynamic-update-slice_fusion.1 = (f32[5,6,8,1025]{3,2,1,0:T(8,128)S(1)}, f32[1,6,8,1025]{3,2,1,0:T(8,128)S(1)}, f32[1,6,8,1025]{3,2,1,0:T(8,128)S(1)}, ...) fusion(f32[5,6,8,1030]{3,2,1,0:T(8,128)S(1)} %broadcast_select_, ...), kind=kLoop, calls=%fused_computation.412 | loop fusion | flops 35768400 | bytes 17215680
  86.4 1.5 add_dynamic-update-slice_fusion.7
  88.0 5.7 %add_dynamic-update-slice_fusion.6 = (f32[5,6,8,1025]{3,2,1,0:T(8,128)S(1)}, f32[1,6,8,1025]{3,2,1,0:T(8,128)S(1)}, f32[1,6,8,1025]{3,2,1,0:T(8,128)S(1)}, f32[1,6,8,1025]{3,2,1,0:T(8,128)S(1)}) fusion(f32[5,6,8,1025]{3,2,1,0:T(8,128)S(1)} %get-tuple-element.61, f32[1,6,8,1025]{3,2,1,0:T(8,128)S(1)} %get-tuple-element.67, ...), kind=kLoop, calls=%fused_computation.294 | loop fusion | flops 31734000 | bytes 9953280
  93.6 1.5 add_dynamic-update-slice_fusion.5
  95.2 0.3 add_dynamic-update-slice_fusion.4
  95.5 1.3 copy-done.2
  96.8 0.6 multiply_add_fusion
  97.4 0.2 copy.6
  97.6 0.5 slice.1254
  99.4 10.3 %all-gather.4.cloned.1.call-done = f32[4,5,3,8,1024]{4,3,2,1,0:T(8,128)} async-done(((f32[1,5,3,8,1024]{4,3,2,1,0:T(8,128)}), f32[4,5,3,8,1024]{4,3,2,1,0:T(8,128)}) %all-gather.4.cloned.1.call-update) | async-done | bytes 1966096 | tf_op jit(solution)/shard_map/all_gather | solution.py:208
  109.7 1.1 fusion.237
  110.8 3.8 %collective-permute-start.4 = (f32[5,3,8,1024]{3,2,1,0:T(8,128)S(1)}, f32[5,3,8,1024]{3,2,1,0:T(8,128)S(1)}, u32[]{:S(2)}, u32[]{:S(2)}) collective-permute-start(f32[5,3,8,1024]{3,2,1,0:T(8,128)S(1)} %fusion.237), channel_id=1, source_target_pairs={{0,132},{4,136},{8,140},{12,144},{16,148},{20,152},{24,156},{28,16... | collective-permute-start | bytes 1474568 | tf_op jit(solution)/shard_map/ppermute | solution.py:224
  114.6 0.2 collective-permute-start.5
  114.8 1.1 constant_dynamic-slice_fusion
  116.0 0.6 slice.1255
  117.9 1.4 fusion.4.padded_ref
  119.3 7.9 %shard_map.37 = f32[5,4,8,1024]{3,2,1,0:T(8,128)} custom-call(f32[5,9,8,1024]{3,2,1,0:T(8,128)} %fusion.4.padded_ref), custom_call_target="tpu_custom_call" | custom-call | tf_op jit(solution)/shard_map/pallas_call | solution.py:251
  127.2 1.2 broadcast_add_fusion
  128.5 0.5 slice.1257
  130.4 9.0 %collective-permute-done.5 = f32[5,3,8,1024]{3,2,1,0:T(8,128)} collective-permute-done((f32[5,3,8,1024]{3,2,1,0:T(8,128)S(1)}, f32[5,3,8,1024]{3,2,1,0:T(8,128)}, u32[]{:S(2)}, u32[]{:S(2)}) %collective-permute-start.5) | collective-permute-done | bytes 491552 | tf_op jit(solution)/shard_map/ppermute | solution.py:224
  139.3 1.3 fusion.8
  140.6 0.2 fusion.9
  140.9 1.3 maximum_select_fusion.1.padded_ref
  142.2 7.1 %shard_map.38 = f32[5,3,8,1024]{3,2,1,0:T(8,128)} custom-call(f32[5,8,8,1024]{3,2,1,0:T(8,128)} %maximum_select_fusion.1.padded_ref), custom_call_target="tpu_custom_call" | custom-call | tf_op jit(solution)/shard_map/pallas_call | solution.py:251
  149.3 1.3 maximum_select_fusion.2
  150.6 1.2 fusion.7
  (46 shorter events, 1.2 us)
Async XLA Ops:
  6.5 9.8 %copy-start = (f32[5,6,8,1024]{3,2,1,0:T(8,128)S(1)}, f32[5,6,8,1024]{3,2,1,0:T(8,128)}, u32[]{:S(2)}) copy-start(f32[5,6,8,1024]{3,2,1,0:T(8,128)} %param.12) | copy-start | bytes 2949124
  6.5 67.4 %all-gather.6.cloned.1.call-start = ((), (), s32[]{:S(2)}) async-start(), calls=%async_computation.1 | async-start | bytes 4423680 | tf_op jit(solution)/shard_map/all_gather | solution.py:200
  9.1 28.4 %collective-permute-start = (f32[5,6,3,1024]{3,2,1,0:T(4,128)}, f32[5,6,3,1024]{3,2,1,0:T(4,128)}, u32[]{:S(2)}, u32[]{:S(2)}) collective-permute-start(f32[5,6,3,1024]{3,2,1,0:T(4,128)} %get-tuple-element.139), channel_id=1, source_target_pairs={{0,1},{1,2},{2,3},{4,5},{5,6},{6,7},{8,9},{9,10},{10,11},{12,13},{... | collective-permute-start | bytes 1105928 | tf_op jit(solution)/shard_map/ppermute | solution.py:20
  13.7 25.0 %collective-permute-start.1 = (f32[5,6,3,1024]{3,2,1,0:T(4,128)S(1)}, f32[5,6,3,1024]{3,2,1,0:T(4,128)}, u32[]{:S(2)}, u32[]{:S(2)}) collective-permute-start(f32[5,6,3,1024]{3,2,1,0:T(4,128)S(1)} %get-tuple-element.140), channel_id=1, source_target_pairs={{1,0},{2,1},{3,2},{5,4},{6,5},{7,6},{9,8},{10,9},{11,10},{13,12},{... | collective-permute-start | bytes 1105928 | tf_op jit(solution)/shard_map/ppermute | solution.py:22
  19.5 90.2 %all-gather.4.cloned.1.call-start = ((), (), s32[]{:S(2)}) async-start(), calls=%async_computation | async-start | bytes 2457600 | tf_op jit(solution)/shard_map/all_gather | solution.py:208
  20.3 15.0 %collective-permute-start.2 = (f32[5,6,8,3]{3,2,1,0:T(8,128)}, f32[5,6,8,3]{3,2,1,0:T(8,128)S(1)}, u32[]{:S(2)}, u32[]{:S(2)}) collective-permute-start(f32[5,6,8,3]{3,2,1,0:T(8,128)} %get-tuple-element.132), channel_id=1, source_target_pairs={{0,4},{4,8},{8,12},{12,16},{16,20},{20,24},{24,28},{28,32},{32,36}... | collective-permute-start | bytes 8648 | tf_op jit(solution)/shard_map/ppermute | solution.py:20
  21.2 14.7 %collective-permute-start.3 = (f32[5,6,8,3]{3,2,1,0:T(8,128)S(1)}, f32[5,6,8,3]{3,2,1,0:T(8,128)}, u32[]{:S(2)}, u32[]{:S(2)}) collective-permute-start(f32[5,6,8,3]{3,2,1,0:T(8,128)S(1)} %get-tuple-element.131), channel_id=1, source_target_pairs={{4,0},{8,4},{12,8},{16,12},{20,16},{24,20},{28,24},{32,28},{36,32}... | collective-permute-start | bytes 8648 | tf_op jit(solution)/shard_map/ppermute | solution.py:22
  35.3 0.6 copy-start.11
  70.1 1.3 copy-start.1
  75.0 1.8 %copy-start.5 = (f32[1,5,3,8,1024]{4,3,2,1,0:T(8,128)}, f32[1,5,3,8,1024]{4,3,2,1,0:T(8,128)S(1)}, u32[]{:S(2)}) copy-start(f32[1,5,3,8,1024]{4,3,2,1,0:T(8,128)S(1)} %constant_dynamic-slice_fusion.1) | copy-start | bytes 1474564
  78.8 1.2 copy-start.3
  93.6 1.8 %copy-start.8 = (f32[5,6,8,1024]{3,2,1,0:T(8,128)S(1)}, f32[5,6,8,1024]{3,2,1,0:T(8,128)}, u32[]{:S(2)}) copy-start(f32[5,6,8,1024]{3,2,1,0:T(8,128)} %param.11) | copy-start | bytes 2949124
  95.2 1.6 copy-start.2
  97.6 20.3 %copy-start.9 = (f32[5,1,8,1024]{3,2,1,0:T(8,128)S(1)}, f32[5,1,8,1024]{3,2,1,0:T(8,128)}, u32[]{:S(2)}) copy-start(f32[5,1,8,1024]{3,2,1,0:T(8,128)} %get-tuple-element.129) | copy-start | bytes 491524
  97.6 20.3 %copy-start.10 = (f32[5,1,8,1024]{3,2,1,0:T(8,128)S(1)}, f32[5,1,8,1024]{3,2,1,0:T(8,128)}, u32[]{:S(2)}) copy-start(f32[5,1,8,1024]{3,2,1,0:T(8,128)} %get-tuple-element.130) | copy-start | bytes 491524
  110.8 19.6 %collective-permute-start.4 = (f32[5,3,8,1024]{3,2,1,0:T(8,128)S(1)}, f32[5,3,8,1024]{3,2,1,0:T(8,128)S(1)}, u32[]{:S(2)}, u32[]{:S(2)}) collective-permute-start(f32[5,3,8,1024]{3,2,1,0:T(8,128)S(1)} %fusion.237), channel_id=1, source_target_pairs={{0,132},{4,136},{8,140},{12,144},{16,148},{20,152},{24,156},{28,16... | collective-permute-start | bytes 1474568 | tf_op jit(solution)/shard_map/ppermute | solution.py:224
  114.6 24.7 %collective-permute-start.5 = (f32[5,3,8,1024]{3,2,1,0:T(8,128)S(1)}, f32[5,3,8,1024]{3,2,1,0:T(8,128)}, u32[]{:S(2)}, u32[]{:S(2)}) collective-permute-start(f32[5,3,8,1024]{3,2,1,0:T(8,128)S(1)} %fusion.237), channel_id=1, source_target_pairs={{0,128},{4,132},{8,136},{12,140},{16,144},{20,148},{24,152},{28,15... | collective-permute-start | bytes 1474568 | tf_op jit(solution)/shard_map/ppermute | solution.py:224
  130.3 10.6 %copy-start.6 = (f32[5,5,8,1024]{3,2,1,0:T(8,128)S(1)}, f32[5,5,8,1024]{3,2,1,0:T(8,128)}, u32[]{:S(2)}) copy-start(f32[5,5,8,1024]{3,2,1,0:T(8,128)} %get-tuple-element.127) | copy-start | bytes 2457604
  130.3 10.6 %copy-start.7 = (f32[5,5,8,1024]{3,2,1,0:T(8,128)S(1)}, f32[5,5,8,1024]{3,2,1,0:T(8,128)}, u32[]{:S(2)}) copy-start(f32[5,5,8,1024]{3,2,1,0:T(8,128)} %get-tuple-element.128) | copy-start | bytes 2457604
  140.9 8.4 %copy-start.4 = (f32[5,4,8,1024]{3,2,1,0:T(8,128)S(1)}, f32[5,4,8,1024]{3,2,1,0:T(8,128)}, u32[]{:S(2)}) copy-start(f32[5,4,8,1024]{3,2,1,0:T(8,128)} %shard_map.37) | copy-start | bytes 1966084
Sparse Core Ops, SparseCore 0:
  19.6 54.2 all-gather.5
  78.8 30.8 all-gather.3

commit v3 on v2

--- a/solution.py
+++ b/solution.py
@@ -245,7 +245,7 @@
 
 def axial_faces(padded):
     components, planes, bands, width = padded.shape
-    lanes = 128
+    lanes = 256
     block = (components, planes, bands, lanes)
     out_block = (components, planes - 5, bands, lanes)
     return pl.pallas_call(

time: 160 us -> 158 us (0.988)
  Pallas kernels: 15 us -> 12.8 us
    pallas_call x2, Pallas kernels: 15 us -> 12.8 us  [axial_faces(): pl.pallas_call(axial_kernel, grid=(width // lanes,), in_specs=[pl.BlockSp...]
  transfers between devices with their start and end apart: 8 -> 8, of which waited for: 3 -> 3; matrix products, arithmetic and copies ran while one was open for 43% -> 43% of each run, Pallas kernels for 5% -> 4%
where the time goes in v3:
time: 158 us; the launch traced here: 157 us
  other arithmetic  58.7 us (37%)
  local copies, waits for them, and re-layouts  25.7 us (16%)
  between operations  21 us (13%)
  waiting for transfers between devices  20.9 us (13%)
  starting transfers between devices  18.4 us (12%)
  Pallas kernels  12.8 us (8%)
    unnamed x8, other arithmetic  43 us
    pallas_call x2, Pallas kernels, axial_faces(): pl.pallas_call(axial_kernel, grid=(width // lanes,), in_specs=[pl.BlockSp...  12.8 us
    all_gather x1, waiting for transfers between devices, pick_row(): gathered = lax.all_gather(slab, 'tx')  10.3 us
    ppermute x1, waiting for transfers between devices, cross_blocks(): lax.ppermute(slab, axes, this_route)  9.77 us
    ppermute x2, starting transfers between devices, padded_2(): lax.ppermute(head, axis, [((i + 1) % count, i) for i in range(ends)])  8.79 us
    ppermute x2, starting transfers between devices, padded_2(): lax.ppermute(tail, axis, [(i, (i + 1) % count) for i in range(ends)])  5.49 us
    slice x8, local copies, waits for them, and re-layouts, flip_radial(): return jnp.concatenate([turned[:3], -turned[3:4], turned[4:]], axis=0)  4.85 us
    unnamed x29, local copies, waits for them, and re-layouts  4.66 us
  transfers between devices with their start and end apart: 8, of which 3 were waited for; matrix products, arithmetic and copies ran while one was open for 43% of the time, Pallas kernels for 4%

profile of v3, /device:TPU:1, one launch (start us, length us, event | category | flops | bytes accessed | tf_op | source)
XLA Modules:
  0.0 157.4 jit_solution(9940440580211752109)
XLA Ops:
  6.5 2.7 %fusion.235 = (f32[5,6,3,1024]{3,2,1,0:T(4,128)}, f32[5,6,3,1024]{3,2,1,0:T(4,128)S(1)}) fusion(f32[5,6,8,1024]{3,2,1,0:T(8,128)} %param.12), kind=kLoop, calls=%fused_computation.447 | loop fusion | bytes 1474560 | tf_op jit(solution)/shard_map/slice | solution.py:17
  9.2 4.6 %collective-permute-start = (f32[5,6,3,1024]{3,2,1,0:T(4,128)}, f32[5,6,3,1024]{3,2,1,0:T(4,128)}, u32[]{:S(2)}, u32[]{:S(2)}) collective-permute-start(f32[5,6,3,1024]{3,2,1,0:T(4,128)} %get-tuple-element.139), channel_id=1, source_target_pairs={{0,1},{1,2},{2,3},{4,5},{5,6},{6,7},{8,9},{9,10},{10,11},{12,13},{... | collective-permute-start | bytes 1105928 | tf_op jit(solution)/shard_map/ppermute | solution.py:20
  13.8 2.6 %collective-permute-start.1 = (f32[5,6,3,1024]{3,2,1,0:T(4,128)S(1)}, f32[5,6,3,1024]{3,2,1,0:T(4,128)}, u32[]{:S(2)}, u32[]{:S(2)}) collective-permute-start(f32[5,6,3,1024]{3,2,1,0:T(4,128)S(1)} %get-tuple-element.140), channel_id=1, source_target_pairs={{1,0},{2,1},{3,2},{5,4},{6,5},{7,6},{9,8},{10,9},{11,10},{13,12},{... | collective-permute-start | bytes 1105928 | tf_op jit(solution)/shard_map/ppermute | solution.py:22
  16.5 3.0 %rev.2 = f32[5,3,8,1024]{3,2,1,0:T(8,128)} reverse(f32[5,3,8,1024]{3,2,1,0:T(8,128)S(1)} %slice_select_fusion), dimensions={3} | reverse | bytes 983040 | tf_op jit(solution)/shard_map/rev | solution.py:278
  19.6 0.7 fusion.232
  20.4 0.9 collective-permute-start.2
  21.3 6.1 %collective-permute-start.3 = (f32[5,6,8,3]{3,2,1,0:T(8,128)S(1)}, f32[5,6,8,3]{3,2,1,0:T(8,128)}, u32[]{:S(2)}, u32[]{:S(2)}) collective-permute-start(f32[5,6,8,3]{3,2,1,0:T(8,128)S(1)} %get-tuple-element.131), channel_id=1, source_target_pairs={{4,0},{8,4},{12,8},{16,12},{20,16},{24,20},{28,24},{32,28},{36,32}... | collective-permute-start | bytes 8648 | tf_op jit(solution)/shard_map/ppermute | solution.py:22
  27.4 0.1 fusion.233
  27.6 1.4 fusion.230
  29.0 0.8 fusion.231
  30.6 0.3 slice.888
  31.0 2.6 %slice.890 = f32[1,6,3,1024]{3,2,1,0:T(4,128)} reverse(f32[1,6,3,1024]{3,2,1,0:T(4,128)S(1)} %get-tuple-element.138), dimensions={2} | reverse | bytes 147456 | tf_op jit(solution)/shard_map/slice | solution.py:174
  33.5 0.5 slice.886
  34.1 0.3 slice.896
  34.4 0.3 slice.898
  34.8 0.5 slice.894
  35.4 0.6 copy-done.11
  36.0 1.5 concatenate.59
  37.6 1.2 maximum_select_fusion.3
  38.8 1.2 maximum_select_fusion.4
  40.1 0.4 pad_maximum_fusion
  40.5 0.4 fusion.2
  41.0 0.4 broadcast_multiply_fusion
  41.4 0.2 slice_add_fusion.2
  41.8 12.4 %constant_dynamic-update-slice_fusion = (f32[5,6,9,1024]{3,2,1,0:T(8,128)S(1)}, f32[1,6,9,1024]{3,2,1,0:T(8,128)S(1)}, f32[1,6,9,1024]{3,2,1,0:T(8,128)S(1)}, f3...) fusion(f32[1,6,14,1024]{3,2,1,0:T(8,128)S(1)} %get-tuple-elemen, ...), kind=kLoop, calls=%fused_computation.411 | loop fusion | flops 42190848 | bytes 22044672
  54.2 2.8 %add_dynamic-update-slice_fusion.3 = (f32[5,6,9,1024]{3,2,1,0:T(8,128)S(1)}, f32[1,6,9,1024]{3,2,1,0:T(8,128)S(1)}) fusion(f32[5,6,9,1024]{3,2,1,0:T(8,128)S(1)} %get-tuple-element.93, f32[1,6,9,1024]{3,2,1,0:T(8,128)S(1)} %get-tuple-element.110, f32[1,6,9,1024]{3,2,1,0:T(8,128)S(1)} %get-tuple-element.94, f32[1,6,9,1024]{3,2,1,0:T(8,128)S(1)} %get-tuple-element.120, ...), kind=kLoop, calls=%fused_computation.171 | loop fusion | flops 9897984 | bytes 11010048
  57.0 2.8 %add_dynamic-update-slice_fusion.2 = (f32[5,6,9,1024]{3,2,1,0:T(8,128)S(1)}, f32[1,6,9,1024]{3,2,1,0:T(8,128)S(1)}) fusion(f32[5,6,9,1024]{3,2,1,0:T(8,128)S(1)} %get-tuple-element.91, f32[1,6,9,1024]{3,2,1,0:T(8,128)S(1)} %get-tuple-element.111, f32[1,6,9,1024]{3,2,1,0:T(8,128)S(1)} %get-tuple-element.94, f32[1,6,9,1024]{3,2,1,0:T(8,128)S(1)} %get-tuple-element.120, ...), kind=kLoop, calls=%fused_computation.163 | loop fusion | flops 9897984 | bytes 11010048
  59.9 9.8 %add_dynamic-update-slice_fusion.1 = (f32[5,6,9,1024]{3,2,1,0:T(8,128)S(1)}, f32[1,6,9,1024]{3,2,1,0:T(8,128)S(1)}, f32[1,6,9,1024]{3,2,1,0:T(8,128)S(1)}, f32[1,6,9,1024]{3,2,1,0:T(8,128)S(1)}) fusion(f32[5,6,9,1024]{3,2,1,0:T(8,128)S(1)} %get-tuple-element.89, f32[1,6,9,1024]{3,2,1,0:T(8,128)S(1)} %get-tuple-element.97, ...), kind=kLoop, calls=%fused_computation.140 | loop fusion | flops 35665920 | bytes 17694720
  69.7 0.5 add_dynamic-update-slice_fusion
  70.2 0.2 slice_subtract_fusion.2
  70.4 0.2 copy.4
  70.6 0.9 copy-done.1
  71.5 0.5 slice.1176
  73.3 0.8 all-gather.6.cloned.1.call-done
  74.0 1.1 constant_dynamic-slice_fusion.1
  75.2 0.6 slice.1177
  77.1 1.7 %fusion.5 = f32[5,6,8,1025]{3,2,1,0:T(8,128)} fusion(f32[5,6,8,1030]{3,2,1,0:T(8,128)S(1)} %broadcast_select_fusion), kind=kLoop, calls=%fused_computation.70 | loop fusion | flops 492000 | bytes 2952000 | tf_op jit(solution)/shard_map/mul | solution.py:88
  79.0 1.1 copy-done.3
  80.1 6.4 %constant_dynamic-update-slice_fusion.1 = (f32[5,6,8,1025]{3,2,1,0:T(8,128)S(1)}, f32[1,6,8,1025]{3,2,1,0:T(8,128)S(1)}, f32[1,6,8,1025]{3,2,1,0:T(8,128)S(1)}, ...) fusion(f32[5,6,8,1030]{3,2,1,0:T(8,128)S(1)} %broadcast_select_, ...), kind=kLoop, calls=%fused_computation.412 | loop fusion | flops 35768400 | bytes 17215680
  86.5 1.5 add_dynamic-update-slice_fusion.7
  88.0 5.7 %add_dynamic-update-slice_fusion.6 = (f32[5,6,8,1025]{3,2,1,0:T(8,128)S(1)}, f32[1,6,8,1025]{3,2,1,0:T(8,128)S(1)}, f32[1,6,8,1025]{3,2,1,0:T(8,128)S(1)}, f32[1,6,8,1025]{3,2,1,0:T(8,128)S(1)}) fusion(f32[5,6,8,1025]{3,2,1,0:T(8,128)S(1)} %get-tuple-element.61, f32[1,6,8,1025]{3,2,1,0:T(8,128)S(1)} %get-tuple-element.67, ...), kind=kLoop, calls=%fused_computation.294 | loop fusion | flops 31734000 | bytes 9953280
  93.7 1.5 add_dynamic-update-slice_fusion.5
  95.3 0.3 add_dynamic-update-slice_fusion.4
  95.6 1.3 copy-done.2
  96.8 0.6 multiply_add_fusion
  97.5 0.2 copy.6
  97.7 0.5 slice.1254
  99.5 10.3 %all-gather.4.cloned.1.call-done = f32[4,5,3,8,1024]{4,3,2,1,0:T(8,128)} async-done(((f32[1,5,3,8,1024]{4,3,2,1,0:T(8,128)}), f32[4,5,3,8,1024]{4,3,2,1,0:T(8,128)}) %all-gather.4.cloned.1.call-update) | async-done | bytes 1966096 | tf_op jit(solution)/shard_map/all_gather | solution.py:208
  109.8 1.1 fusion.237
  110.9 3.8 %collective-permute-start.4 = (f32[5,3,8,1024]{3,2,1,0:T(8,128)S(1)}, f32[5,3,8,1024]{3,2,1,0:T(8,128)S(1)}, u32[]{:S(2)}, u32[]{:S(2)}) collective-permute-start(f32[5,3,8,1024]{3,2,1,0:T(8,128)S(1)} %fusion.237), channel_id=1, source_target_pairs={{0,132},{4,136},{8,140},{12,144},{16,148},{20,152},{24,156},{28,16... | collective-permute-start | bytes 1474568 | tf_op jit(solution)/shard_map/ppermute | solution.py:224
  114.7 0.2 collective-permute-start.5
  114.9 1.1 constant_dynamic-slice_fusion
  116.1 0.6 slice.1255
  118.0 1.4 fusion.4.padded_ref
  119.4 7.1 %shard_map.37 = f32[5,4,8,1024]{3,2,1,0:T(8,128)} custom-call(f32[5,9,8,1024]{3,2,1,0:T(8,128)} %fusion.4.padded_ref), custom_call_target="tpu_custom_call" | custom-call | tf_op jit(solution)/shard_map/pallas_call | solution.py:251
  126.5 1.2 broadcast_add_fusion
  127.8 0.5 slice.1257
  129.6 9.8 %collective-permute-done.5 = f32[5,3,8,1024]{3,2,1,0:T(8,128)} collective-permute-done((f32[5,3,8,1024]{3,2,1,0:T(8,128)S(1)}, f32[5,3,8,1024]{3,2,1,0:T(8,128)}, u32[]{:S(2)}, u32[]{:S(2)}) %collective-permute-start.5) | collective-permute-done | bytes 491552 | tf_op jit(solution)/shard_map/ppermute | solution.py:224
  139.4 1.3 fusion.8
  140.7 0.2 fusion.9
  141.0 1.3 maximum_select_fusion.1.padded_ref
  142.3 5.7 %shard_map.38 = f32[5,3,8,1024]{3,2,1,0:T(8,128)} custom-call(f32[5,8,8,1024]{3,2,1,0:T(8,128)} %maximum_select_fusion.1.padded_ref), custom_call_target="tpu_custom_call" | custom-call | tf_op jit(solution)/shard_map/pallas_call | solution.py:251
  148.0 1.4 maximum_select_fusion.2
  149.4 1.2 fusion.7
  (46 shorter events, 1.2 us)
Async XLA Ops:
  6.5 9.9 %copy-start = (f32[5,6,8,1024]{3,2,1,0:T(8,128)S(1)}, f32[5,6,8,1024]{3,2,1,0:T(8,128)}, u32[]{:S(2)}) copy-start(f32[5,6,8,1024]{3,2,1,0:T(8,128)} %param.12) | copy-start | bytes 2949124
  6.5 67.5 %all-gather.6.cloned.1.call-start = ((), (), s32[]{:S(2)}) async-start(), calls=%async_computation.1 | async-start | bytes 4423680 | tf_op jit(solution)/shard_map/all_gather | solution.py:200
  9.2 28.4 %collective-permute-start = (f32[5,6,3,1024]{3,2,1,0:T(4,128)}, f32[5,6,3,1024]{3,2,1,0:T(4,128)}, u32[]{:S(2)}, u32[]{:S(2)}) collective-permute-start(f32[5,6,3,1024]{3,2,1,0:T(4,128)} %get-tuple-element.139), channel_id=1, source_target_pairs={{0,1},{1,2},{2,3},{4,5},{5,6},{6,7},{8,9},{9,10},{10,11},{12,13},{... | collective-permute-start | bytes 1105928 | tf_op jit(solution)/shard_map/ppermute | solution.py:20
  13.8 25.0 %collective-permute-start.1 = (f32[5,6,3,1024]{3,2,1,0:T(4,128)S(1)}, f32[5,6,3,1024]{3,2,1,0:T(4,128)}, u32[]{:S(2)}, u32[]{:S(2)}) collective-permute-start(f32[5,6,3,1024]{3,2,1,0:T(4,128)S(1)} %get-tuple-element.140), channel_id=1, source_target_pairs={{1,0},{2,1},{3,2},{5,4},{6,5},{7,6},{9,8},{10,9},{11,10},{13,12},{... | collective-permute-start | bytes 1105928 | tf_op jit(solution)/shard_map/ppermute | solution.py:22
  19.6 90.2 %all-gather.4.cloned.1.call-start = ((), (), s32[]{:S(2)}) async-start(), calls=%async_computation | async-start | bytes 2457600 | tf_op jit(solution)/shard_map/all_gather | solution.py:208
  20.4 15.0 %collective-permute-start.2 = (f32[5,6,8,3]{3,2,1,0:T(8,128)}, f32[5,6,8,3]{3,2,1,0:T(8,128)S(1)}, u32[]{:S(2)}, u32[]{:S(2)}) collective-permute-start(f32[5,6,8,3]{3,2,1,0:T(8,128)} %get-tuple-element.132), channel_id=1, source_target_pairs={{0,4},{4,8},{8,12},{12,16},{16,20},{20,24},{24,28},{28,32},{32,36}... | collective-permute-start | bytes 8648 | tf_op jit(solution)/shard_map/ppermute | solution.py:20
  21.3 14.7 %collective-permute-start.3 = (f32[5,6,8,3]{3,2,1,0:T(8,128)S(1)}, f32[5,6,8,3]{3,2,1,0:T(8,128)}, u32[]{:S(2)}, u32[]{:S(2)}) collective-permute-start(f32[5,6,8,3]{3,2,1,0:T(8,128)S(1)} %get-tuple-element.131), channel_id=1, source_target_pairs={{4,0},{8,4},{12,8},{16,12},{20,16},{24,20},{28,24},{32,28},{36,32}... | collective-permute-start | bytes 8648 | tf_op jit(solution)/shard_map/ppermute | solution.py:22
  35.4 0.6 copy-start.11
  70.2 1.3 copy-start.1
  75.1 1.8 %copy-start.5 = (f32[1,5,3,8,1024]{4,3,2,1,0:T(8,128)}, f32[1,5,3,8,1024]{4,3,2,1,0:T(8,128)S(1)}, u32[]{:S(2)}) copy-start(f32[1,5,3,8,1024]{4,3,2,1,0:T(8,128)S(1)} %constant_dynamic-slice_fusion.1) | copy-start | bytes 1474564
  78.9 1.2 copy-start.3
  93.7 1.8 %copy-start.8 = (f32[5,6,8,1024]{3,2,1,0:T(8,128)S(1)}, f32[5,6,8,1024]{3,2,1,0:T(8,128)}, u32[]{:S(2)}) copy-start(f32[5,6,8,1024]{3,2,1,0:T(8,128)} %param.11) | copy-start | bytes 2949124
  95.3 1.6 %copy-start.2 = (f32[5,6,9,1024]{3,2,1,0:T(8,128)S(1)}, f32[5,6,9,1024]{3,2,1,0:T(8,128)}, u32[]{:S(2)}) copy-start(f32[5,6,9,1024]{3,2,1,0:T(8,128)} %copy-done.1) | copy-start | bytes 3317764
  97.7 20.3 %copy-start.9 = (f32[5,1,8,1024]{3,2,1,0:T(8,128)S(1)}, f32[5,1,8,1024]{3,2,1,0:T(8,128)}, u32[]{:S(2)}) copy-start(f32[5,1,8,1024]{3,2,1,0:T(8,128)} %get-tuple-element.129) | copy-start | bytes 491524
  97.7 20.3 %copy-start.10 = (f32[5,1,8,1024]{3,2,1,0:T(8,128)S(1)}, f32[5,1,8,1024]{3,2,1,0:T(8,128)}, u32[]{:S(2)}) copy-start(f32[5,1,8,1024]{3,2,1,0:T(8,128)} %get-tuple-element.130) | copy-start | bytes 491524
  110.9 18.8 %collective-permute-start.4 = (f32[5,3,8,1024]{3,2,1,0:T(8,128)S(1)}, f32[5,3,8,1024]{3,2,1,0:T(8,128)S(1)}, u32[]{:S(2)}, u32[]{:S(2)}) collective-permute-start(f32[5,3,8,1024]{3,2,1,0:T(8,128)S(1)} %fusion.237), channel_id=1, source_target_pairs={{0,132},{4,136},{8,140},{12,144},{16,148},{20,152},{24,156},{28,16... | collective-permute-start | bytes 1474568 | tf_op jit(solution)/shard_map/ppermute | solution.py:224
  114.7 24.7 %collective-permute-start.5 = (f32[5,3,8,1024]{3,2,1,0:T(8,128)S(1)}, f32[5,3,8,1024]{3,2,1,0:T(8,128)}, u32[]{:S(2)}, u32[]{:S(2)}) collective-permute-start(f32[5,3,8,1024]{3,2,1,0:T(8,128)S(1)} %fusion.237), channel_id=1, source_target_pairs={{0,128},{4,132},{8,136},{12,140},{16,144},{20,148},{24,152},{28,15... | collective-permute-start | bytes 1474568 | tf_op jit(solution)/shard_map/ppermute | solution.py:224
  129.6 11.4 %copy-start.6 = (f32[5,5,8,1024]{3,2,1,0:T(8,128)S(1)}, f32[5,5,8,1024]{3,2,1,0:T(8,128)}, u32[]{:S(2)}) copy-start(f32[5,5,8,1024]{3,2,1,0:T(8,128)} %get-tuple-element.127) | copy-start | bytes 2457604
  129.6 11.4 %copy-start.7 = (f32[5,5,8,1024]{3,2,1,0:T(8,128)S(1)}, f32[5,5,8,1024]{3,2,1,0:T(8,128)}, u32[]{:S(2)}) copy-start(f32[5,5,8,1024]{3,2,1,0:T(8,128)} %get-tuple-element.128) | copy-start | bytes 2457604
  141.0 7.0 %copy-start.4 = (f32[5,4,8,1024]{3,2,1,0:T(8,128)S(1)}, f32[5,4,8,1024]{3,2,1,0:T(8,128)}, u32[]{:S(2)}) copy-start(f32[5,4,8,1024]{3,2,1,0:T(8,128)} %shard_map.37) | copy-start | bytes 1966084
Sparse Core Ops, SparseCore 0:
  19.7 54.2 all-gather.5
  78.9 30.8 all-gather.3

commit v4 on v3

--- a/solution.py
+++ b/solution.py
@@ -245,7 +245,7 @@
 
 def axial_faces(padded):
     components, planes, bands, width = padded.shape
-    lanes = 256
+    lanes = 512
     block = (components, planes, bands, lanes)
     out_block = (components, planes - 5, bands, lanes)
     return pl.pallas_call(

time: 158 us -> 158 us (level)
  transfers between devices with their start and end apart: 8 -> 8, of which waited for: 3 -> 3; matrix products, arithmetic and copies ran while one was open for 43% -> 43% of each run, Pallas kernels for 4% -> 5%
where the time goes in v4:
time: 158 us; the launch traced here: 157 us
  other arithmetic  58.6 us (37%)
  local copies, waits for them, and re-layouts  25.7 us (16%)
  between operations  21 us (13%)
  waiting for transfers between devices  20.6 us (13%)
  starting transfers between devices  18.4 us (12%)
  Pallas kernels  13.1 us (8%)
    unnamed x8, other arithmetic  43 us
    pallas_call x2, Pallas kernels, axial_faces(): pl.pallas_call(axial_kernel, grid=(width // lanes,), in_specs=[pl.BlockSp...  13.1 us
    all_gather x1, waiting for transfers between devices, pick_row(): gathered = lax.all_gather(slab, 'tx')  10.3 us
    ppermute x1, waiting for transfers between devices, cross_blocks(): lax.ppermute(slab, axes, this_route)  9.56 us
    ppermute x2, starting transfers between devices, padded_2(): lax.ppermute(head, axis, [((i + 1) % count, i) for i in range(ends)])  8.79 us
    ppermute x2, starting transfers between devices, padded_2(): lax.ppermute(tail, axis, [(i, (i + 1) % count) for i in range(ends)])  5.49 us
    slice x8, local copies, waits for them, and re-layouts, flip_radial(): return jnp.concatenate([turned[:3], -turned[3:4], turned[4:]], axis=0)  4.85 us
    unnamed x29, local copies, waits for them, and re-layouts  4.66 us
  transfers between devices with their start and end apart: 8, of which 3 were waited for; matrix products, arithmetic and copies ran while one was open for 43% of the time, Pallas kernels for 5%

profile of v4, /device:TPU:1, one launch (start us, length us, event | category | flops | bytes accessed | tf_op | source)
XLA Modules:
  0.0 157.5 jit_solution(16269868860453775469)
XLA Ops:
  6.5 2.7 %fusion.235 = (f32[5,6,3,1024]{3,2,1,0:T(4,128)}, f32[5,6,3,1024]{3,2,1,0:T(4,128)S(1)}) fusion(f32[5,6,8,1024]{3,2,1,0:T(8,128)} %param.12), kind=kLoop, calls=%fused_computation.447 | loop fusion | bytes 1474560 | tf_op jit(solution)/shard_map/slice | solution.py:17
  9.2 4.6 %collective-permute-start = (f32[5,6,3,1024]{3,2,1,0:T(4,128)}, f32[5,6,3,1024]{3,2,1,0:T(4,128)}, u32[]{:S(2)}, u32[]{:S(2)}) collective-permute-start(f32[5,6,3,1024]{3,2,1,0:T(4,128)} %get-tuple-element.139), channel_id=1, source_target_pairs={{0,1},{1,2},{2,3},{4,5},{5,6},{6,7},{8,9},{9,10},{10,11},{12,13},{... | collective-permute-start | bytes 1105928 | tf_op jit(solution)/shard_map/ppermute | solution.py:20
  13.8 2.6 %collective-permute-start.1 = (f32[5,6,3,1024]{3,2,1,0:T(4,128)S(1)}, f32[5,6,3,1024]{3,2,1,0:T(4,128)}, u32[]{:S(2)}, u32[]{:S(2)}) collective-permute-start(f32[5,6,3,1024]{3,2,1,0:T(4,128)S(1)} %get-tuple-element.140), channel_id=1, source_target_pairs={{1,0},{2,1},{3,2},{5,4},{6,5},{7,6},{9,8},{10,9},{11,10},{13,12},{... | collective-permute-start | bytes 1105928 | tf_op jit(solution)/shard_map/ppermute | solution.py:22
  16.5 3.0 %rev.2 = f32[5,3,8,1024]{3,2,1,0:T(8,128)} reverse(f32[5,3,8,1024]{3,2,1,0:T(8,128)S(1)} %slice_select_fusion), dimensions={3} | reverse | bytes 983040 | tf_op jit(solution)/shard_map/rev | solution.py:278
  19.6 0.7 fusion.232
  20.4 0.9 collective-permute-start.2
  21.3 6.1 %collective-permute-start.3 = (f32[5,6,8,3]{3,2,1,0:T(8,128)S(1)}, f32[5,6,8,3]{3,2,1,0:T(8,128)}, u32[]{:S(2)}, u32[]{:S(2)}) collective-permute-start(f32[5,6,8,3]{3,2,1,0:T(8,128)S(1)} %get-tuple-element.131), channel_id=1, source_target_pairs={{4,0},{8,4},{12,8},{16,12},{20,16},{24,20},{28,24},{32,28},{36,32}... | collective-permute-start | bytes 8648 | tf_op jit(solution)/shard_map/ppermute | solution.py:22
  27.4 0.1 fusion.233
  27.6 1.4 fusion.230
  29.0 0.8 fusion.231
  30.6 0.3 slice.888
  31.0 2.6 %slice.890 = f32[1,6,3,1024]{3,2,1,0:T(4,128)} reverse(f32[1,6,3,1024]{3,2,1,0:T(4,128)S(1)} %get-tuple-element.138), dimensions={2} | reverse | bytes 147456 | tf_op jit(solution)/shard_map/slice | solution.py:174
  33.5 0.5 slice.886
  34.1 0.3 slice.896
  34.4 0.3 slice.898
  34.8 0.5 slice.894
  35.4 0.6 copy-done.11
  36.0 1.5 concatenate.59
  37.6 1.2 maximum_select_fusion.3
  38.8 1.2 maximum_select_fusion.4
  40.1 0.4 pad_maximum_fusion
  40.5 0.4 fusion.2
  41.0 0.4 broadcast_multiply_fusion
  41.4 0.2 slice_add_fusion.2
  41.8 12.4 %constant_dynamic-update-slice_fusion = (f32[5,6,9,1024]{3,2,1,0:T(8,128)S(1)}, f32[1,6,9,1024]{3,2,1,0:T(8,128)S(1)}, f32[1,6,9,1024]{3,2,1,0:T(8,128)S(1)}, f3...) fusion(f32[1,6,14,1024]{3,2,1,0:T(8,128)S(1)} %get-tuple-elemen, ...), kind=kLoop, calls=%fused_computation.411 | loop fusion | flops 42190848 | bytes 22044672
  54.2 2.8 %add_dynamic-update-slice_fusion.3 = (f32[5,6,9,1024]{3,2,1,0:T(8,128)S(1)}, f32[1,6,9,1024]{3,2,1,0:T(8,128)S(1)}) fusion(f32[5,6,9,1024]{3,2,1,0:T(8,128)S(1)} %get-tuple-element.93, f32[1,6,9,1024]{3,2,1,0:T(8,128)S(1)} %get-tuple-element.110, f32[1,6,9,1024]{3,2,1,0:T(8,128)S(1)} %get-tuple-element.94, f32[1,6,9,1024]{3,2,1,0:T(8,128)S(1)} %get-tuple-element.120, ...), kind=kLoop, calls=%fused_computation.171 | loop fusion | flops 9897984 | bytes 11010048
  57.0 2.8 %add_dynamic-update-slice_fusion.2 = (f32[5,6,9,1024]{3,2,1,0:T(8,128)S(1)}, f32[1,6,9,1024]{3,2,1,0:T(8,128)S(1)}) fusion(f32[5,6,9,1024]{3,2,1,0:T(8,128)S(1)} %get-tuple-element.91, f32[1,6,9,1024]{3,2,1,0:T(8,128)S(1)} %get-tuple-element.111, f32[1,6,9,1024]{3,2,1,0:T(8,128)S(1)} %get-tuple-element.94, f32[1,6,9,1024]{3,2,1,0:T(8,128)S(1)} %get-tuple-element.120, ...), kind=kLoop, calls=%fused_computation.163 | loop fusion | flops 9897984 | bytes 11010048
  59.9 9.8 %add_dynamic-update-slice_fusion.1 = (f32[5,6,9,1024]{3,2,1,0:T(8,128)S(1)}, f32[1,6,9,1024]{3,2,1,0:T(8,128)S(1)}, f32[1,6,9,1024]{3,2,1,0:T(8,128)S(1)}, f32[1,6,9,1024]{3,2,1,0:T(8,128)S(1)}) fusion(f32[5,6,9,1024]{3,2,1,0:T(8,128)S(1)} %get-tuple-element.89, f32[1,6,9,1024]{3,2,1,0:T(8,128)S(1)} %get-tuple-element.97, ...), kind=kLoop, calls=%fused_computation.140 | loop fusion | flops 35665920 | bytes 17694720
  69.7 0.5 add_dynamic-update-slice_fusion
  70.2 0.2 slice_subtract_fusion.2
  70.4 0.2 copy.4
  70.6 0.9 copy-done.1
  71.5 0.5 slice.1176
  73.3 0.8 all-gather.6.cloned.1.call-done
  74.0 1.1 constant_dynamic-slice_fusion.1
  75.2 0.6 slice.1177
  77.1 1.7 %fusion.5 = f32[5,6,8,1025]{3,2,1,0:T(8,128)} fusion(f32[5,6,8,1030]{3,2,1,0:T(8,128)S(1)} %broadcast_select_fusion), kind=kLoop, calls=%fused_computation.70 | loop fusion | flops 492000 | bytes 2952000 | tf_op jit(solution)/shard_map/mul | solution.py:88
  79.0 1.1 copy-done.3
  80.1 6.4 %constant_dynamic-update-slice_fusion.1 = (f32[5,6,8,1025]{3,2,1,0:T(8,128)S(1)}, f32[1,6,8,1025]{3,2,1,0:T(8,128)S(1)}, f32[1,6,8,1025]{3,2,1,0:T(8,128)S(1)}, ...) fusion(f32[5,6,8,1030]{3,2,1,0:T(8,128)S(1)} %broadcast_select_, ...), kind=kLoop, calls=%fused_computation.412 | loop fusion | flops 35768400 | bytes 17215680
  86.5 1.5 add_dynamic-update-slice_fusion.7
  88.0 5.7 %add_dynamic-update-slice_fusion.6 = (f32[5,6,8,1025]{3,2,1,0:T(8,128)S(1)}, f32[1,6,8,1025]{3,2,1,0:T(8,128)S(1)}, f32[1,6,8,1025]{3,2,1,0:T(8,128)S(1)}, f32[1,6,8,1025]{3,2,1,0:T(8,128)S(1)}) fusion(f32[5,6,8,1025]{3,2,1,0:T(8,128)S(1)} %get-tuple-element.61, f32[1,6,8,1025]{3,2,1,0:T(8,128)S(1)} %get-tuple-element.67, ...), kind=kLoop, calls=%fused_computation.294 | loop fusion | flops 31734000 | bytes 9953280
  93.7 1.5 add_dynamic-update-slice_fusion.5
  95.3 0.3 add_dynamic-update-slice_fusion.4
  95.6 1.3 copy-done.2
  96.8 0.6 multiply_add_fusion
  97.5 0.2 copy.6
  97.7 0.5 slice.1254
  99.5 10.3 %all-gather.4.cloned.1.call-done = f32[4,5,3,8,1024]{4,3,2,1,0:T(8,128)} async-done(((f32[1,5,3,8,1024]{4,3,2,1,0:T(8,128)}), f32[4,5,3,8,1024]{4,3,2,1,0:T(8,128)}) %all-gather.4.cloned.1.call-update) | async-done | bytes 1966096 | tf_op jit(solution)/shard_map/all_gather | solution.py:208
  109.8 1.1 fusion.237
  110.9 3.8 %collective-permute-start.4 = (f32[5,3,8,1024]{3,2,1,0:T(8,128)S(1)}, f32[5,3,8,1024]{3,2,1,0:T(8,128)S(1)}, u32[]{:S(2)}, u32[]{:S(2)}) collective-permute-start(f32[5,3,8,1024]{3,2,1,0:T(8,128)S(1)} %fusion.237), channel_id=1, source_target_pairs={{0,132},{4,136},{8,140},{12,144},{16,148},{20,152},{24,156},{28,16... | collective-permute-start | bytes 1474568 | tf_op jit(solution)/shard_map/ppermute | solution.py:224
  114.7 0.2 collective-permute-start.5
  114.9 1.1 constant_dynamic-slice_fusion
  116.1 0.6 slice.1255
  118.0 1.4 fusion.4.padded_ref
  119.4 7.3 %shard_map.37 = f32[5,4,8,1024]{3,2,1,0:T(8,128)} custom-call(f32[5,9,8,1024]{3,2,1,0:T(8,128)} %fusion.4.padded_ref), custom_call_target="tpu_custom_call" | custom-call | tf_op jit(solution)/shard_map/pallas_call | solution.py:251
  126.7 1.2 broadcast_add_fusion
  128.0 0.5 slice.1257
  129.8 9.6 %collective-permute-done.5 = f32[5,3,8,1024]{3,2,1,0:T(8,128)} collective-permute-done((f32[5,3,8,1024]{3,2,1,0:T(8,128)S(1)}, f32[5,3,8,1024]{3,2,1,0:T(8,128)}, u32[]{:S(2)}, u32[]{:S(2)}) %collective-permute-start.5) | collective-permute-done | bytes 491552 | tf_op jit(solution)/shard_map/ppermute | solution.py:224
  139.4 1.3 fusion.8
  140.7 0.2 fusion.9
  141.0 1.3 maximum_select_fusion.1.padded_ref
  142.2 5.9 %shard_map.38 = f32[5,3,8,1024]{3,2,1,0:T(8,128)} custom-call(f32[5,8,8,1024]{3,2,1,0:T(8,128)} %maximum_select_fusion.1.padded_ref), custom_call_target="tpu_custom_call" | custom-call | tf_op jit(solution)/shard_map/pallas_call | solution.py:251
  148.1 1.4 maximum_select_fusion.2
  149.5 1.2 fusion.7
  (46 shorter events, 1.2 us)
Async XLA Ops:
  6.5 9.9 %copy-start = (f32[5,6,8,1024]{3,2,1,0:T(8,128)S(1)}, f32[5,6,8,1024]{3,2,1,0:T(8,128)}, u32[]{:S(2)}) copy-start(f32[5,6,8,1024]{3,2,1,0:T(8,128)} %param.12) | copy-start | bytes 2949124
  6.5 67.5 %all-gather.6.cloned.1.call-start = ((), (), s32[]{:S(2)}) async-start(), calls=%async_computation.1 | async-start | bytes 4423680 | tf_op jit(solution)/shard_map/all_gather | solution.py:200
  9.2 28.4 %collective-permute-start = (f32[5,6,3,1024]{3,2,1,0:T(4,128)}, f32[5,6,3,1024]{3,2,1,0:T(4,128)}, u32[]{:S(2)}, u32[]{:S(2)}) collective-permute-start(f32[5,6,3,1024]{3,2,1,0:T(4,128)} %get-tuple-element.139), channel_id=1, source_target_pairs={{0,1},{1,2},{2,3},{4,5},{5,6},{6,7},{8,9},{9,10},{10,11},{12,13},{... | collective-permute-start | bytes 1105928 | tf_op jit(solution)/shard_map/ppermute | solution.py:20
  13.8 25.0 %collective-permute-start.1 = (f32[5,6,3,1024]{3,2,1,0:T(4,128)S(1)}, f32[5,6,3,1024]{3,2,1,0:T(4,128)}, u32[]{:S(2)}, u32[]{:S(2)}) collective-permute-start(f32[5,6,3,1024]{3,2,1,0:T(4,128)S(1)} %get-tuple-element.140), channel_id=1, source_target_pairs={{1,0},{2,1},{3,2},{5,4},{6,5},{7,6},{9,8},{10,9},{11,10},{13,12},{... | collective-permute-start | bytes 1105928 | tf_op jit(solution)/shard_map/ppermute | solution.py:22
  19.6 90.2 %all-gather.4.cloned.1.call-start = ((), (), s32[]{:S(2)}) async-start(), calls=%async_computation | async-start | bytes 2457600 | tf_op jit(solution)/shard_map/all_gather | solution.py:208
  20.4 15.0 %collective-permute-start.2 = (f32[5,6,8,3]{3,2,1,0:T(8,128)}, f32[5,6,8,3]{3,2,1,0:T(8,128)S(1)}, u32[]{:S(2)}, u32[]{:S(2)}) collective-permute-start(f32[5,6,8,3]{3,2,1,0:T(8,128)} %get-tuple-element.132), channel_id=1, source_target_pairs={{0,4},{4,8},{8,12},{12,16},{16,20},{20,24},{24,28},{28,32},{32,36}... | collective-permute-start | bytes 8648 | tf_op jit(solution)/shard_map/ppermute | solution.py:20
  21.3 14.7 %collective-permute-start.3 = (f32[5,6,8,3]{3,2,1,0:T(8,128)S(1)}, f32[5,6,8,3]{3,2,1,0:T(8,128)}, u32[]{:S(2)}, u32[]{:S(2)}) collective-permute-start(f32[5,6,8,3]{3,2,1,0:T(8,128)S(1)} %get-tuple-element.131), channel_id=1, source_target_pairs={{4,0},{8,4},{12,8},{16,12},{20,16},{24,20},{28,24},{32,28},{36,32}... | collective-permute-start | bytes 8648 | tf_op jit(solution)/shard_map/ppermute | solution.py:22
  35.4 0.6 copy-start.11
  70.2 1.3 copy-start.1
  75.1 1.8 %copy-start.5 = (f32[1,5,3,8,1024]{4,3,2,1,0:T(8,128)}, f32[1,5,3,8,1024]{4,3,2,1,0:T(8,128)S(1)}, u32[]{:S(2)}) copy-start(f32[1,5,3,8,1024]{4,3,2,1,0:T(8,128)S(1)} %constant_dynamic-slice_fusion.1) | copy-start | bytes 1474564
  78.9 1.2 copy-start.3
  93.7 1.8 %copy-start.8 = (f32[5,6,8,1024]{3,2,1,0:T(8,128)S(1)}, f32[5,6,8,1024]{3,2,1,0:T(8,128)}, u32[]{:S(2)}) copy-start(f32[5,6,8,1024]{3,2,1,0:T(8,128)} %param.11) | copy-start | bytes 2949124
  95.3 1.6 %copy-start.2 = (f32[5,6,9,1024]{3,2,1,0:T(8,128)S(1)}, f32[5,6,9,1024]{3,2,1,0:T(8,128)}, u32[]{:S(2)}) copy-start(f32[5,6,9,1024]{3,2,1,0:T(8,128)} %copy-done.1) | copy-start | bytes 3317764
  97.7 20.3 %copy-start.9 = (f32[5,1,8,1024]{3,2,1,0:T(8,128)S(1)}, f32[5,1,8,1024]{3,2,1,0:T(8,128)}, u32[]{:S(2)}) copy-start(f32[5,1,8,1024]{3,2,1,0:T(8,128)} %get-tuple-element.129) | copy-start | bytes 491524
  97.7 20.3 %copy-start.10 = (f32[5,1,8,1024]{3,2,1,0:T(8,128)S(1)}, f32[5,1,8,1024]{3,2,1,0:T(8,128)}, u32[]{:S(2)}) copy-start(f32[5,1,8,1024]{3,2,1,0:T(8,128)} %get-tuple-element.130) | copy-start | bytes 491524
  110.9 19.0 %collective-permute-start.4 = (f32[5,3,8,1024]{3,2,1,0:T(8,128)S(1)}, f32[5,3,8,1024]{3,2,1,0:T(8,128)S(1)}, u32[]{:S(2)}, u32[]{:S(2)}) collective-permute-start(f32[5,3,8,1024]{3,2,1,0:T(8,128)S(1)} %fusion.237), channel_id=1, source_target_pairs={{0,132},{4,136},{8,140},{12,144},{16,148},{20,152},{24,156},{28,16... | collective-permute-start | bytes 1474568 | tf_op jit(solution)/shard_map/ppermute | solution.py:224
  114.7 24.7 %collective-permute-start.5 = (f32[5,3,8,1024]{3,2,1,0:T(8,128)S(1)}, f32[5,3,8,1024]{3,2,1,0:T(8,128)}, u32[]{:S(2)}, u32[]{:S(2)}) collective-permute-start(f32[5,3,8,1024]{3,2,1,0:T(8,128)S(1)} %fusion.237), channel_id=1, source_target_pairs={{0,128},{4,132},{8,136},{12,140},{16,144},{20,148},{24,152},{28,15... | collective-permute-start | bytes 1474568 | tf_op jit(solution)/shard_map/ppermute | solution.py:224
  129.8 11.1 %copy-start.6 = (f32[5,5,8,1024]{3,2,1,0:T(8,128)S(1)}, f32[5,5,8,1024]{3,2,1,0:T(8,128)}, u32[]{:S(2)}) copy-start(f32[5,5,8,1024]{3,2,1,0:T(8,128)} %get-tuple-element.127) | copy-start | bytes 2457604
  129.8 11.1 %copy-start.7 = (f32[5,5,8,1024]{3,2,1,0:T(8,128)S(1)}, f32[5,5,8,1024]{3,2,1,0:T(8,128)}, u32[]{:S(2)}) copy-start(f32[5,5,8,1024]{3,2,1,0:T(8,128)} %get-tuple-element.128) | copy-start | bytes 2457604
  141.0 7.2 %copy-start.4 = (f32[5,4,8,1024]{3,2,1,0:T(8,128)S(1)}, f32[5,4,8,1024]{3,2,1,0:T(8,128)}, u32[]{:S(2)}) copy-start(f32[5,4,8,1024]{3,2,1,0:T(8,128)} %shard_map.37) | copy-start | bytes 1966084
Sparse Core Ops, SparseCore 0:
  19.7 54.2 all-gather.5
  78.9 30.8 all-gather.3

commit v5 on v3

--- a/solution.py
+++ b/solution.py
@@ -76,7 +76,31 @@
     )
 
 
-def face_flux(padded, fluxes, axis, count, normal, first, second):
+def weno_merged(far_left, left_cell, centre, right_cell, far_right):
+    smooth_low = 13.0 / 12.0 * jnp.square(far_left - 2.0 * left_cell + centre) + 0.25 * jnp.square(
+        far_left - 4.0 * left_cell + 3.0 * centre
+    )
+    smooth_mid = 13.0 / 12.0 * jnp.square(
+        left_cell - 2.0 * centre + right_cell
+    ) + 0.25 * jnp.square(left_cell - right_cell)
+    smooth_high = 13.0 / 12.0 * jnp.square(
+        centre - 2.0 * right_cell + far_right
+    ) + 0.25 * jnp.square(3.0 * centre - 4.0 * right_cell + far_right)
+    spread_low = jnp.square(weno_epsilon + smooth_low)
+    spread_mid = jnp.square(weno_epsilon + smooth_mid)
+    spread_high = jnp.square(weno_epsilon + smooth_high)
+    weight_low = 0.1 * (spread_mid * spread_high)
+    weight_mid = 0.6 * (spread_low * spread_high)
+    weight_high = 0.3 * (spread_low * spread_mid)
+    guess_low = 2.0 * far_left - 7.0 * left_cell + 11.0 * centre
+    guess_mid = -left_cell + 5.0 * centre + 2.0 * right_cell
+    guess_high = 2.0 * centre + 5.0 * right_cell - far_right
+    return (weight_low * guess_low + weight_mid * guess_mid + weight_high * guess_high) / (
+        6.0 * (weight_low + weight_mid + weight_high)
+    )
+
+
+def face_flux(padded, fluxes, axis, count, normal, first, second, weno=weno_side):
     states = [
         lax.slice_in_dim(padded, shift_index, shift_index + count + 1, axis=axis)
         for shift_index in range(6)
@@ -138,8 +162,8 @@
             for cell in range(6)
         ]
         recon.append(
-            weno_side(plus_vals[0], plus_vals[1], plus_vals[2], plus_vals[3], plus_vals[4])
-            + weno_side(minus_vals[5], minus_vals[4], minus_vals[3], minus_vals[2], minus_vals[1])
+            weno(plus_vals[0], plus_vals[1], plus_vals[2], plus_vals[3], plus_vals[4])
+            + weno(minus_vals[5], minus_vals[4], minus_vals[3], minus_vals[2], minus_vals[1])
         )
     wave_minus, entropy, shear_first, shear_second, wave_plus = recon
     acoustic = wave_minus + entropy + wave_plus
@@ -239,7 +263,7 @@
     parts = [padded[index_part] * velocity for index_part in range(5)]
     parts[1] = parts[1] + pressure
     parts[4] = parts[4] + pressure * velocity
-    faces = face_flux(padded, jnp.stack(parts), 1, count, 1, 2, 3)
+    faces = face_flux(padded, jnp.stack(parts), 1, count, 1, 2, 3, weno_merged)
     out_ref[...] = faces
 
 

time: 158 us -> 158 us (level)
  no operation moved by 1% of the time
where the time goes in v5:
time: 158 us; the launch traced here: 157 us
  other arithmetic  58.7 us (37%)
  local copies, waits for them, and re-layouts  25.7 us (16%)
  between operations  21 us (13%)
  waiting for transfers between devices  20.9 us (13%)
  starting transfers between devices  18.4 us (12%)
  Pallas kernels  12.7 us (8%)
    unnamed x8, other arithmetic  43 us
    pallas_call x2, Pallas kernels, axial_faces(): pl.pallas_call(axial_kernel, grid=(width // lanes,), in_specs=[pl.BlockSp...  12.7 us
    all_gather x1, waiting for transfers between devices, pick_row(): gathered = lax.all_gather(slab, 'tx')  10.3 us
    ppermute x1, waiting for transfers between devices, cross_blocks(): lax.ppermute(slab, axes, this_route)  9.82 us
    ppermute x2, starting transfers between devices, padded_2(): lax.ppermute(head, axis, [((i + 1) % count, i) for i in range(ends)])  8.79 us
    ppermute x2, starting transfers between devices, padded_2(): lax.ppermute(tail, axis, [(i, (i + 1) % count) for i in range(ends)])  5.49 us
    slice x8, local copies, waits for them, and re-layouts, flip_radial(): return jnp.concatenate([turned[:3], -turned[3:4], turned[4:]], axis=0)  4.85 us
    unnamed x29, local copies, waits for them, and re-layouts  4.66 us
  transfers between devices with their start and end apart: 8, of which 3 were waited for; matrix products, arithmetic and copies ran while one was open for 43% of the time, Pallas kernels for 4%

profile of v5, /device:TPU:1, one launch (start us, length us, event | category | flops | bytes accessed | tf_op | source)
XLA Modules:
  0.0 157.4 jit_solution(17098288363924295799)
XLA Ops:
  6.5 2.7 %fusion.235 = (f32[5,6,3,1024]{3,2,1,0:T(4,128)}, f32[5,6,3,1024]{3,2,1,0:T(4,128)S(1)}) fusion(f32[5,6,8,1024]{3,2,1,0:T(8,128)} %param.12), kind=kLoop, calls=%fused_computation.447 | loop fusion | bytes 1474560 | tf_op jit(solution)/shard_map/slice | solution.py:17
  9.2 4.6 %collective-permute-start = (f32[5,6,3,1024]{3,2,1,0:T(4,128)}, f32[5,6,3,1024]{3,2,1,0:T(4,128)}, u32[]{:S(2)}, u32[]{:S(2)}) collective-permute-start(f32[5,6,3,1024]{3,2,1,0:T(4,128)} %get-tuple-element.139), channel_id=1, source_target_pairs={{0,1},{1,2},{2,3},{4,5},{5,6},{6,7},{8,9},{9,10},{10,11},{12,13},{... | collective-permute-start | bytes 1105928 | tf_op jit(solution)/shard_map/ppermute | solution.py:20
  13.8 2.6 %collective-permute-start.1 = (f32[5,6,3,1024]{3,2,1,0:T(4,128)S(1)}, f32[5,6,3,1024]{3,2,1,0:T(4,128)}, u32[]{:S(2)}, u32[]{:S(2)}) collective-permute-start(f32[5,6,3,1024]{3,2,1,0:T(4,128)S(1)} %get-tuple-element.140), channel_id=1, source_target_pairs={{1,0},{2,1},{3,2},{5,4},{6,5},{7,6},{9,8},{10,9},{11,10},{13,12},{... | collective-permute-start | bytes 1105928 | tf_op jit(solution)/shard_map/ppermute | solution.py:22
  16.5 3.0 %rev.2 = f32[5,3,8,1024]{3,2,1,0:T(8,128)} reverse(f32[5,3,8,1024]{3,2,1,0:T(8,128)S(1)} %slice_select_fusion), dimensions={3} | reverse | bytes 983040 | tf_op jit(solution)/shard_map/rev | solution.py:302
  19.6 0.7 fusion.232
  20.4 0.9 collective-permute-start.2
  21.3 6.1 %collective-permute-start.3 = (f32[5,6,8,3]{3,2,1,0:T(8,128)S(1)}, f32[5,6,8,3]{3,2,1,0:T(8,128)}, u32[]{:S(2)}, u32[]{:S(2)}) collective-permute-start(f32[5,6,8,3]{3,2,1,0:T(8,128)S(1)} %get-tuple-element.131), channel_id=1, source_target_pairs={{4,0},{8,4},{12,8},{16,12},{20,16},{24,20},{28,24},{32,28},{36,32}... | collective-permute-start | bytes 8648 | tf_op jit(solution)/shard_map/ppermute | solution.py:22
  27.4 0.1 fusion.233
  27.6 1.4 fusion.230
  29.0 0.8 fusion.231
  30.6 0.3 slice.888
  31.0 2.6 %slice.890 = f32[1,6,3,1024]{3,2,1,0:T(4,128)} reverse(f32[1,6,3,1024]{3,2,1,0:T(4,128)S(1)} %get-tuple-element.138), dimensions={2} | reverse | bytes 147456 | tf_op jit(solution)/shard_map/slice | solution.py:198
  33.5 0.5 slice.886
  34.1 0.3 slice.896
  34.4 0.3 slice.898
  34.8 0.5 slice.894
  35.4 0.6 copy-done.11
  36.0 1.5 concatenate.59
  37.6 1.2 maximum_select_fusion.3
  38.8 1.2 maximum_select_fusion.4
  40.1 0.4 pad_maximum_fusion
  40.5 0.4 fusion.2
  41.0 0.4 broadcast_multiply_fusion
  41.4 0.2 slice_add_fusion.2
  41.8 12.4 %constant_dynamic-update-slice_fusion = (f32[5,6,9,1024]{3,2,1,0:T(8,128)S(1)}, f32[1,6,9,1024]{3,2,1,0:T(8,128)S(1)}, f32[1,6,9,1024]{3,2,1,0:T(8,128)S(1)}, f3...) fusion(f32[1,6,14,1024]{3,2,1,0:T(8,128)S(1)} %get-tuple-elemen, ...), kind=kLoop, calls=%fused_computation.411 | loop fusion | flops 42190848 | bytes 22044672
  54.2 2.8 %add_dynamic-update-slice_fusion.3 = (f32[5,6,9,1024]{3,2,1,0:T(8,128)S(1)}, f32[1,6,9,1024]{3,2,1,0:T(8,128)S(1)}) fusion(f32[5,6,9,1024]{3,2,1,0:T(8,128)S(1)} %get-tuple-element.93, f32[1,6,9,1024]{3,2,1,0:T(8,128)S(1)} %get-tuple-element.110, f32[1,6,9,1024]{3,2,1,0:T(8,128)S(1)} %get-tuple-element.94, f32[1,6,9,1024]{3,2,1,0:T(8,128)S(1)} %get-tuple-element.120, ...), kind=kLoop, calls=%fused_computation.171 | loop fusion | flops 9897984 | bytes 11010048
  57.0 2.8 %add_dynamic-update-slice_fusion.2 = (f32[5,6,9,1024]{3,2,1,0:T(8,128)S(1)}, f32[1,6,9,1024]{3,2,1,0:T(8,128)S(1)}) fusion(f32[5,6,9,1024]{3,2,1,0:T(8,128)S(1)} %get-tuple-element.91, f32[1,6,9,1024]{3,2,1,0:T(8,128)S(1)} %get-tuple-element.111, f32[1,6,9,1024]{3,2,1,0:T(8,128)S(1)} %get-tuple-element.94, f32[1,6,9,1024]{3,2,1,0:T(8,128)S(1)} %get-tuple-element.120, ...), kind=kLoop, calls=%fused_computation.163 | loop fusion | flops 9897984 | bytes 11010048
  59.9 9.8 %add_dynamic-update-slice_fusion.1 = (f32[5,6,9,1024]{3,2,1,0:T(8,128)S(1)}, f32[1,6,9,1024]{3,2,1,0:T(8,128)S(1)}, f32[1,6,9,1024]{3,2,1,0:T(8,128)S(1)}, f32[1,6,9,1024]{3,2,1,0:T(8,128)S(1)}) fusion(f32[5,6,9,1024]{3,2,1,0:T(8,128)S(1)} %get-tuple-element.89, f32[1,6,9,1024]{3,2,1,0:T(8,128)S(1)} %get-tuple-element.97, ...), kind=kLoop, calls=%fused_computation.140 | loop fusion | flops 35665920 | bytes 17694720
  69.7 0.5 add_dynamic-update-slice_fusion
  70.2 0.2 slice_subtract_fusion.2
  70.4 0.2 copy.4
  70.6 0.9 copy-done.1
  71.5 0.5 slice.1176
  73.3 0.8 all-gather.6.cloned.1.call-done
  74.0 1.1 constant_dynamic-slice_fusion.1
  75.2 0.6 slice.1177
  77.1 1.7 %fusion.5 = f32[5,6,8,1025]{3,2,1,0:T(8,128)} fusion(f32[5,6,8,1030]{3,2,1,0:T(8,128)S(1)} %broadcast_select_fusion), kind=kLoop, calls=%fused_computation.70 | loop fusion | flops 492000 | bytes 2952000 | tf_op jit(solution)/shard_map/mul | solution.py:112
  79.0 1.1 copy-done.3
  80.1 6.4 %constant_dynamic-update-slice_fusion.1 = (f32[5,6,8,1025]{3,2,1,0:T(8,128)S(1)}, f32[1,6,8,1025]{3,2,1,0:T(8,128)S(1)}, f32[1,6,8,1025]{3,2,1,0:T(8,128)S(1)}, ...) fusion(f32[5,6,8,1030]{3,2,1,0:T(8,128)S(1)} %broadcast_select_, ...), kind=kLoop, calls=%fused_computation.412 | loop fusion | flops 35768400 | bytes 17215680
  86.5 1.5 add_dynamic-update-slice_fusion.7
  88.0 5.7 %add_dynamic-update-slice_fusion.6 = (f32[5,6,8,1025]{3,2,1,0:T(8,128)S(1)}, f32[1,6,8,1025]{3,2,1,0:T(8,128)S(1)}, f32[1,6,8,1025]{3,2,1,0:T(8,128)S(1)}, f32[1,6,8,1025]{3,2,1,0:T(8,128)S(1)}) fusion(f32[5,6,8,1025]{3,2,1,0:T(8,128)S(1)} %get-tuple-element.61, f32[1,6,8,1025]{3,2,1,0:T(8,128)S(1)} %get-tuple-element.67, ...), kind=kLoop, calls=%fused_computation.294 | loop fusion | flops 31734000 | bytes 9953280
  93.7 1.5 add_dynamic-update-slice_fusion.5
  95.3 0.3 add_dynamic-update-slice_fusion.4
  95.6 1.3 copy-done.2
  96.8 0.6 multiply_add_fusion
  97.5 0.2 copy.6
  97.7 0.5 slice.1254
  99.5 10.3 %all-gather.4.cloned.1.call-done = f32[4,5,3,8,1024]{4,3,2,1,0:T(8,128)} async-done(((f32[1,5,3,8,1024]{4,3,2,1,0:T(8,128)}), f32[4,5,3,8,1024]{4,3,2,1,0:T(8,128)}) %all-gather.4.cloned.1.call-update) | async-done | bytes 1966096 | tf_op jit(solution)/shard_map/all_gather | solution.py:232
  109.8 1.1 fusion.237
  110.9 3.8 %collective-permute-start.4 = (f32[5,3,8,1024]{3,2,1,0:T(8,128)S(1)}, f32[5,3,8,1024]{3,2,1,0:T(8,128)S(1)}, u32[]{:S(2)}, u32[]{:S(2)}) collective-permute-start(f32[5,3,8,1024]{3,2,1,0:T(8,128)S(1)} %fusion.237), channel_id=1, source_target_pairs={{0,132},{4,136},{8,140},{12,144},{16,148},{20,152},{24,156},{28,16... | collective-permute-start | bytes 1474568 | tf_op jit(solution)/shard_map/ppermute | solution.py:248
  114.7 0.2 collective-permute-start.5
  114.9 1.1 constant_dynamic-slice_fusion
  116.1 0.6 slice.1255
  118.0 1.4 fusion.4.padded_ref
  119.4 7.0 %shard_map.37 = f32[5,4,8,1024]{3,2,1,0:T(8,128)} custom-call(f32[5,9,8,1024]{3,2,1,0:T(8,128)} %fusion.4.padded_ref), custom_call_target="tpu_custom_call" | custom-call | tf_op jit(solution)/shard_map/pallas_call | solution.py:275
  126.4 1.2 broadcast_add_fusion
  127.8 0.5 slice.1257
  129.6 9.8 %collective-permute-done.5 = f32[5,3,8,1024]{3,2,1,0:T(8,128)} collective-permute-done((f32[5,3,8,1024]{3,2,1,0:T(8,128)S(1)}, f32[5,3,8,1024]{3,2,1,0:T(8,128)}, u32[]{:S(2)}, u32[]{:S(2)}) %collective-permute-start.5) | collective-permute-done | bytes 491552 | tf_op jit(solution)/shard_map/ppermute | solution.py:248
  139.4 1.4 fusion.8
  140.8 0.2 fusion.9
  141.1 1.3 maximum_select_fusion.1.padded_ref
  142.3 5.7 %shard_map.38 = f32[5,3,8,1024]{3,2,1,0:T(8,128)} custom-call(f32[5,8,8,1024]{3,2,1,0:T(8,128)} %maximum_select_fusion.1.padded_ref), custom_call_target="tpu_custom_call" | custom-call | tf_op jit(solution)/shard_map/pallas_call | solution.py:275
  148.0 1.4 maximum_select_fusion.2
  149.4 1.2 fusion.7
  (46 shorter events, 1.2 us)
Async XLA Ops:
  6.5 9.9 %copy-start = (f32[5,6,8,1024]{3,2,1,0:T(8,128)S(1)}, f32[5,6,8,1024]{3,2,1,0:T(8,128)}, u32[]{:S(2)}) copy-start(f32[5,6,8,1024]{3,2,1,0:T(8,128)} %param.12) | copy-start | bytes 2949124
  6.5 67.5 %all-gather.6.cloned.1.call-start = ((), (), s32[]{:S(2)}) async-start(), calls=%async_computation.1 | async-start | bytes 4423680 | tf_op jit(solution)/shard_map/all_gather | solution.py:224
  9.2 28.4 %collective-permute-start = (f32[5,6,3,1024]{3,2,1,0:T(4,128)}, f32[5,6,3,1024]{3,2,1,0:T(4,128)}, u32[]{:S(2)}, u32[]{:S(2)}) collective-permute-start(f32[5,6,3,1024]{3,2,1,0:T(4,128)} %get-tuple-element.139), channel_id=1, source_target_pairs={{0,1},{1,2},{2,3},{4,5},{5,6},{6,7},{8,9},{9,10},{10,11},{12,13},{... | collective-permute-start | bytes 1105928 | tf_op jit(solution)/shard_map/ppermute | solution.py:20
  13.8 25.0 %collective-permute-start.1 = (f32[5,6,3,1024]{3,2,1,0:T(4,128)S(1)}, f32[5,6,3,1024]{3,2,1,0:T(4,128)}, u32[]{:S(2)}, u32[]{:S(2)}) collective-permute-start(f32[5,6,3,1024]{3,2,1,0:T(4,128)S(1)} %get-tuple-element.140), channel_id=1, source_target_pairs={{1,0},{2,1},{3,2},{5,4},{6,5},{7,6},{9,8},{10,9},{11,10},{13,12},{... | collective-permute-start | bytes 1105928 | tf_op jit(solution)/shard_map/ppermute | solution.py:22
  19.6 90.2 %all-gather.4.cloned.1.call-start = ((), (), s32[]{:S(2)}) async-start(), calls=%async_computation | async-start | bytes 2457600 | tf_op jit(solution)/shard_map/all_gather | solution.py:232
  20.4 15.0 %collective-permute-start.2 = (f32[5,6,8,3]{3,2,1,0:T(8,128)}, f32[5,6,8,3]{3,2,1,0:T(8,128)S(1)}, u32[]{:S(2)}, u32[]{:S(2)}) collective-permute-start(f32[5,6,8,3]{3,2,1,0:T(8,128)} %get-tuple-element.132), channel_id=1, source_target_pairs={{0,4},{4,8},{8,12},{12,16},{16,20},{20,24},{24,28},{28,32},{32,36}... | collective-permute-start | bytes 8648 | tf_op jit(solution)/shard_map/ppermute | solution.py:20
  21.3 14.7 %collective-permute-start.3 = (f32[5,6,8,3]{3,2,1,0:T(8,128)S(1)}, f32[5,6,8,3]{3,2,1,0:T(8,128)}, u32[]{:S(2)}, u32[]{:S(2)}) collective-permute-start(f32[5,6,8,3]{3,2,1,0:T(8,128)S(1)} %get-tuple-element.131), channel_id=1, source_target_pairs={{4,0},{8,4},{12,8},{16,12},{20,16},{24,20},{28,24},{32,28},{36,32}... | collective-permute-start | bytes 8648 | tf_op jit(solution)/shard_map/ppermute | solution.py:22
  35.4 0.6 copy-start.11
  70.2 1.3 copy-start.1
  75.1 1.8 %copy-start.5 = (f32[1,5,3,8,1024]{4,3,2,1,0:T(8,128)}, f32[1,5,3,8,1024]{4,3,2,1,0:T(8,128)S(1)}, u32[]{:S(2)}) copy-start(f32[1,5,3,8,1024]{4,3,2,1,0:T(8,128)S(1)} %constant_dynamic-slice_fusion.1) | copy-start | bytes 1474564
  78.9 1.2 copy-start.3
  93.7 1.8 %copy-start.8 = (f32[5,6,8,1024]{3,2,1,0:T(8,128)S(1)}, f32[5,6,8,1024]{3,2,1,0:T(8,128)}, u32[]{:S(2)}) copy-start(f32[5,6,8,1024]{3,2,1,0:T(8,128)} %param.11) | copy-start | bytes 2949124
  95.3 1.6 %copy-start.2 = (f32[5,6,9,1024]{3,2,1,0:T(8,128)S(1)}, f32[5,6,9,1024]{3,2,1,0:T(8,128)}, u32[]{:S(2)}) copy-start(f32[5,6,9,1024]{3,2,1,0:T(8,128)} %copy-done.1) | copy-start | bytes 3317764
  97.7 20.3 %copy-start.9 = (f32[5,1,8,1024]{3,2,1,0:T(8,128)S(1)}, f32[5,1,8,1024]{3,2,1,0:T(8,128)}, u32[]{:S(2)}) copy-start(f32[5,1,8,1024]{3,2,1,0:T(8,128)} %get-tuple-element.129) | copy-start | bytes 491524
  97.7 20.3 %copy-start.10 = (f32[5,1,8,1024]{3,2,1,0:T(8,128)S(1)}, f32[5,1,8,1024]{3,2,1,0:T(8,128)}, u32[]{:S(2)}) copy-start(f32[5,1,8,1024]{3,2,1,0:T(8,128)} %get-tuple-element.130) | copy-start | bytes 491524
  110.9 18.7 %collective-permute-start.4 = (f32[5,3,8,1024]{3,2,1,0:T(8,128)S(1)}, f32[5,3,8,1024]{3,2,1,0:T(8,128)S(1)}, u32[]{:S(2)}, u32[]{:S(2)}) collective-permute-start(f32[5,3,8,1024]{3,2,1,0:T(8,128)S(1)} %fusion.237), channel_id=1, source_target_pairs={{0,132},{4,136},{8,140},{12,144},{16,148},{20,152},{24,156},{28,16... | collective-permute-start | bytes 1474568 | tf_op jit(solution)/shard_map/ppermute | solution.py:248
  114.7 24.7 %collective-permute-start.5 = (f32[5,3,8,1024]{3,2,1,0:T(8,128)S(1)}, f32[5,3,8,1024]{3,2,1,0:T(8,128)}, u32[]{:S(2)}, u32[]{:S(2)}) collective-permute-start(f32[5,3,8,1024]{3,2,1,0:T(8,128)S(1)} %fusion.237), channel_id=1, source_target_pairs={{0,128},{4,132},{8,136},{12,140},{16,144},{20,148},{24,152},{28,15... | collective-permute-start | bytes 1474568 | tf_op jit(solution)/shard_map/ppermute | solution.py:248
  129.6 11.5 %copy-start.6 = (f32[5,5,8,1024]{3,2,1,0:T(8,128)S(1)}, f32[5,5,8,1024]{3,2,1,0:T(8,128)}, u32[]{:S(2)}) copy-start(f32[5,5,8,1024]{3,2,1,0:T(8,128)} %get-tuple-element.127) | copy-start | bytes 2457604
  129.6 11.5 %copy-start.7 = (f32[5,5,8,1024]{3,2,1,0:T(8,128)S(1)}, f32[5,5,8,1024]{3,2,1,0:T(8,128)}, u32[]{:S(2)}) copy-start(f32[5,5,8,1024]{3,2,1,0:T(8,128)} %get-tuple-element.128) | copy-start | bytes 2457604
  141.1 7.0 %copy-start.4 = (f32[5,4,8,1024]{3,2,1,0:T(8,128)S(1)}, f32[5,4,8,1024]{3,2,1,0:T(8,128)}, u32[]{:S(2)}) copy-start(f32[5,4,8,1024]{3,2,1,0:T(8,128)} %shard_map.37) | copy-start | bytes 1966084
Sparse Core Ops, SparseCore 0:
  19.7 54.2 all-gather.5
  78.9 30.8 all-gather.3

commit v6 on v3

--- a/solution.py
+++ b/solution.py
@@ -3,6 +3,7 @@
 from jax import lax
 from jax.sharding import PartitionSpec as P
 from jax.experimental import pallas as pl
+from jax.experimental.pallas import tpu as pltpu
 
 gamma_ratio = 1.4
 weno_epsilon = 1e-06
@@ -257,6 +258,40 @@
     )(padded)
 
 
+def mortar_kernel(flag_ref, section_ref, ghost_ref, out_ref):
+    front = flag_ref[0] == 0
+    cells = section_ref[...]
+    ghost = ghost_ref[...]
+    planes = cells.shape[1]
+    upper = [cells[:, index] for index in range(1, planes)] + [ghost[:, index] for index in range(3)]
+    lower = [ghost[:, index] for index in range(3)] + [cells[:, index] for index in range(planes - 1)]
+    padded = jnp.stack([jnp.where(front, a, b) for a, b in zip(upper, lower)], axis=1)
+    count = padded.shape[1] - 6
+    pressure = pressure_of(padded)
+    velocity = padded[1] / padded[0]
+    parts = [padded[index_part] * velocity for index_part in range(5)]
+    parts[1] = parts[1] + pressure
+    parts[4] = parts[4] + pressure * velocity
+    out_ref[...] = face_flux(padded, jnp.stack(parts), 1, count, 1, 2, 3)
+
+
+def mortar_faces_of(section_state, ghost):
+    components, planes, bands, width = section_state.shape
+    lanes = 256
+    flag = lax.axis_index("blk").astype(jnp.int32).reshape(1)
+    return pl.pallas_call(
+        mortar_kernel,
+        grid=(width // lanes,),
+        in_specs=[
+            pl.BlockSpec(memory_space=pltpu.SMEM),
+            pl.BlockSpec((components, planes, bands, lanes), lambda i: (0, 0, 0, i)),
+            pl.BlockSpec((components, 3, bands, lanes), lambda i: (0, 0, 0, i)),
+        ],
+        out_specs=pl.BlockSpec((components, 3, bands, lanes), lambda i: (0, 0, 0, i)),
+        out_shape=jax.ShapeDtypeStruct((components, 3, bands, width), section_state.dtype),
+    )(flag, section_state, ghost)
+
+
 def shards(base_state, section_state, rotor_step):
     planes = section_state.shape[1]
     bands = section_state.shape[2]
@@ -300,12 +335,7 @@
     ghost = flip_theta(
         (1.0 - fraction) * window[..., 1 : width + 1] + fraction * window[..., :width]
     )
-    mortar_window = jnp.where(
-        front,
-        jnp.concatenate([section_state[:, 1:], ghost], axis=1),
-        jnp.concatenate([ghost, section_state[:, :-1]], axis=1),
-    )
-    mortar_faces = axial_faces(mortar_window)
+    mortar_faces = mortar_faces_of(section_state, ghost)
     faces = jnp.where(
         front,
         jnp.concatenate([local_faces, mortar_faces], axis=1),

time: 158 us -> 158 us (level)
    pallas_call x0 -> x1, Pallas kernels: none -> 5.89 us  [mortar_faces_of(): pl.pallas_call(mortar_kernel, grid=(width // lanes,), in_specs=[pl.BlockS...]
    pallas_call x2 -> x1, Pallas kernels: 12.8 us -> 7.06 us  [axial_faces(): pl.pallas_call(axial_kernel, grid=(width // lanes,), in_specs=[pl.BlockSp...]
    unnamed x29 -> x25, local copies, waits for them, and re-layouts: 4.66 us -> 4.65 us
  transfers between devices with their start and end apart: 8 -> 8, of which waited for: 3 -> 3; matrix products, arithmetic and copies ran while one was open for 43% -> 42% of each run, Pallas kernels for 4% -> 4%
where the time goes in v6:
time: 158 us; the launch traced here: 157 us
  other arithmetic  58.1 us (37%)
  local copies, waits for them, and re-layouts  24.2 us (15%)
  waiting for transfers between devices  22.2 us (14%)
  between operations  21.2 us (13%)
  starting transfers between devices  18.4 us (12%)
  Pallas kernels  12.9 us (8%)
    unnamed x8, other arithmetic  43 us
    all_gather x1, waiting for transfers between devices, pick_row(): gathered = lax.all_gather(slab, 'tx')  10.3 us
    ppermute x1, waiting for transfers between devices, cross_blocks(): lax.ppermute(slab, axes, this_route)  9.75 us
    ppermute x2, starting transfers between devices, padded_2(): lax.ppermute(head, axis, [((i + 1) % count, i) for i in range(ends)])  8.8 us
    pallas_call x1, Pallas kernels, axial_faces(): pl.pallas_call(axial_kernel, grid=(width // lanes,), in_specs=[pl.BlockSp...  7.06 us
    pallas_call x1, Pallas kernels, mortar_faces_of(): pl.pallas_call(mortar_kernel, grid=(width // lanes,), in_specs=[pl.BlockS...  5.89 us
    ppermute x2, starting transfers between devices, padded_2(): lax.ppermute(tail, axis, [(i, (i + 1) % count) for i in range(ends)])  5.48 us
    slice x8, local copies, waits for them, and re-layouts, flip_radial(): return jnp.concatenate([turned[:3], -turned[3:4], turned[4:]], axis=0)  4.86 us
  transfers between devices with their start and end apart: 8, of which 3 were waited for; matrix products, arithmetic and copies ran while one was open for 42% of the time, Pallas kernels for 4%

profile of v6, /device:TPU:1, one launch (start us, length us, event | category | flops | bytes accessed | tf_op | source)
XLA Modules:
  0.0 157.0 jit_solution(7047901431764886487)
XLA Ops:
  6.5 2.6 %fusion.234 = (f32[5,6,3,1024]{3,2,1,0:T(4,128)}, f32[5,6,3,1024]{3,2,1,0:T(4,128)S(1)}) fusion(f32[5,6,8,1024]{3,2,1,0:T(8,128)} %section_ref.1), kind=kLoop, calls=%fused_computation.446 | loop fusion | bytes 1474560 | tf_op jit(solution)/shard_map/slice | solution.py:18
  9.1 4.6 %collective-permute-start = (f32[5,6,3,1024]{3,2,1,0:T(4,128)}, f32[5,6,3,1024]{3,2,1,0:T(4,128)}, u32[]{:S(2)}, u32[]{:S(2)}) collective-permute-start(f32[5,6,3,1024]{3,2,1,0:T(4,128)} %get-tuple-element.137), channel_id=1, source_target_pairs={{0,1},{1,2},{2,3},{4,5},{5,6},{6,7},{8,9},{9,10},{10,11},{12,13},{... | collective-permute-start | bytes 1105928 | tf_op jit(solution)/shard_map/ppermute | solution.py:21
  13.7 2.7 %collective-permute-start.1 = (f32[5,6,3,1024]{3,2,1,0:T(4,128)S(1)}, f32[5,6,3,1024]{3,2,1,0:T(4,128)}, u32[]{:S(2)}, u32[]{:S(2)}) collective-permute-start(f32[5,6,3,1024]{3,2,1,0:T(4,128)S(1)} %get-tuple-element.138), channel_id=1, source_target_pairs={{1,0},{2,1},{3,2},{5,4},{6,5},{7,6},{9,8},{10,9},{11,10},{13,12},{... | collective-permute-start | bytes 1105928 | tf_op jit(solution)/shard_map/ppermute | solution.py:23
  16.5 3.0 %rev.2 = f32[5,3,8,1024]{3,2,1,0:T(8,128)} reverse(f32[5,3,8,1024]{3,2,1,0:T(8,128)S(1)} %slice_select_fusion), dimensions={3} | reverse | bytes 983040 | tf_op jit(solution)/shard_map/rev | solution.py:313
  19.5 0.8 fusion.231
  20.3 0.9 collective-permute-start.2
  21.2 6.1 %collective-permute-start.3 = (f32[5,6,8,3]{3,2,1,0:T(8,128)S(1)}, f32[5,6,8,3]{3,2,1,0:T(8,128)}, u32[]{:S(2)}, u32[]{:S(2)}) collective-permute-start(f32[5,6,8,3]{3,2,1,0:T(8,128)S(1)} %get-tuple-element.129), channel_id=1, source_target_pairs={{4,0},{8,4},{12,8},{16,12},{20,16},{24,20},{28,24},{32,28},{36,32}... | collective-permute-start | bytes 8648 | tf_op jit(solution)/shard_map/ppermute | solution.py:23
  27.3 0.1 fusion.232
  27.5 0.8 fusion.230
  29.1 0.3 slice.882
  29.4 2.6 %slice.884 = f32[1,6,3,1024]{3,2,1,0:T(4,128)} reverse(f32[1,6,3,1024]{3,2,1,0:T(4,128)S(1)} %get-tuple-element.136), dimensions={2} | reverse | bytes 147456 | tf_op jit(solution)/shard_map/slice | solution.py:175
  32.0 0.5 slice.880
  32.6 0.3 slice.890
  32.9 0.3 slice.892
  33.3 0.5 slice.888
  33.9 0.7 copy-done.9
  34.6 1.5 concatenate.53
  36.1 1.2 maximum_select_fusion.2
  37.4 1.2 maximum_select_fusion.3
  38.6 0.4 pad_maximum_fusion
  39.0 0.4 fusion.2
  39.5 0.4 broadcast_multiply_fusion
  39.9 0.2 slice_add_fusion.2
  40.3 12.4 %constant_dynamic-update-slice_fusion = (f32[5,6,9,1024]{3,2,1,0:T(8,128)S(1)}, f32[1,6,9,1024]{3,2,1,0:T(8,128)S(1)}, f32[1,6,9,1024]{3,2,1,0:T(8,128)S(1)}, f3...) fusion(f32[1,6,14,1024]{3,2,1,0:T(8,128)S(1)} %get-tuple-elemen, ...), kind=kLoop, calls=%fused_computation.411 | loop fusion | flops 42190848 | bytes 22044672
  52.7 2.8 %add_dynamic-update-slice_fusion.3 = (f32[5,6,9,1024]{3,2,1,0:T(8,128)S(1)}, f32[1,6,9,1024]{3,2,1,0:T(8,128)S(1)}) fusion(f32[5,6,9,1024]{3,2,1,0:T(8,128)S(1)} %get-tuple-element.93, f32[1,6,9,1024]{3,2,1,0:T(8,128)S(1)} %get-tuple-element.110, f32[1,6,9,1024]{3,2,1,0:T(8,128)S(1)} %get-tuple-element.94, f32[1,6,9,1024]{3,2,1,0:T(8,128)S(1)} %get-tuple-element.120, ...), kind=kLoop, calls=%fused_computation.171 | loop fusion | flops 9897984 | bytes 11010048
  55.5 2.8 %add_dynamic-update-slice_fusion.2 = (f32[5,6,9,1024]{3,2,1,0:T(8,128)S(1)}, f32[1,6,9,1024]{3,2,1,0:T(8,128)S(1)}) fusion(f32[5,6,9,1024]{3,2,1,0:T(8,128)S(1)} %get-tuple-element.91, f32[1,6,9,1024]{3,2,1,0:T(8,128)S(1)} %get-tuple-element.111, f32[1,6,9,1024]{3,2,1,0:T(8,128)S(1)} %get-tuple-element.94, f32[1,6,9,1024]{3,2,1,0:T(8,128)S(1)} %get-tuple-element.120, ...), kind=kLoop, calls=%fused_computation.163 | loop fusion | flops 9897984 | bytes 11010048
  58.4 9.8 %add_dynamic-update-slice_fusion.1 = (f32[5,6,9,1024]{3,2,1,0:T(8,128)S(1)}, f32[1,6,9,1024]{3,2,1,0:T(8,128)S(1)}, f32[1,6,9,1024]{3,2,1,0:T(8,128)S(1)}, f32[1,6,9,1024]{3,2,1,0:T(8,128)S(1)}) fusion(f32[5,6,9,1024]{3,2,1,0:T(8,128)S(1)} %get-tuple-element.89, f32[1,6,9,1024]{3,2,1,0:T(8,128)S(1)} %get-tuple-element.97, ...), kind=kLoop, calls=%fused_computation.140 | loop fusion | flops 35665920 | bytes 17694720
  68.2 0.5 add_dynamic-update-slice_fusion
  68.7 0.2 slice_subtract_fusion.2
  68.9 0.2 copy.4
  69.1 0.9 copy-done.1
  70.0 0.6 slice.1168
  71.8 2.1 %all-gather.6.cloned.1.call-done = f32[40,3,8,1024]{3,2,1,0:T(8,128)} async-done(((f32[5,3,8,1024]{3,2,1,0:T(8,128)}), f32[40,3,8,1024]{3,2,1,0:T(8,128)}) %all-gather.6.cloned.1.call-update) | async-done | bytes 3932176 | tf_op jit(solution)/shard_map/all_gather | solution.py:201
  73.9 1.1 constant_dynamic-slice_fusion.1
  75.1 0.6 slice.1169
  77.1 1.6 %fusion.5 = f32[5,6,8,1025]{3,2,1,0:T(8,128)} fusion(f32[5,6,8,1030]{3,2,1,0:T(8,128)S(1)} %broadcast_select_fusion), kind=kLoop, calls=%fused_computation.69 | loop fusion | flops 492000 | bytes 2952000 | tf_op jit(solution)/shard_map/mul | solution.py:89
  79.1 1.1 copy-done.3
  80.2 6.4 %constant_dynamic-update-slice_fusion.1 = (f32[5,6,8,1025]{3,2,1,0:T(8,128)S(1)}, f32[1,6,8,1025]{3,2,1,0:T(8,128)S(1)}, f32[1,6,8,1025]{3,2,1,0:T(8,128)S(1)}, ...) fusion(f32[5,6,8,1030]{3,2,1,0:T(8,128)S(1)} %broadcast_select_, ...), kind=kLoop, calls=%fused_computation.412 | loop fusion | flops 35768400 | bytes 17215680
  86.6 1.5 add_dynamic-update-slice_fusion.7
  88.1 5.7 %add_dynamic-update-slice_fusion.6 = (f32[5,6,8,1025]{3,2,1,0:T(8,128)S(1)}, f32[1,6,8,1025]{3,2,1,0:T(8,128)S(1)}, f32[1,6,8,1025]{3,2,1,0:T(8,128)S(1)}, f32[1,6,8,1025]{3,2,1,0:T(8,128)S(1)}) fusion(f32[5,6,8,1025]{3,2,1,0:T(8,128)S(1)} %get-tuple-element.61, f32[1,6,8,1025]{3,2,1,0:T(8,128)S(1)} %get-tuple-element.67, ...), kind=kLoop, calls=%fused_computation.294 | loop fusion | flops 31734000 | bytes 9953280
  93.8 1.5 add_dynamic-update-slice_fusion.5
  95.3 0.3 add_dynamic-update-slice_fusion.4
  95.6 1.3 copy-done.2
  96.9 0.6 multiply_add_fusion
  97.5 0.2 copy.6
  97.7 0.5 slice.1246
  99.6 10.3 %all-gather.4.cloned.1.call-done = f32[4,5,3,8,1024]{4,3,2,1,0:T(8,128)} async-done(((f32[1,5,3,8,1024]{4,3,2,1,0:T(8,128)}), f32[4,5,3,8,1024]{4,3,2,1,0:T(8,128)}) %all-gather.4.cloned.1.call-update) | async-done | bytes 1966096 | tf_op jit(solution)/shard_map/all_gather | solution.py:209
  109.9 1.1 fusion.236
  110.9 3.8 %collective-permute-start.4 = (f32[5,3,8,1024]{3,2,1,0:T(8,128)S(1)}, f32[5,3,8,1024]{3,2,1,0:T(8,128)S(1)}, u32[]{:S(2)}, u32[]{:S(2)}) collective-permute-start(f32[5,3,8,1024]{3,2,1,0:T(8,128)S(1)} %fusion.236), channel_id=1, source_target_pairs={{0,132},{4,136},{8,140},{12,144},{16,148},{20,152},{24,156},{28,16... | collective-permute-start | bytes 1474568 | tf_op jit(solution)/shard_map/ppermute | solution.py:225
  114.7 0.2 collective-permute-start.5
  115.0 1.1 constant_dynamic-slice_fusion
  116.1 0.5 slice.1247
  118.0 1.4 fusion.4.padded_ref
  119.4 7.1 %shard_map.37 = f32[5,4,8,1024]{3,2,1,0:T(8,128)} custom-call(f32[5,9,8,1024]{3,2,1,0:T(8,128)} %fusion.4.padded_ref), custom_call_target="tpu_custom_call" | custom-call | tf_op jit(solution)/shard_map/pallas_call | solution.py:252
  126.4 1.2 broadcast_add_fusion
  127.6 0.1 copy.8
  127.8 0.6 slice.1249
  129.7 9.8 %collective-permute-done.5 = f32[5,3,8,1024]{3,2,1,0:T(8,128)} collective-permute-done((f32[5,3,8,1024]{3,2,1,0:T(8,128)S(1)}, f32[5,3,8,1024]{3,2,1,0:T(8,128)}, u32[]{:S(2)}, u32[]{:S(2)}) %collective-permute-start.5) | collective-permute-done | bytes 491552 | tf_op jit(solution)/shard_map/ppermute | solution.py:225
  139.5 1.3 fusion.8
  140.7 0.2 fusion.9
  141.0 0.8 pad_maximum_fusion.1.ghost_ref
  141.8 5.9 %shard_map.38 = f32[5,3,8,1024]{3,2,1,0:T(8,128)} custom-call(s32[1]{0:T(128)} %bitcast.8.flag_ref, f32[5,6,8,1024]{3,2,1,0:T(8,128)} %section_ref.1, f32[5,3,8,1024]{3,2,1,0:T(8,128)} %pad_maximum_fusion.1.ghost_ref), custom_call_target="tpu_custom_call" | custom-call | tf_op jit(solution)/shard_map/pallas_call | solution.py:282
  147.7 1.3 maximum_select_fusion.1
  149.0 1.2 fusion.7
  (41 shorter events, 1.1 us)
Async XLA Ops:
  6.5 9.9 %copy-start = (f32[5,6,8,1024]{3,2,1,0:T(8,128)S(1)}, f32[5,6,8,1024]{3,2,1,0:T(8,128)}, u32[]{:S(2)}) copy-start(f32[5,6,8,1024]{3,2,1,0:T(8,128)} %section_ref.1) | copy-start | bytes 2949124
  6.5 67.4 %all-gather.6.cloned.1.call-start = ((), (), s32[]{:S(2)}) async-start(), calls=%async_computation.1 | async-start | bytes 4423680 | tf_op jit(solution)/shard_map/all_gather | solution.py:201
  9.1 27.0 %collective-permute-start = (f32[5,6,3,1024]{3,2,1,0:T(4,128)}, f32[5,6,3,1024]{3,2,1,0:T(4,128)}, u32[]{:S(2)}, u32[]{:S(2)}) collective-permute-start(f32[5,6,3,1024]{3,2,1,0:T(4,128)} %get-tuple-element.137), channel_id=1, source_target_pairs={{0,1},{1,2},{2,3},{4,5},{5,6},{6,7},{8,9},{9,10},{10,11},{12,13},{... | collective-permute-start | bytes 1105928 | tf_op jit(solution)/shard_map/ppermute | solution.py:21
  13.7 23.6 %collective-permute-start.1 = (f32[5,6,3,1024]{3,2,1,0:T(4,128)S(1)}, f32[5,6,3,1024]{3,2,1,0:T(4,128)}, u32[]{:S(2)}, u32[]{:S(2)}) collective-permute-start(f32[5,6,3,1024]{3,2,1,0:T(4,128)S(1)} %get-tuple-element.138), channel_id=1, source_target_pairs={{1,0},{2,1},{3,2},{5,4},{6,5},{7,6},{9,8},{10,9},{11,10},{13,12},{... | collective-permute-start | bytes 1105928 | tf_op jit(solution)/shard_map/ppermute | solution.py:23
  19.5 90.4 %all-gather.4.cloned.1.call-start = ((), (), s32[]{:S(2)}) async-start(), calls=%async_computation | async-start | bytes 2457600 | tf_op jit(solution)/shard_map/all_gather | solution.py:209
  20.3 13.6 %collective-permute-start.2 = (f32[5,6,8,3]{3,2,1,0:T(8,128)}, f32[5,6,8,3]{3,2,1,0:T(8,128)S(1)}, u32[]{:S(2)}, u32[]{:S(2)}) collective-permute-start(f32[5,6,8,3]{3,2,1,0:T(8,128)} %get-tuple-element.130), channel_id=1, source_target_pairs={{0,4},{4,8},{8,12},{12,16},{16,20},{20,24},{24,28},{28,32},{32,36}... | collective-permute-start | bytes 8648 | tf_op jit(solution)/shard_map/ppermute | solution.py:21
  21.2 13.4 %collective-permute-start.3 = (f32[5,6,8,3]{3,2,1,0:T(8,128)S(1)}, f32[5,6,8,3]{3,2,1,0:T(8,128)}, u32[]{:S(2)}, u32[]{:S(2)}) collective-permute-start(f32[5,6,8,3]{3,2,1,0:T(8,128)S(1)} %get-tuple-element.129), channel_id=1, source_target_pairs={{4,0},{8,4},{12,8},{16,12},{20,16},{24,20},{28,24},{32,28},{36,32}... | collective-permute-start | bytes 8648 | tf_op jit(solution)/shard_map/ppermute | solution.py:23
  33.9 0.7 copy-start.9
  68.7 1.3 copy-start.1
  75.0 2.0 %copy-start.5 = (f32[1,5,3,8,1024]{4,3,2,1,0:T(8,128)}, f32[1,5,3,8,1024]{4,3,2,1,0:T(8,128)S(1)}, u32[]{:S(2)}) copy-start(f32[1,5,3,8,1024]{4,3,2,1,0:T(8,128)S(1)} %constant_dynamic-slice_fusion.1) | copy-start | bytes 1474564
  78.9 1.2 copy-start.3
  93.8 1.8 %copy-start.6 = (f32[5,6,8,1024]{3,2,1,0:T(8,128)S(1)}, f32[5,6,8,1024]{3,2,1,0:T(8,128)}, u32[]{:S(2)}) copy-start(f32[5,6,8,1024]{3,2,1,0:T(8,128)} %param.11) | copy-start | bytes 2949124
  95.3 1.6 %copy-start.2 = (f32[5,6,9,1024]{3,2,1,0:T(8,128)S(1)}, f32[5,6,9,1024]{3,2,1,0:T(8,128)}, u32[]{:S(2)}) copy-start(f32[5,6,9,1024]{3,2,1,0:T(8,128)} %copy-done.1) | copy-start | bytes 3317764
  97.7 20.2 %copy-start.7 = (f32[5,1,8,1024]{3,2,1,0:T(8,128)S(1)}, f32[5,1,8,1024]{3,2,1,0:T(8,128)}, u32[]{:S(2)}) copy-start(f32[5,1,8,1024]{3,2,1,0:T(8,128)} %get-tuple-element.127) | copy-start | bytes 491524
  97.7 20.2 %copy-start.8 = (f32[5,1,8,1024]{3,2,1,0:T(8,128)S(1)}, f32[5,1,8,1024]{3,2,1,0:T(8,128)}, u32[]{:S(2)}) copy-start(f32[5,1,8,1024]{3,2,1,0:T(8,128)} %get-tuple-element.128) | copy-start | bytes 491524
  110.9 18.8 %collective-permute-start.4 = (f32[5,3,8,1024]{3,2,1,0:T(8,128)S(1)}, f32[5,3,8,1024]{3,2,1,0:T(8,128)S(1)}, u32[]{:S(2)}, u32[]{:S(2)}) collective-permute-start(f32[5,3,8,1024]{3,2,1,0:T(8,128)S(1)} %fusion.236), channel_id=1, source_target_pairs={{0,132},{4,136},{8,140},{12,144},{16,148},{20,152},{24,156},{28,16... | collective-permute-start | bytes 1474568 | tf_op jit(solution)/shard_map/ppermute | solution.py:225
  114.7 24.7 %collective-permute-start.5 = (f32[5,3,8,1024]{3,2,1,0:T(8,128)S(1)}, f32[5,3,8,1024]{3,2,1,0:T(8,128)}, u32[]{:S(2)}, u32[]{:S(2)}) collective-permute-start(f32[5,3,8,1024]{3,2,1,0:T(8,128)S(1)} %fusion.236), channel_id=1, source_target_pairs={{0,128},{4,132},{8,136},{12,140},{16,144},{20,148},{24,152},{28,15... | collective-permute-start | bytes 1474568 | tf_op jit(solution)/shard_map/ppermute | solution.py:225
  140.9 6.8 %copy-start.4 = (f32[5,4,8,1024]{3,2,1,0:T(8,128)S(1)}, f32[5,4,8,1024]{3,2,1,0:T(8,128)}, u32[]{:S(2)}) copy-start(f32[5,4,8,1024]{3,2,1,0:T(8,128)} %shard_map.37) | copy-start | bytes 1966084
Sparse Core Ops, SparseCore 0:
  19.6 54.2 all-gather.5
  78.9 30.8 all-gather.3

commit v7 on v6

--- a/solution.py
+++ b/solution.py
@@ -258,7 +258,7 @@
     )(padded)
 
 
-def mortar_kernel(flag_ref, section_ref, ghost_ref, out_ref):
+def mortar_kernel(flag_ref, section_ref, ghost_ref, edge_ref, partial_ref, out_ref):
     front = flag_ref[0] == 0
     cells = section_ref[...]
     ghost = ghost_ref[...]
@@ -272,24 +272,35 @@
     parts = [padded[index_part] * velocity for index_part in range(5)]
     parts[1] = parts[1] + pressure
     parts[4] = parts[4] + pressure * velocity
-    out_ref[...] = face_flux(padded, jnp.stack(parts), 1, count, 1, 2, 3)
-
-
-def mortar_faces_of(section_state, ghost):
+    faces = face_flux(padded, jnp.stack(parts), 1, count, 1, 2, 3)
+    edge = edge_ref[...][:, 0]
+    after_front = [faces[:, 0] - edge, faces[:, 1] - faces[:, 0], faces[:, 2] - faces[:, 1]]
+    after_aft = [faces[:, 1] - faces[:, 0], faces[:, 2] - faces[:, 1], edge - faces[:, 2]]
+    axial = jnp.stack([jnp.where(front, a, b) for a, b in zip(after_front, after_aft)], axis=1)
+    out_ref[...] = partial_ref[...] - 0.25 * step_ratio * axial
+
+
+def mortar_planes_of(section_state, ghost, edge, partial):
     components, planes, bands, width = section_state.shape
     lanes = 256
     flag = lax.axis_index("blk").astype(jnp.int32).reshape(1)
+    late = lambda i, flag_ref: (0, 1 - flag_ref[0], 0, i)
     return pl.pallas_call(
         mortar_kernel,
-        grid=(width // lanes,),
-        in_specs=[
-            pl.BlockSpec(memory_space=pltpu.SMEM),
-            pl.BlockSpec((components, planes, bands, lanes), lambda i: (0, 0, 0, i)),
-            pl.BlockSpec((components, 3, bands, lanes), lambda i: (0, 0, 0, i)),
-        ],
-        out_specs=pl.BlockSpec((components, 3, bands, lanes), lambda i: (0, 0, 0, i)),
-        out_shape=jax.ShapeDtypeStruct((components, 3, bands, width), section_state.dtype),
-    )(flag, section_state, ghost)
+        grid_spec=pltpu.PrefetchScalarGridSpec(
+            num_scalar_prefetch=1,
+            grid=(width // lanes,),
+            in_specs=[
+                pl.BlockSpec((components, planes, bands, lanes), lambda i, flag_ref: (0, 0, 0, i)),
+                pl.BlockSpec((components, 3, bands, lanes), lambda i, flag_ref: (0, 0, 0, i)),
+                pl.BlockSpec((components, 1, bands, lanes), lambda i, flag_ref: (0, 0, 0, i)),
+                pl.BlockSpec((components, 3, bands, lanes), late),
+            ],
+            out_specs=pl.BlockSpec((components, 3, bands, lanes), late),
+        ),
+        out_shape=jax.ShapeDtypeStruct(partial.shape, partial.dtype),
+        input_output_aliases={4: 0},
+    )(flag, section_state, ghost, edge, partial)
 
 
 def shards(base_state, section_state, rotor_step):
@@ -331,20 +342,21 @@
     local_window = hold(local_window, chosen)
     local_faces = axial_faces(local_window)
     settled = 0.75 * base_state + 0.25 * (section_state - step_ratio * (radial + azimuthal))
-    window = window_of(this_slab, next_slab, rotor_step, local_faces + settled[:, :1, :, :1])
+    half = planes // 2
+    early = jnp.where(front, settled[:, :half], settled[:, half:]) - 0.25 * step_ratio * (
+        local_faces[:, 1:] - local_faces[:, :-1]
+    )
+    partial = jnp.where(
+        front,
+        jnp.concatenate([early, settled[:, half:]], axis=1),
+        jnp.concatenate([settled[:, :half], early], axis=1),
+    )
+    edge = jnp.where(front, local_faces[:, -1:], local_faces[:, :1])
+    window = window_of(this_slab, next_slab, rotor_step, partial[:, :1, :, :1] + edge[:, :, :1, :1])
     ghost = flip_theta(
         (1.0 - fraction) * window[..., 1 : width + 1] + fraction * window[..., :width]
     )
-    mortar_faces = mortar_faces_of(section_state, ghost)
-    faces = jnp.where(
-        front,
-        jnp.concatenate([local_faces, mortar_faces], axis=1),
-        jnp.concatenate([mortar_faces, local_faces], axis=1),
-    )
-    axial = lax.slice_in_dim(faces, 1, planes + 1, axis=1) - lax.slice_in_dim(
-        faces, 0, planes, axis=1
-    )
-    return settled - 0.25 * step_ratio * axial
+    return mortar_planes_of(section_state, ghost, edge, partial)
 
 
 def solution(mesh):

time: 158 us -> 155 us (0.981)
  local copies, waits for them, and re-layouts: 24.2 us -> 22.3 us
    unnamed x25 -> x24, local copies, waits for them, and re-layouts: 4.65 us -> 3.89 us
  transfers between devices with their start and end apart: 8 -> 8, of which waited for: 3 -> 3; matrix products, arithmetic and copies ran while one was open for 42% -> 43% of each run, Pallas kernels for 4% -> 5%
where the time goes in v7:
time: 155 us
  other arithmetic  57.1 us (37%)
  waiting for transfers between devices  23.5 us (15%)
  local copies, waits for them, and re-layouts  22.3 us (14%)
  between operations  19.9 us (13%)
  starting transfers between devices  18.5 us (12%)
  Pallas kernels  13.3 us (9%)
    unnamed x8, other arithmetic  43 us
    all_gather x1, waiting for transfers between devices, pick_row(): gathered = lax.all_gather(slab, 'tx')  10.3 us
    ppermute x1, waiting for transfers between devices, cross_blocks(): lax.ppermute(slab, axes, this_route)  10.1 us
    ppermute x2, starting transfers between devices, padded_2(): lax.ppermute(head, axis, [((i + 1) % count, i) for i in range(ends)])  8.89 us
    pallas_call x1, Pallas kernels, axial_faces(): pl.pallas_call(axial_kernel, grid=(width // lanes,), in_specs=[pl.BlockSp...  7.06 us
    pallas_call x1, Pallas kernels, mortar_planes_of(): pl.pallas_call(mortar_kernel, grid_spec=pltpu.PrefetchScalarGridSpec(num_...  6.29 us
    ppermute x2, starting transfers between devices, padded_2(): lax.ppermute(tail, axis, [(i, (i + 1) % count) for i in range(ends)])  5.55 us
    slice x8, local copies, waits for them, and re-layouts, flip_radial(): return jnp.concatenate([turned[:3], -turned[3:4], turned[4:]], axis=0)  4.88 us
  transfers between devices with their start and end apart: 8, of which 3 were waited for; matrix products, arithmetic and copies ran while one was open for 43% of the time, Pallas kernels for 5%

profile of v7, /device:TPU:1, one launch (start us, length us, event | category | flops | bytes accessed | tf_op | source)
XLA Modules:
  0.0 154.7 jit_solution(8344523148444406940)
XLA Ops:
  6.5 2.6 %fusion.236 = (f32[5,6,3,1024]{3,2,1,0:T(4,128)}, f32[5,6,3,1024]{3,2,1,0:T(4,128)S(1)}) fusion(f32[5,6,8,1024]{3,2,1,0:T(8,128)} %section_ref.1), kind=kLoop, calls=%fused_computation.449 | loop fusion | bytes 1474560 | tf_op jit(solution)/shard_map/slice | solution.py:18
  9.1 4.6 %collective-permute-start = (f32[5,6,3,1024]{3,2,1,0:T(4,128)}, f32[5,6,3,1024]{3,2,1,0:T(4,128)}, u32[]{:S(2)}, u32[]{:S(2)}) collective-permute-start(f32[5,6,3,1024]{3,2,1,0:T(4,128)} %get-tuple-element.140), channel_id=1, source_target_pairs={{0,1},{1,2},{2,3},{4,5},{5,6},{6,7},{8,9},{9,10},{10,11},{12,13},{... | collective-permute-start | bytes 1105928 | tf_op jit(solution)/shard_map/ppermute | solution.py:21
  13.7 2.7 %collective-permute-start.1 = (f32[5,6,3,1024]{3,2,1,0:T(4,128)S(1)}, f32[5,6,3,1024]{3,2,1,0:T(4,128)}, u32[]{:S(2)}, u32[]{:S(2)}) collective-permute-start(f32[5,6,3,1024]{3,2,1,0:T(4,128)S(1)} %get-tuple-element.141), channel_id=1, source_target_pairs={{1,0},{2,1},{3,2},{5,4},{6,5},{7,6},{9,8},{10,9},{11,10},{13,12},{... | collective-permute-start | bytes 1105928 | tf_op jit(solution)/shard_map/ppermute | solution.py:23
  16.5 3.0 %rev.2 = f32[5,3,8,1024]{3,2,1,0:T(8,128)} reverse(f32[5,3,8,1024]{3,2,1,0:T(8,128)S(1)} %slice_select_fusion), dimensions={3} | reverse | bytes 983040 | tf_op jit(solution)/shard_map/rev | solution.py:324
  19.5 0.1 fusion.233
  19.6 1.0 collective-permute-start.2
  20.6 6.2 %collective-permute-start.3 = (f32[5,6,8,3]{3,2,1,0:T(8,128)S(1)}, f32[5,6,8,3]{3,2,1,0:T(8,128)}, u32[]{:S(2)}, u32[]{:S(2)}) collective-permute-start(f32[5,6,8,3]{3,2,1,0:T(8,128)S(1)} %get-tuple-element.132), channel_id=1, source_target_pairs={{4,0},{8,4},{12,8},{16,12},{20,16},{24,20},{28,24},{32,28},{36,32}... | collective-permute-start | bytes 8648 | tf_op jit(solution)/shard_map/ppermute | solution.py:23
  26.8 0.1 fusion.234
  27.0 0.8 fusion.232
  28.6 0.3 slice.901
  28.9 2.6 %slice.903 = f32[1,6,3,1024]{3,2,1,0:T(4,128)} reverse(f32[1,6,3,1024]{3,2,1,0:T(4,128)S(1)} %get-tuple-element.139), dimensions={2} | reverse | bytes 147456 | tf_op jit(solution)/shard_map/slice | solution.py:175
  31.5 0.5 slice.899
  32.1 0.3 slice.909
  32.4 0.3 slice.911
  32.8 0.5 slice.907
  33.4 1.5 concatenate.53
  35.0 1.2 maximum_select_fusion.2
  36.2 1.2 maximum_select_fusion.3
  37.4 0.4 pad_maximum_fusion
  37.8 0.4 fusion.2
  38.3 0.4 broadcast_multiply_fusion
  38.8 0.2 slice_add_fusion.2
  39.0 0.1 slice_add_fusion.1
  39.1 12.4 %constant_dynamic-update-slice_fusion = (f32[5,6,9,1024]{3,2,1,0:T(8,128)S(1)}, f32[1,6,9,1024]{3,2,1,0:T(8,128)S(1)}, f32[1,6,9,1024]{3,2,1,0:T(8,128)S(1)}, f3...) fusion(f32[1,6,14,1024]{3,2,1,0:T(8,128)S(1)} %get-tuple-elemen, ...), kind=kLoop, calls=%fused_computation.411 | loop fusion | flops 42190848 | bytes 22044672
  51.5 2.8 %add_dynamic-update-slice_fusion.3 = (f32[5,6,9,1024]{3,2,1,0:T(8,128)S(1)}, f32[1,6,9,1024]{3,2,1,0:T(8,128)S(1)}) fusion(f32[5,6,9,1024]{3,2,1,0:T(8,128)S(1)} %get-tuple-element.93, f32[1,6,9,1024]{3,2,1,0:T(8,128)S(1)} %get-tuple-element.110, f32[1,6,9,1024]{3,2,1,0:T(8,128)S(1)} %get-tuple-element.94, f32[1,6,9,1024]{3,2,1,0:T(8,128)S(1)} %get-tuple-element.120, ...), kind=kLoop, calls=%fused_computation.171 | loop fusion | flops 9897984 | bytes 11010048
  54.4 2.8 %add_dynamic-update-slice_fusion.2 = (f32[5,6,9,1024]{3,2,1,0:T(8,128)S(1)}, f32[1,6,9,1024]{3,2,1,0:T(8,128)S(1)}) fusion(f32[5,6,9,1024]{3,2,1,0:T(8,128)S(1)} %get-tuple-element.91, f32[1,6,9,1024]{3,2,1,0:T(8,128)S(1)} %get-tuple-element.111, f32[1,6,9,1024]{3,2,1,0:T(8,128)S(1)} %get-tuple-element.94, f32[1,6,9,1024]{3,2,1,0:T(8,128)S(1)} %get-tuple-element.120, ...), kind=kLoop, calls=%fused_computation.163 | loop fusion | flops 9897984 | bytes 11010048
  57.2 9.8 %add_dynamic-update-slice_fusion.1 = (f32[5,6,9,1024]{3,2,1,0:T(8,128)S(1)}, f32[1,6,9,1024]{3,2,1,0:T(8,128)S(1)}, f32[1,6,9,1024]{3,2,1,0:T(8,128)S(1)}, f32[1,6,9,1024]{3,2,1,0:T(8,128)S(1)}) fusion(f32[5,6,9,1024]{3,2,1,0:T(8,128)S(1)} %get-tuple-element.89, f32[1,6,9,1024]{3,2,1,0:T(8,128)S(1)} %get-tuple-element.97, ...), kind=kLoop, calls=%fused_computation.140 | loop fusion | flops 35665920 | bytes 17694720
  67.0 0.5 add_dynamic-update-slice_fusion
  67.6 0.2 slice_subtract_fusion.1
  67.7 0.2 copy.5
  67.9 0.9 copy-done.1
  68.8 0.6 slice.1190
  70.8 3.1 %all-gather.6.cloned.1.call-done = f32[40,3,8,1024]{3,2,1,0:T(8,128)} async-done(((f32[5,3,8,1024]{3,2,1,0:T(8,128)}), f32[40,3,8,1024]{3,2,1,0:T(8,128)}) %all-gather.6.cloned.1.call-update) | async-done | bytes 3932176 | tf_op jit(solution)/shard_map/all_gather | solution.py:201
  73.9 1.1 constant_dynamic-slice_fusion.1
  75.1 0.6 slice.1191
  76.9 1.6 %fusion.5 = f32[5,6,8,1025]{3,2,1,0:T(8,128)} fusion(f32[5,6,8,1030]{3,2,1,0:T(8,128)S(1)} %broadcast_select_fusion), kind=kLoop, calls=%fused_computation.68 | loop fusion | flops 492000 | bytes 2952000 | tf_op jit(solution)/shard_map/mul | solution.py:89
  78.8 1.1 copy-done.3
  79.9 6.4 %constant_dynamic-update-slice_fusion.1 = (f32[5,6,8,1025]{3,2,1,0:T(8,128)S(1)}, f32[1,6,8,1025]{3,2,1,0:T(8,128)S(1)}, f32[1,6,8,1025]{3,2,1,0:T(8,128)S(1)}, ...) fusion(f32[5,6,8,1030]{3,2,1,0:T(8,128)S(1)} %broadcast_select_, ...), kind=kLoop, calls=%fused_computation.412 | loop fusion | flops 35768400 | bytes 17215680
  86.3 1.5 add_dynamic-update-slice_fusion.7
  87.9 5.7 %add_dynamic-update-slice_fusion.6 = (f32[5,6,8,1025]{3,2,1,0:T(8,128)S(1)}, f32[1,6,8,1025]{3,2,1,0:T(8,128)S(1)}, f32[1,6,8,1025]{3,2,1,0:T(8,128)S(1)}, f32[1,6,8,1025]{3,2,1,0:T(8,128)S(1)}) fusion(f32[5,6,8,1025]{3,2,1,0:T(8,128)S(1)} %get-tuple-element.61, f32[1,6,8,1025]{3,2,1,0:T(8,128)S(1)} %get-tuple-element.67, ...), kind=kLoop, calls=%fused_computation.293 | loop fusion | flops 31734000 | bytes 9953280
  93.5 1.5 add_dynamic-update-slice_fusion.5
  95.1 0.3 add_dynamic-update-slice_fusion.4
  95.4 1.3 copy-done.2
  96.7 0.6 multiply_add_fusion
  97.3 0.2 copy.7
  97.5 0.5 slice.1268
  99.3 10.3 %all-gather.4.cloned.1.call-done = f32[4,5,3,8,1024]{4,3,2,1,0:T(8,128)} async-done(((f32[1,5,3,8,1024]{4,3,2,1,0:T(8,128)}), f32[4,5,3,8,1024]{4,3,2,1,0:T(8,128)}) %all-gather.4.cloned.1.call-update) | async-done | bytes 1966096 | tf_op jit(solution)/shard_map/all_gather | solution.py:209
  109.6 1.1 fusion.238
  110.7 3.8 %collective-permute-start.4 = (f32[5,3,8,1024]{3,2,1,0:T(8,128)S(1)}, f32[5,3,8,1024]{3,2,1,0:T(8,128)S(1)}, u32[]{:S(2)}, u32[]{:S(2)}) collective-permute-start(f32[5,3,8,1024]{3,2,1,0:T(8,128)S(1)} %fusion.238), channel_id=1, source_target_pairs={{0,132},{4,136},{8,140},{12,144},{16,148},{20,152},{24,156},{28,16... | collective-permute-start | bytes 1474568 | tf_op jit(solution)/shard_map/ppermute | solution.py:225
  114.5 0.2 collective-permute-start.5
  114.7 1.1 constant_dynamic-slice_fusion
  115.9 0.5 slice.1271
  117.7 1.4 fusion.4.padded_ref
  119.1 7.1 %shard_map.37 = f32[5,4,8,1024]{3,2,1,0:T(8,128)} custom-call(f32[5,9,8,1024]{3,2,1,0:T(8,128)} %fusion.4.padded_ref), custom_call_target="tpu_custom_call" | custom-call | tf_op jit(solution)/shard_map/pallas_call | solution.py:252
  126.1 1.0 slice_select_fusion.1.edge_ref
  127.2 0.1 slice_reduce_fusion
  127.3 1.3 fusion.231
  128.6 0.1 maximum_select_fusion.1.partial_ref
  128.8 0.2 fusion.186
  129.1 10.1 %collective-permute-done.5 = f32[5,3,8,1024]{3,2,1,0:T(8,128)} collective-permute-done((f32[5,3,8,1024]{3,2,1,0:T(8,128)S(1)}, f32[5,3,8,1024]{3,2,1,0:T(8,128)}, u32[]{:S(2)}, u32[]{:S(2)}) %collective-permute-start.5) | collective-permute-done | bytes 491552 | tf_op jit(solution)/shard_map/ppermute | solution.py:225
  139.2 1.3 fusion.6
  140.5 0.2 fusion.7
  140.8 0.8 pad_maximum_fusion.1.ghost_ref
  141.6 6.3 %shard_map.38 = f32[5,6,8,1024]{3,2,1,0:T(8,128)} custom-call(s32[1]{0:T(128)} %bitcast.flag_ref, f32[5,6,8,1024]{3,2,1,0:T(8,128)} %section_ref.1, f32[5,3,8,1024]{3,2,1,0:T(8,128)} %pad_maximum_fusion.1.ghost_ref, f32[5,1,8,1024]{3,2,1,0:T(8,128)} %copy-done.7, f32[5,6,8,1024]{3,2,1,0:T(8,128)} %copy-done.5), custom_call_target="tpu_custom_call", output_to_operand_aliasing={{}: (4, {})} | custom-call | tf_op jit(solution)/shard_map/pallas_call | solution.py:288
  (41 shorter events, 1.0 us)
Async XLA Ops:
  6.5 9.9 %copy-start = (f32[5,6,8,1024]{3,2,1,0:T(8,128)S(1)}, f32[5,6,8,1024]{3,2,1,0:T(8,128)}, u32[]{:S(2)}) copy-start(f32[5,6,8,1024]{3,2,1,0:T(8,128)} %section_ref.1) | copy-start | bytes 2949124
  6.5 67.4 %all-gather.6.cloned.1.call-start = ((), (), s32[]{:S(2)}) async-start(), calls=%async_computation.1 | async-start | bytes 4423680 | tf_op jit(solution)/shard_map/all_gather | solution.py:201
  9.1 25.8 %collective-permute-start = (f32[5,6,3,1024]{3,2,1,0:T(4,128)}, f32[5,6,3,1024]{3,2,1,0:T(4,128)}, u32[]{:S(2)}, u32[]{:S(2)}) collective-permute-start(f32[5,6,3,1024]{3,2,1,0:T(4,128)} %get-tuple-element.140), channel_id=1, source_target_pairs={{0,1},{1,2},{2,3},{4,5},{5,6},{6,7},{8,9},{9,10},{10,11},{12,13},{... | collective-permute-start | bytes 1105928 | tf_op jit(solution)/shard_map/ppermute | solution.py:21
  13.7 22.5 %collective-permute-start.1 = (f32[5,6,3,1024]{3,2,1,0:T(4,128)S(1)}, f32[5,6,3,1024]{3,2,1,0:T(4,128)}, u32[]{:S(2)}, u32[]{:S(2)}) collective-permute-start(f32[5,6,3,1024]{3,2,1,0:T(4,128)S(1)} %get-tuple-element.141), channel_id=1, source_target_pairs={{1,0},{2,1},{3,2},{5,4},{6,5},{7,6},{9,8},{10,9},{11,10},{13,12},{... | collective-permute-start | bytes 1105928 | tf_op jit(solution)/shard_map/ppermute | solution.py:23
  19.5 90.2 %all-gather.4.cloned.1.call-start = ((), (), s32[]{:S(2)}) async-start(), calls=%async_computation | async-start | bytes 2457600 | tf_op jit(solution)/shard_map/all_gather | solution.py:209
  19.6 13.8 %collective-permute-start.2 = (f32[5,6,8,3]{3,2,1,0:T(8,128)S(1)}, f32[5,6,8,3]{3,2,1,0:T(8,128)}, u32[]{:S(2)}, u32[]{:S(2)}) collective-permute-start(f32[5,6,8,3]{3,2,1,0:T(8,128)S(1)} %get-tuple-element.133), channel_id=1, source_target_pairs={{0,4},{4,8},{8,12},{12,16},{16,20},{20,24},{24,28},{28,32},{32,36}... | collective-permute-start | bytes 8648 | tf_op jit(solution)/shard_map/ppermute | solution.py:21
  20.6 12.8 %collective-permute-start.3 = (f32[5,6,8,3]{3,2,1,0:T(8,128)S(1)}, f32[5,6,8,3]{3,2,1,0:T(8,128)}, u32[]{:S(2)}, u32[]{:S(2)}) collective-permute-start(f32[5,6,8,3]{3,2,1,0:T(8,128)S(1)} %get-tuple-element.132), channel_id=1, source_target_pairs={{4,0},{8,4},{12,8},{16,12},{20,16},{24,20},{28,24},{32,28},{36,32}... | collective-permute-start | bytes 8648 | tf_op jit(solution)/shard_map/ppermute | solution.py:23
  67.5 1.3 copy-start.1
  75.0 1.8 %copy-start.4 = (f32[1,5,3,8,1024]{4,3,2,1,0:T(8,128)}, f32[1,5,3,8,1024]{4,3,2,1,0:T(8,128)S(1)}, u32[]{:S(2)}) copy-start(f32[1,5,3,8,1024]{4,3,2,1,0:T(8,128)S(1)} %constant_dynamic-slice_fusion.1) | copy-start | bytes 1474564
  78.7 1.2 copy-start.3
  93.5 1.8 %copy-start.6 = (f32[5,6,8,1024]{3,2,1,0:T(8,128)S(1)}, f32[5,6,8,1024]{3,2,1,0:T(8,128)}, u32[]{:S(2)}) copy-start(f32[5,6,8,1024]{3,2,1,0:T(8,128)} %param.11) | copy-start | bytes 2949124
  95.1 1.6 %copy-start.2 = (f32[5,6,9,1024]{3,2,1,0:T(8,128)S(1)}, f32[5,6,9,1024]{3,2,1,0:T(8,128)}, u32[]{:S(2)}) copy-start(f32[5,6,9,1024]{3,2,1,0:T(8,128)} %copy-done.1) | copy-start | bytes 3317764
  97.5 20.2 %copy-start.8 = (f32[5,1,8,1024]{3,2,1,0:T(8,128)S(1)}, f32[5,1,8,1024]{3,2,1,0:T(8,128)}, u32[]{:S(2)}) copy-start(f32[5,1,8,1024]{3,2,1,0:T(8,128)} %get-tuple-element.130) | copy-start | bytes 491524
  97.5 20.2 %copy-start.9 = (f32[5,1,8,1024]{3,2,1,0:T(8,128)S(1)}, f32[5,1,8,1024]{3,2,1,0:T(8,128)}, u32[]{:S(2)}) copy-start(f32[5,1,8,1024]{3,2,1,0:T(8,128)} %get-tuple-element.131) | copy-start | bytes 491524
  110.7 18.4 %collective-permute-start.4 = (f32[5,3,8,1024]{3,2,1,0:T(8,128)S(1)}, f32[5,3,8,1024]{3,2,1,0:T(8,128)S(1)}, u32[]{:S(2)}, u32[]{:S(2)}) collective-permute-start(f32[5,3,8,1024]{3,2,1,0:T(8,128)S(1)} %fusion.238), channel_id=1, source_target_pairs={{0,132},{4,136},{8,140},{12,144},{16,148},{20,152},{24,156},{28,16... | collective-permute-start | bytes 1474568 | tf_op jit(solution)/shard_map/ppermute | solution.py:225
  114.5 24.7 %collective-permute-start.5 = (f32[5,3,8,1024]{3,2,1,0:T(8,128)S(1)}, f32[5,3,8,1024]{3,2,1,0:T(8,128)}, u32[]{:S(2)}, u32[]{:S(2)}) collective-permute-start(f32[5,3,8,1024]{3,2,1,0:T(8,128)S(1)} %fusion.238), channel_id=1, source_target_pairs={{0,128},{4,132},{8,136},{12,140},{16,144},{20,148},{24,152},{28,15... | collective-permute-start | bytes 1474568 | tf_op jit(solution)/shard_map/ppermute | solution.py:225
  127.2 1.6 %copy-start.7 = (f32[5,1,8,1024]{3,2,1,0:T(8,128)}, f32[5,1,8,1024]{3,2,1,0:T(8,128)S(1)}, u32[]{:S(2)}) copy-start(f32[5,1,8,1024]{3,2,1,0:T(8,128)S(1)} %slice_select_fusion.1.edge_ref) | copy-start | bytes 491524
  128.8 12.0 %copy-start.5 = (f32[5,6,8,1024]{3,2,1,0:T(8,128)}, f32[5,6,8,1024]{3,2,1,0:T(8,128)S(1)}, u32[]{:S(2)}) copy-start(f32[5,6,8,1024]{3,2,1,0:T(8,128)S(1)} %maximum_select_fusion.1.partial_ref) | copy-start | bytes 2949124
Sparse Core Ops, SparseCore 0:
  19.6 54.2 all-gather.5
  78.7 30.8 all-gather.3

commit v8 on v7

--- a/solution.py
+++ b/solution.py
@@ -199,7 +199,9 @@
     rows, columns, centre_row, centre_column = route_parts(rotor_step, slab.shape[3])
     source_column = (centre_column - lax.axis_index("tz")) % columns
     gathered = lax.all_gather(slab, "tz")
-    return lax.dynamic_index_in_dim(gathered, after(before, source_column), 0, keepdims=False)
+    return lax.dynamic_index_in_dim(gathered, after(before, source_column), 0, keepdims=False)[
+        ..., ::-1
+    ]
 
 
 def pick_row(slab, rotor_step, before):
@@ -321,7 +323,7 @@
     radial_padded = jnp.concatenate([lower_wall, section_state, upper_wall], axis=2)
     block_index = lax.axis_index("blk")
     front = block_index == 0
-    outgoing = jnp.where(front, section_state[:, -3:], section_state[:, :3])[..., ::-1]
+    outgoing = jnp.where(front, section_state[:, -3:], section_state[:, :3])
     radial = divergence(radial_padded, 2, bands, 3, 1, 2)
     chosen = pick_column(outgoing, rotor_step, radial)
     theta_padded = hold(theta_padded, chosen)

time: 155 us -> 154 us (level)
  local copies, waits for them, and re-layouts: 22.3 us -> 20.1 us
    rev x1, local copies, waits for them, and re-layouts: 2.98 us -> 0.75 us  [pick_column(): lax.dynamic_index_in_dim(gathered, after(before, source_column), 0, keepd...]
  transfers between devices with their start and end apart: 8 -> 8, of which waited for: 3 -> 3; matrix products, arithmetic and copies ran while one was open for 43% -> 42% of each run, Pallas kernels for 5% -> 5%
where the time goes in v8:
time: 154 us; the launch traced here: 153 us
  other arithmetic  57.9 us (38%)
  waiting for transfers between devices  23.5 us (15%)
  local copies, waits for them, and re-layouts  20.1 us (13%)
  between operations  19.9 us (13%)
  starting transfers between devices  18.5 us (12%)
  Pallas kernels  13.3 us (9%)
    unnamed x8, other arithmetic  43 us
    all_gather x1, waiting for transfers between devices, pick_row(): gathered = lax.all_gather(slab, 'tx')  10.3 us
    ppermute x1, waiting for transfers between devices, cross_blocks(): lax.ppermute(slab, axes, this_route)  10.1 us
    ppermute x2, starting transfers between devices, padded_2(): lax.ppermute(head, axis, [((i + 1) % count, i) for i in range(ends)])  8.89 us
    pallas_call x1, Pallas kernels, axial_faces(): pl.pallas_call(axial_kernel, grid=(width // lanes,), in_specs=[pl.BlockSp...  7.06 us
    pallas_call x1, Pallas kernels, mortar_planes_of(): pl.pallas_call(mortar_kernel, grid_spec=pltpu.PrefetchScalarGridSpec(num_...  6.29 us
    ppermute x2, starting transfers between devices, padded_2(): lax.ppermute(tail, axis, [(i, (i + 1) % count) for i in range(ends)])  5.55 us
    slice x8, local copies, waits for them, and re-layouts, flip_radial(): return jnp.concatenate([turned[:3], -turned[3:4], turned[4:]], axis=0)  4.88 us
  transfers between devices with their start and end apart: 8, of which 3 were waited for; matrix products, arithmetic and copies ran while one was open for 42% of the time, Pallas kernels for 5%

profile of v8, /device:TPU:1, one launch (start us, length us, event | category | flops | bytes accessed | tf_op | source)
XLA Modules:
  0.0 153.3 jit_solution(6086079882374188255)
XLA Ops:
  6.5 2.6 %fusion.236 = (f32[5,6,3,1024]{3,2,1,0:T(4,128)}, f32[5,6,3,1024]{3,2,1,0:T(4,128)S(1)}) fusion(f32[5,6,8,1024]{3,2,1,0:T(8,128)} %section_ref.1), kind=kLoop, calls=%fused_computation.449 | loop fusion | bytes 1474560 | tf_op jit(solution)/shard_map/slice | solution.py:18
  9.1 4.6 %collective-permute-start = (f32[5,6,3,1024]{3,2,1,0:T(4,128)}, f32[5,6,3,1024]{3,2,1,0:T(4,128)}, u32[]{:S(2)}, u32[]{:S(2)}) collective-permute-start(f32[5,6,3,1024]{3,2,1,0:T(4,128)} %get-tuple-element.140), channel_id=1, source_target_pairs={{0,1},{1,2},{2,3},{4,5},{5,6},{6,7},{8,9},{9,10},{10,11},{12,13},{... | collective-permute-start | bytes 1105928 | tf_op jit(solution)/shard_map/ppermute | solution.py:21
  13.7 2.7 %collective-permute-start.1 = (f32[5,6,3,1024]{3,2,1,0:T(4,128)S(1)}, f32[5,6,3,1024]{3,2,1,0:T(4,128)}, u32[]{:S(2)}, u32[]{:S(2)}) collective-permute-start(f32[5,6,3,1024]{3,2,1,0:T(4,128)S(1)} %get-tuple-element.141), channel_id=1, source_target_pairs={{1,0},{2,1},{3,2},{5,4},{6,5},{7,6},{9,8},{10,9},{11,10},{13,12},{... | collective-permute-start | bytes 1105928 | tf_op jit(solution)/shard_map/ppermute | solution.py:23
  16.4 0.8 slice_select_fusion
  17.4 1.0 collective-permute-start.2
  18.4 6.2 %collective-permute-start.3 = (f32[5,6,8,3]{3,2,1,0:T(8,128)S(1)}, f32[5,6,8,3]{3,2,1,0:T(8,128)}, u32[]{:S(2)}, u32[]{:S(2)}) collective-permute-start(f32[5,6,8,3]{3,2,1,0:T(8,128)S(1)} %get-tuple-element.132), channel_id=1, source_target_pairs={{4,0},{8,4},{12,8},{16,12},{20,16},{24,20},{28,24},{32,28},{36,32}... | collective-permute-start | bytes 8648 | tf_op jit(solution)/shard_map/ppermute | solution.py:23
  24.6 0.1 fusion.234
  24.8 0.8 fusion.232
  26.4 0.3 slice.901
  26.7 2.6 %slice.903 = f32[1,6,3,1024]{3,2,1,0:T(4,128)} reverse(f32[1,6,3,1024]{3,2,1,0:T(4,128)S(1)} %get-tuple-element.139), dimensions={2} | reverse | bytes 147456 | tf_op jit(solution)/shard_map/slice | solution.py:175
  29.3 0.5 slice.899
  29.9 0.3 slice.909
  30.2 0.3 slice.911
  30.6 0.5 slice.907
  31.2 1.5 %concatenate.53 = f32[5,6,8,1030]{3,2,1,0:T(8,128)S(1)} concatenate(f32[5,6,8,3]{3,2,1,0:T(8,128)} %collective-permute-done.2, f32[5,6,8,1024]{3,2,1,0:T(8,128)S(1)} %copy-done, f32[5,6,8,3]{3,2,1,0:T(8,128)} %collective-permute-done.3), dimensions={3} | concatenate | bytes 1977600 | tf_op jit(solution)/shard_map/concatenate | solution.py:19
  32.8 1.2 maximum_select_fusion.2
  34.0 1.2 maximum_select_fusion.3
  35.2 0.4 pad_maximum_fusion
  35.6 0.4 fusion.2
  36.1 0.4 broadcast_multiply_fusion
  36.6 0.2 slice_add_fusion.2
  36.8 0.1 slice_add_fusion.1
  36.9 12.4 %constant_dynamic-update-slice_fusion = (f32[5,6,9,1024]{3,2,1,0:T(8,128)S(1)}, f32[1,6,9,1024]{3,2,1,0:T(8,128)S(1)}, f32[1,6,9,1024]{3,2,1,0:T(8,128)S(1)}, f3...) fusion(f32[1,6,14,1024]{3,2,1,0:T(8,128)S(1)} %get-tuple-elemen, ...), kind=kLoop, calls=%fused_computation.412 | loop fusion | flops 42190848 | bytes 22044672
  49.3 2.8 %add_dynamic-update-slice_fusion.3 = (f32[5,6,9,1024]{3,2,1,0:T(8,128)S(1)}, f32[1,6,9,1024]{3,2,1,0:T(8,128)S(1)}) fusion(f32[5,6,9,1024]{3,2,1,0:T(8,128)S(1)} %get-tuple-element.93, f32[1,6,9,1024]{3,2,1,0:T(8,128)S(1)} %get-tuple-element.110, f32[1,6,9,1024]{3,2,1,0:T(8,128)S(1)} %get-tuple-element.94, f32[1,6,9,1024]{3,2,1,0:T(8,128)S(1)} %get-tuple-element.120, ...), kind=kLoop, calls=%fused_computation.172 | loop fusion | flops 9897984 | bytes 11010048
  52.2 2.8 %add_dynamic-update-slice_fusion.2 = (f32[5,6,9,1024]{3,2,1,0:T(8,128)S(1)}, f32[1,6,9,1024]{3,2,1,0:T(8,128)S(1)}) fusion(f32[5,6,9,1024]{3,2,1,0:T(8,128)S(1)} %get-tuple-element.91, f32[1,6,9,1024]{3,2,1,0:T(8,128)S(1)} %get-tuple-element.111, f32[1,6,9,1024]{3,2,1,0:T(8,128)S(1)} %get-tuple-element.94, f32[1,6,9,1024]{3,2,1,0:T(8,128)S(1)} %get-tuple-element.120, ...), kind=kLoop, calls=%fused_computation.164 | loop fusion | flops 9897984 | bytes 11010048
  55.0 9.8 %add_dynamic-update-slice_fusion.1 = (f32[5,6,9,1024]{3,2,1,0:T(8,128)S(1)}, f32[1,6,9,1024]{3,2,1,0:T(8,128)S(1)}, f32[1,6,9,1024]{3,2,1,0:T(8,128)S(1)}, f32[1,6,9,1024]{3,2,1,0:T(8,128)S(1)}) fusion(f32[5,6,9,1024]{3,2,1,0:T(8,128)S(1)} %get-tuple-element.89, f32[1,6,9,1024]{3,2,1,0:T(8,128)S(1)} %get-tuple-element.97, ...), kind=kLoop, calls=%fused_computation.141 | loop fusion | flops 35665920 | bytes 17694720
  64.8 0.5 add_dynamic-update-slice_fusion
  65.4 0.2 slice_subtract_fusion.1
  65.5 0.2 copy.5
  65.7 0.9 copy-done.1
  66.6 0.6 slice.1190
  68.6 3.1 %all-gather.5.cloned.1.call-done = f32[40,3,8,1024]{3,2,1,0:T(8,128)} async-done(((f32[5,3,8,1024]{3,2,1,0:T(8,128)}), f32[40,3,8,1024]{3,2,1,0:T(8,128)}) %all-gather.5.cloned.1.call-update) | async-done | bytes 3932176 | tf_op jit(solution)/shard_map/all_gather | solution.py:201
  71.7 1.1 dynamic-slice_bitcast_fusion
  72.8 0.7 rev.2
  73.6 0.6 slice.1191
  75.5 1.6 %fusion.5 = f32[5,6,8,1025]{3,2,1,0:T(8,128)} fusion(f32[5,6,8,1030]{3,2,1,0:T(8,128)S(1)} %broadcast_select_fusion), kind=kLoop, calls=%fused_computation.68 | loop fusion | flops 492000 | bytes 2952000 | tf_op jit(solution)/shard_map/mul | solution.py:89
  77.4 1.1 copy-done.3
  78.5 6.4 %constant_dynamic-update-slice_fusion.1 = (f32[5,6,8,1025]{3,2,1,0:T(8,128)S(1)}, f32[1,6,8,1025]{3,2,1,0:T(8,128)S(1)}, f32[1,6,8,1025]{3,2,1,0:T(8,128)S(1)}, ...) fusion(f32[5,6,8,1030]{3,2,1,0:T(8,128)S(1)} %broadcast_select_, ...), kind=kLoop, calls=%fused_computation.413 | loop fusion | flops 35768400 | bytes 17215680
  84.9 1.5 %add_dynamic-update-slice_fusion.7 = (f32[5,6,8,1025]{3,2,1,0:T(8,128)S(1)}, f32[1,6,8,1025]{3,2,1,0:T(8,128)S(1)}) fusion(f32[5,6,8,1025]{3,2,1,0:T(8,128)S(1)} %get-tuple-element.63, f32[1,6,8,1025]{3,2,1,0:T(8,128)S(1)} %get-tuple-element.80, f32[1,6,8,1025]{3,2,1,0:T(8,128)S(1)} %get-tuple-element.64, f32[1,6,8,1025]{3,2,1,0:T(8,128)S(1)} %get-tuple-element.82, ...), kind=kLoop, calls=%fused_computation.317 | loop fusion | flops 8511600 | bytes 6414336
  86.4 5.7 %add_dynamic-update-slice_fusion.6 = (f32[5,6,8,1025]{3,2,1,0:T(8,128)S(1)}, f32[1,6,8,1025]{3,2,1,0:T(8,128)S(1)}, f32[1,6,8,1025]{3,2,1,0:T(8,128)S(1)}, f32[1,6,8,1025]{3,2,1,0:T(8,128)S(1)}) fusion(f32[5,6,8,1025]{3,2,1,0:T(8,128)S(1)} %get-tuple-element.61, f32[1,6,8,1025]{3,2,1,0:T(8,128)S(1)} %get-tuple-element.67, ...), kind=kLoop, calls=%fused_computation.294 | loop fusion | flops 31734000 | bytes 9953280
  92.1 1.5 add_dynamic-update-slice_fusion.5
  93.6 0.3 add_dynamic-update-slice_fusion.4
  93.9 1.3 copy-done.2
  95.2 0.6 multiply_add_fusion
  95.8 0.2 copy.7
  96.0 0.5 slice.1268
  97.9 10.3 %all-gather.7.cloned.1.call-done = f32[20,3,8,1024]{3,2,1,0:T(8,128)} async-done(((f32[5,3,8,1024]{3,2,1,0:T(8,128)}), f32[20,3,8,1024]{3,2,1,0:T(8,128)}) %all-gather.7.cloned.1.call-update) | async-done | bytes 1966096 | tf_op jit(solution)/shard_map/all_gather | solution.py:211
  108.2 1.1 fusion.238
  109.2 3.8 %collective-permute-start.4 = (f32[5,3,8,1024]{3,2,1,0:T(8,128)S(1)}, f32[5,3,8,1024]{3,2,1,0:T(8,128)S(1)}, u32[]{:S(2)}, u32[]{:S(2)}) collective-permute-start(f32[5,3,8,1024]{3,2,1,0:T(8,128)S(1)} %fusion.238), channel_id=1, source_target_pairs={{0,132},{4,136},{8,140},{12,144},{16,148},{20,152},{24,156},{28,16... | collective-permute-start | bytes 1474568 | tf_op jit(solution)/shard_map/ppermute | solution.py:227
  113.0 0.2 collective-permute-start.5
  113.3 1.1 constant_dynamic-slice_fusion
  114.4 0.5 slice.1271
  116.3 1.4 fusion.4.padded_ref
  117.6 7.1 %shard_map.37 = f32[5,4,8,1024]{3,2,1,0:T(8,128)} custom-call(f32[5,9,8,1024]{3,2,1,0:T(8,128)} %fusion.4.padded_ref), custom_call_target="tpu_custom_call" | custom-call | tf_op jit(solution)/shard_map/pallas_call | solution.py:254
  124.7 1.0 slice_select_fusion.1.edge_ref
  125.7 0.1 slice_reduce_fusion
  125.9 1.3 fusion.231
  127.2 0.1 maximum_select_fusion.1.partial_ref
  127.4 0.2 fusion.186
  127.7 10.1 %collective-permute-done.5 = f32[5,3,8,1024]{3,2,1,0:T(8,128)} collective-permute-done((f32[5,3,8,1024]{3,2,1,0:T(8,128)S(1)}, f32[5,3,8,1024]{3,2,1,0:T(8,128)}, u32[]{:S(2)}, u32[]{:S(2)}) %collective-permute-start.5) | collective-permute-done | bytes 491552 | tf_op jit(solution)/shard_map/ppermute | solution.py:227
  137.8 1.3 fusion.6
  139.1 0.2 fusion.7
  139.4 0.8 pad_maximum_fusion.1.ghost_ref
  140.2 6.3 %shard_map.38 = f32[5,6,8,1024]{3,2,1,0:T(8,128)} custom-call(s32[1]{0:T(128)} %bitcast.flag_ref, f32[5,6,8,1024]{3,2,1,0:T(8,128)} %section_ref.1, f32[5,3,8,1024]{3,2,1,0:T(8,128)} %pad_maximum_fusion.1.ghost_ref, f32[5,1,8,1024]{3,2,1,0:T(8,128)} %copy-done.7, f32[5,6,8,1024]{3,2,1,0:T(8,128)} %copy-done.5), custom_call_target="tpu_custom_call", output_to_operand_aliasing={{}: (4, {})} | custom-call | tf_op jit(solution)/shard_map/pallas_call | solution.py:290
  (41 shorter events, 1.0 us)
Async XLA Ops:
  6.5 9.9 %copy-start = (f32[5,6,8,1024]{3,2,1,0:T(8,128)S(1)}, f32[5,6,8,1024]{3,2,1,0:T(8,128)}, u32[]{:S(2)}) copy-start(f32[5,6,8,1024]{3,2,1,0:T(8,128)} %section_ref.1) | copy-start | bytes 2949124
  6.5 65.2 %all-gather.5.cloned.1.call-start = ((), (), s32[]{:S(2)}) async-start(), calls=%async_computation | async-start | bytes 4423680 | tf_op jit(solution)/shard_map/all_gather | solution.py:201
  9.1 23.6 %collective-permute-start = (f32[5,6,3,1024]{3,2,1,0:T(4,128)}, f32[5,6,3,1024]{3,2,1,0:T(4,128)}, u32[]{:S(2)}, u32[]{:S(2)}) collective-permute-start(f32[5,6,3,1024]{3,2,1,0:T(4,128)} %get-tuple-element.140), channel_id=1, source_target_pairs={{0,1},{1,2},{2,3},{4,5},{5,6},{6,7},{8,9},{9,10},{10,11},{12,13},{... | collective-permute-start | bytes 1105928 | tf_op jit(solution)/shard_map/ppermute | solution.py:21
  13.7 20.3 %collective-permute-start.1 = (f32[5,6,3,1024]{3,2,1,0:T(4,128)S(1)}, f32[5,6,3,1024]{3,2,1,0:T(4,128)}, u32[]{:S(2)}, u32[]{:S(2)}) collective-permute-start(f32[5,6,3,1024]{3,2,1,0:T(4,128)S(1)} %get-tuple-element.141), channel_id=1, source_target_pairs={{1,0},{2,1},{3,2},{5,4},{6,5},{7,6},{9,8},{10,9},{11,10},{13,12},{... | collective-permute-start | bytes 1105928 | tf_op jit(solution)/shard_map/ppermute | solution.py:23
  17.3 90.9 %all-gather.7.cloned.1.call-start = ((), (), s32[]{:S(2)}) async-start(), calls=%async_computation.1 | async-start | bytes 2457600 | tf_op jit(solution)/shard_map/all_gather | solution.py:211
  17.4 13.8 %collective-permute-start.2 = (f32[5,6,8,3]{3,2,1,0:T(8,128)S(1)}, f32[5,6,8,3]{3,2,1,0:T(8,128)}, u32[]{:S(2)}, u32[]{:S(2)}) collective-permute-start(f32[5,6,8,3]{3,2,1,0:T(8,128)S(1)} %get-tuple-element.133), channel_id=1, source_target_pairs={{0,4},{4,8},{8,12},{12,16},{16,20},{20,24},{24,28},{28,32},{32,36}... | collective-permute-start | bytes 8648 | tf_op jit(solution)/shard_map/ppermute | solution.py:21
  18.4 12.8 %collective-permute-start.3 = (f32[5,6,8,3]{3,2,1,0:T(8,128)S(1)}, f32[5,6,8,3]{3,2,1,0:T(8,128)}, u32[]{:S(2)}, u32[]{:S(2)}) collective-permute-start(f32[5,6,8,3]{3,2,1,0:T(8,128)S(1)} %get-tuple-element.132), channel_id=1, source_target_pairs={{4,0},{8,4},{12,8},{16,12},{20,16},{24,20},{28,24},{32,28},{36,32}... | collective-permute-start | bytes 8648 | tf_op jit(solution)/shard_map/ppermute | solution.py:23
  65.3 1.3 copy-start.1
  73.5 1.8 %copy-start.4 = (f32[5,3,8,1024]{3,2,1,0:T(8,128)}, f32[5,3,8,1024]{3,2,1,0:T(8,128)S(1)}, u32[]{:S(2)}) copy-start(f32[5,3,8,1024]{3,2,1,0:T(8,128)S(1)} %rev.2) | copy-start | bytes 1474564
  77.2 1.2 copy-start.3
  92.1 1.8 %copy-start.6 = (f32[5,6,8,1024]{3,2,1,0:T(8,128)S(1)}, f32[5,6,8,1024]{3,2,1,0:T(8,128)}, u32[]{:S(2)}) copy-start(f32[5,6,8,1024]{3,2,1,0:T(8,128)} %param.11) | copy-start | bytes 2949124
  93.6 1.6 %copy-start.2 = (f32[5,6,9,1024]{3,2,1,0:T(8,128)S(1)}, f32[5,6,9,1024]{3,2,1,0:T(8,128)}, u32[]{:S(2)}) copy-start(f32[5,6,9,1024]{3,2,1,0:T(8,128)} %copy-done.1) | copy-start | bytes 3317764
  96.0 20.2 %copy-start.8 = (f32[5,1,8,1024]{3,2,1,0:T(8,128)S(1)}, f32[5,1,8,1024]{3,2,1,0:T(8,128)}, u32[]{:S(2)}) copy-start(f32[5,1,8,1024]{3,2,1,0:T(8,128)} %get-tuple-element.130) | copy-start | bytes 491524
  96.0 20.2 %copy-start.9 = (f32[5,1,8,1024]{3,2,1,0:T(8,128)S(1)}, f32[5,1,8,1024]{3,2,1,0:T(8,128)}, u32[]{:S(2)}) copy-start(f32[5,1,8,1024]{3,2,1,0:T(8,128)} %get-tuple-element.131) | copy-start | bytes 491524
  109.2 18.4 %collective-permute-start.4 = (f32[5,3,8,1024]{3,2,1,0:T(8,128)S(1)}, f32[5,3,8,1024]{3,2,1,0:T(8,128)S(1)}, u32[]{:S(2)}, u32[]{:S(2)}) collective-permute-start(f32[5,3,8,1024]{3,2,1,0:T(8,128)S(1)} %fusion.238), channel_id=1, source_target_pairs={{0,132},{4,136},{8,140},{12,144},{16,148},{20,152},{24,156},{28,16... | collective-permute-start | bytes 1474568 | tf_op jit(solution)/shard_map/ppermute | solution.py:227
  113.0 24.7 %collective-permute-start.5 = (f32[5,3,8,1024]{3,2,1,0:T(8,128)S(1)}, f32[5,3,8,1024]{3,2,1,0:T(8,128)}, u32[]{:S(2)}, u32[]{:S(2)}) collective-permute-start(f32[5,3,8,1024]{3,2,1,0:T(8,128)S(1)} %fusion.238), channel_id=1, source_target_pairs={{0,128},{4,132},{8,136},{12,140},{16,144},{20,148},{24,152},{28,15... | collective-permute-start | bytes 1474568 | tf_op jit(solution)/shard_map/ppermute | solution.py:227
  125.7 1.6 %copy-start.7 = (f32[5,1,8,1024]{3,2,1,0:T(8,128)}, f32[5,1,8,1024]{3,2,1,0:T(8,128)S(1)}, u32[]{:S(2)}) copy-start(f32[5,1,8,1024]{3,2,1,0:T(8,128)S(1)} %slice_select_fusion.1.edge_ref) | copy-start | bytes 491524
  127.4 12.0 %copy-start.5 = (f32[5,6,8,1024]{3,2,1,0:T(8,128)}, f32[5,6,8,1024]{3,2,1,0:T(8,128)S(1)}, u32[]{:S(2)}) copy-start(f32[5,6,8,1024]{3,2,1,0:T(8,128)S(1)} %maximum_select_fusion.1.partial_ref) | copy-start | bytes 2949124
Sparse Core Ops, SparseCore 0:
  17.4 54.2 all-gather.4
  77.2 30.8 all-gather.6

commit v9 on v8

--- a/solution.py
+++ b/solution.py
@@ -310,7 +310,9 @@
     bands = section_state.shape[2]
     width = section_state.shape[3]
     fraction = (rotor_step[0] % 4).astype(jnp.float32) / 4.0
-    theta_padded = padded_2(section_state, ((("tx", "tz"), 3),), 3, True)
+    early_front = lax.axis_index("blk") == 0
+    early_out = jnp.where(early_front, section_state[:, -3:], section_state[:, :3])
+    theta_padded = padded_2(hold(section_state, early_out), ((("tx", "tz"), 3),), 3, True)
     radial_raw = padded_2(section_state, (("radial", 2),), 3, False)
     band_index = lax.axis_index("radial")
     band_count = lax.axis_size("radial")
@@ -323,7 +325,7 @@
     radial_padded = jnp.concatenate([lower_wall, section_state, upper_wall], axis=2)
     block_index = lax.axis_index("blk")
     front = block_index == 0
-    outgoing = jnp.where(front, section_state[:, -3:], section_state[:, :3])
+    outgoing = early_out
     radial = divergence(radial_padded, 2, bands, 3, 1, 2)
     chosen = pick_column(outgoing, rotor_step, radial)
     theta_padded = hold(theta_padded, chosen)

time: 154 us -> 160 us (1.039)
  local copies, waits for them, and re-layouts: 20.1 us -> 27 us
  waiting for transfers between devices: 23.5 us -> 20.1 us
    slice x8, local copies, waits for them, and re-layouts: 4.88 us -> 9.29 us  [flip_radial(): return jnp.concatenate([turned[:3], -turned[3:4], turned[4:]], axis=0)]
    all_gather x1, waiting for transfers between devices: 3.08 us -> 0.02 us  [pick_column(): gathered = lax.all_gather(slab, 'tz')]
    unnamed x24 -> x25, local copies, waits for them, and re-layouts: 3.89 us -> 4.97 us
  transfers between devices with their start and end apart: 8 -> 8, of which waited for: 3 -> 2; matrix products, arithmetic and copies ran while one was open for 42% -> 45% of each run, Pallas kernels for 5% -> 4%
where the time goes in v9:
time: 160 us; the launch traced here: 159 us
  other arithmetic  58.9 us (37%)
  local copies, waits for them, and re-layouts  27 us (17%)
  between operations  21.1 us (13%)
  waiting for transfers between devices  20.1 us (13%)
  starting transfers between devices  18.4 us (11%)
  Pallas kernels  13.3 us (8%)
    unnamed x8, other arithmetic  43 us
    ppermute x1, waiting for transfers between devices, cross_blocks(): lax.ppermute(slab, axes, this_route)  10.2 us
    all_gather x1, waiting for transfers between devices, pick_row(): gathered = lax.all_gather(slab, 'tx')  9.85 us
    slice x8, local copies, waits for them, and re-layouts, flip_radial(): return jnp.concatenate([turned[:3], -turned[3:4], turned[4:]], axis=0)  9.29 us
    ppermute x2, starting transfers between devices, padded_2(): lax.ppermute(head, axis, [((i + 1) % count, i) for i in range(ends)])  8.75 us
    pallas_call x1, Pallas kernels, axial_faces(): pl.pallas_call(axial_kernel, grid=(width // lanes,), in_specs=[pl.BlockSp...  7.06 us
    pallas_call x1, Pallas kernels, mortar_planes_of(): pl.pallas_call(mortar_kernel, grid_spec=pltpu.PrefetchScalarGridSpec(num_...  6.29 us
    ppermute x2, starting transfers between devices, padded_2(): lax.ppermute(tail, axis, [(i, (i + 1) % count) for i in range(ends)])  5.53 us
  transfers between devices with their start and end apart: 8, of which 2 were waited for; matrix products, arithmetic and copies ran while one was open for 45% of the time, Pallas kernels for 4%

profile of v9, /device:TPU:1, one launch (start us, length us, event | category | flops | bytes accessed | tf_op | source)
XLA Modules:
  0.0 158.8 jit_solution(9870419516326488332)
XLA Ops:
  6.5 2.8 %fusion.236 = (f32[5,6,3,1024]{3,2,1,0:T(4,128)}, f32[5,6,3,1024]{3,2,1,0:T(4,128)}) fusion(f32[5,6,8,1024]{3,2,1,0:T(8,128)} %section_ref.1), kind=kLoop, calls=%fused_computation.450 | loop fusion | bytes 1474560 | tf_op jit(solution)/shard_map/slice | solution.py:18
  9.3 4.6 %collective-permute-start = (f32[5,6,3,1024]{3,2,1,0:T(4,128)}, f32[5,6,3,1024]{3,2,1,0:T(4,128)}, u32[]{:S(2)}, u32[]{:S(2)}) collective-permute-start(f32[5,6,3,1024]{3,2,1,0:T(4,128)} %get-tuple-element.140), channel_id=1, source_target_pairs={{0,1},{1,2},{2,3},{4,5},{5,6},{6,7},{8,9},{9,10},{10,11},{12,13},{... | collective-permute-start | bytes 1105928 | tf_op jit(solution)/shard_map/ppermute | solution.py:21
  13.9 2.6 %collective-permute-start.1 = (f32[5,6,3,1024]{3,2,1,0:T(4,128)}, f32[5,6,3,1024]{3,2,1,0:T(4,128)}, u32[]{:S(2)}, u32[]{:S(2)}) collective-permute-start(f32[5,6,3,1024]{3,2,1,0:T(4,128)} %get-tuple-element.141), channel_id=1, source_target_pairs={{1,0},{2,1},{3,2},{5,4},{6,5},{7,6},{9,8},{10,9},{11,10},{13,12},{... | collective-permute-start | bytes 1105928 | tf_op jit(solution)/shard_map/ppermute | solution.py:23
  16.6 0.8 slice_select_fusion
  17.5 1.1 copy.7
  18.6 0.5 slice.1196
  20.5 0.8 fusion.233
  21.2 0.9 collective-permute-start.2
  22.2 6.1 %collective-permute-start.3 = (f32[5,6,8,3]{3,2,1,0:T(8,128)}, f32[5,6,8,3]{3,2,1,0:T(8,128)}, u32[]{:S(2)}, u32[]{:S(2)}) collective-permute-start(f32[5,6,8,3]{3,2,1,0:T(8,128)} %get-tuple-element.132), channel_id=1, source_target_pairs={{4,0},{8,4},{12,8},{16,12},{20,16},{24,20},{28,24},{32,28},{36,32}... | collective-permute-start | bytes 8648 | tf_op jit(solution)/shard_map/ppermute | solution.py:23
  28.3 0.1 fusion.234
  28.5 0.8 fusion.232
  30.1 0.3 slice.904
  30.4 0.7 neg.169
  31.1 2.5 %slice.906 = f32[1,6,3,1024]{3,2,1,0:T(4,128)} reverse(f32[1,6,3,1024]{3,2,1,0:T(4,128)S(1)} %get-tuple-element.139), dimensions={2} | reverse | bytes 147456 | tf_op jit(solution)/shard_map/slice | solution.py:175
  33.6 0.5 slice.902
  34.2 0.3 slice.912
  34.6 2.6 %slice.914 = f32[1,6,3,1024]{3,2,1,0:T(4,128)} reverse(f32[1,6,3,1024]{3,2,1,0:T(4,128)S(1)} %get-tuple-element.137), dimensions={2} | reverse | bytes 147456 | tf_op jit(solution)/shard_map/slice | solution.py:175
  37.1 2.8 %slice.910 = f32[3,6,3,1024]{3,2,1,0:T(4,128)} reverse(f32[3,6,3,1024]{3,2,1,0:T(4,128)S(1)} %get-tuple-element.135), dimensions={2} | reverse | bytes 442368 | tf_op jit(solution)/shard_map/slice | solution.py:175
  39.9 1.5 concatenate.53
  41.4 1.3 maximum_select_fusion.2
  42.8 1.4 maximum_select_fusion.3
  44.1 0.4 pad_maximum_fusion
  44.5 0.4 fusion.2
  45.0 0.4 broadcast_multiply_fusion
  45.5 0.2 slice_add_fusion.2
  45.8 12.4 %constant_dynamic-update-slice_fusion = (f32[5,6,9,1024]{3,2,1,0:T(8,128)S(1)}, f32[1,6,9,1024]{3,2,1,0:T(8,128)S(1)}, f32[1,6,9,1024]{3,2,1,0:T(8,128)S(1)}, f3...) fusion(f32[1,6,14,1024]{3,2,1,0:T(8,128)S(1)} %get-tuple-elemen, ...), kind=kLoop, calls=%fused_computation.413 | loop fusion | flops 42190848 | bytes 22044672
  58.2 2.8 %add_dynamic-update-slice_fusion.3 = (f32[5,6,9,1024]{3,2,1,0:T(8,128)S(1)}, f32[1,6,9,1024]{3,2,1,0:T(8,128)S(1)}) fusion(f32[5,6,9,1024]{3,2,1,0:T(8,128)S(1)} %get-tuple-element.93, f32[1,6,9,1024]{3,2,1,0:T(8,128)S(1)} %get-tuple-element.110, f32[1,6,9,1024]{3,2,1,0:T(8,128)S(1)} %get-tuple-element.94, f32[1,6,9,1024]{3,2,1,0:T(8,128)S(1)} %get-tuple-element.120, ...), kind=kLoop, calls=%fused_computation.173 | loop fusion | flops 9897984 | bytes 11010048
  61.1 2.8 %add_dynamic-update-slice_fusion.2 = (f32[5,6,9,1024]{3,2,1,0:T(8,128)S(1)}, f32[1,6,9,1024]{3,2,1,0:T(8,128)S(1)}) fusion(f32[5,6,9,1024]{3,2,1,0:T(8,128)S(1)} %get-tuple-element.91, f32[1,6,9,1024]{3,2,1,0:T(8,128)S(1)} %get-tuple-element.111, f32[1,6,9,1024]{3,2,1,0:T(8,128)S(1)} %get-tuple-element.94, f32[1,6,9,1024]{3,2,1,0:T(8,128)S(1)} %get-tuple-element.120, ...), kind=kLoop, calls=%fused_computation.165 | loop fusion | flops 9897984 | bytes 11010048
  63.9 9.8 %add_dynamic-update-slice_fusion.1 = (f32[5,6,9,1024]{3,2,1,0:T(8,128)S(1)}, f32[1,6,9,1024]{3,2,1,0:T(8,128)S(1)}, f32[1,6,9,1024]{3,2,1,0:T(8,128)S(1)}, f32[1,6,9,1024]{3,2,1,0:T(8,128)S(1)}) fusion(f32[5,6,9,1024]{3,2,1,0:T(8,128)S(1)} %get-tuple-element.89, f32[1,6,9,1024]{3,2,1,0:T(8,128)S(1)} %get-tuple-element.97, ...), kind=kLoop, calls=%fused_computation.142 | loop fusion | flops 35665920 | bytes 17694720
  73.7 0.5 add_dynamic-update-slice_fusion
  74.3 0.2 slice_subtract_fusion.1
  74.4 0.2 copy.5
  74.6 0.9 copy-done.1
  75.5 0.5 slice.1194
  77.4 1.1 dynamic-slice_bitcast_fusion
  78.4 0.7 rev.2
  79.3 0.6 slice.1195
  81.4 1.6 %fusion.5 = f32[5,6,8,1025]{3,2,1,0:T(8,128)} fusion(f32[5,6,8,1030]{3,2,1,0:T(8,128)S(1)} %broadcast_select_fusion), kind=kLoop, calls=%fused_computation.68 | loop fusion | flops 492000 | bytes 2952000 | tf_op jit(solution)/shard_map/mul | solution.py:89
  83.3 1.1 copy-done.3
  84.4 6.4 %constant_dynamic-update-slice_fusion.1 = (f32[5,6,8,1025]{3,2,1,0:T(8,128)S(1)}, f32[1,6,8,1025]{3,2,1,0:T(8,128)S(1)}, f32[1,6,8,1025]{3,2,1,0:T(8,128)S(1)}, ...) fusion(f32[5,6,8,1030]{3,2,1,0:T(8,128)S(1)} %broadcast_select_, ...), kind=kLoop, calls=%fused_computation.414 | loop fusion | flops 35768400 | bytes 17215680
  90.8 1.5 add_dynamic-update-slice_fusion.7
  92.3 5.7 %add_dynamic-update-slice_fusion.6 = (f32[5,6,8,1025]{3,2,1,0:T(8,128)S(1)}, f32[1,6,8,1025]{3,2,1,0:T(8,128)S(1)}, f32[1,6,8,1025]{3,2,1,0:T(8,128)S(1)}, f32[1,6,8,1025]{3,2,1,0:T(8,128)S(1)}) fusion(f32[5,6,8,1025]{3,2,1,0:T(8,128)S(1)} %get-tuple-element.61, f32[1,6,8,1025]{3,2,1,0:T(8,128)S(1)} %get-tuple-element.67, ...), kind=kLoop, calls=%fused_computation.295 | loop fusion | flops 31734000 | bytes 9953280
  98.0 1.5 add_dynamic-update-slice_fusion.5
  99.6 0.3 add_dynamic-update-slice_fusion.4
  99.8 1.3 copy-done.2
  101.1 0.6 multiply_add_fusion
  101.7 0.2 copy.8
  101.9 0.5 slice.1275
  103.7 9.8 %all-gather.7.cloned.1.call-done = f32[20,3,8,1024]{3,2,1,0:T(8,128)} async-done(((f32[5,3,8,1024]{3,2,1,0:T(8,128)}), f32[20,3,8,1024]{3,2,1,0:T(8,128)}) %all-gather.7.cloned.1.call-update) | async-done | bytes 1966096 | tf_op jit(solution)/shard_map/all_gather | solution.py:211
  113.6 1.1 fusion.238
  114.6 3.8 %collective-permute-start.4 = (f32[5,3,8,1024]{3,2,1,0:T(8,128)S(1)}, f32[5,3,8,1024]{3,2,1,0:T(8,128)S(1)}, u32[]{:S(2)}, u32[]{:S(2)}) collective-permute-start(f32[5,3,8,1024]{3,2,1,0:T(8,128)S(1)} %fusion.238), channel_id=1, source_target_pairs={{0,132},{4,136},{8,140},{12,144},{16,148},{20,152},{24,156},{28,16... | collective-permute-start | bytes 1474568 | tf_op jit(solution)/shard_map/ppermute | solution.py:227
  118.4 0.2 collective-permute-start.5
  118.7 1.1 constant_dynamic-slice_fusion
  119.8 0.5 slice.1278
  121.7 1.4 fusion.4.padded_ref
  123.1 7.1 %shard_map.37 = f32[5,4,8,1024]{3,2,1,0:T(8,128)} custom-call(f32[5,9,8,1024]{3,2,1,0:T(8,128)} %fusion.4.padded_ref), custom_call_target="tpu_custom_call" | custom-call | tf_op jit(solution)/shard_map/pallas_call | solution.py:254
  130.1 1.0 slice_select_fusion.1.edge_ref
  131.3 1.3 fusion.231
  132.7 0.2 fusion.186
  133.0 10.2 %collective-permute-done.5 = f32[5,3,8,1024]{3,2,1,0:T(8,128)} collective-permute-done((f32[5,3,8,1024]{3,2,1,0:T(8,128)S(1)}, f32[5,3,8,1024]{3,2,1,0:T(8,128)}, u32[]{:S(2)}, u32[]{:S(2)}) %collective-permute-start.5) | collective-permute-done | bytes 491552 | tf_op jit(solution)/shard_map/ppermute | solution.py:227
  143.2 1.4 fusion.6
  144.6 0.2 fusion.7
  144.8 0.8 pad_maximum_fusion.1.ghost_ref
  145.7 6.3 %shard_map.38 = f32[5,6,8,1024]{3,2,1,0:T(8,128)} custom-call(s32[1]{0:T(128)} %bitcast.flag_ref, f32[5,6,8,1024]{3,2,1,0:T(8,128)} %section_ref.1, f32[5,3,8,1024]{3,2,1,0:T(8,128)} %pad_maximum_fusion.1.ghost_ref, f32[5,1,8,1024]{3,2,1,0:T(8,128)} %copy-done.7, f32[5,6,8,1024]{3,2,1,0:T(8,128)} %copy-done.5), custom_call_target="tpu_custom_call", output_to_operand_aliasing={{}: (4, {})} | custom-call | tf_op jit(solution)/shard_map/pallas_call | solution.py:290
  (44 shorter events, 1.4 us)
Async XLA Ops:
  6.5 10.0 %copy-start = (f32[5,6,8,1024]{3,2,1,0:T(8,128)S(1)}, f32[5,6,8,1024]{3,2,1,0:T(8,128)}, u32[]{:S(2)}) copy-start(f32[5,6,8,1024]{3,2,1,0:T(8,128)} %section_ref.1) | copy-start | bytes 2949124
  6.5 70.8 %all-gather.5.cloned.1.call-start = ((), (), s32[]{:S(2)}) async-start(), calls=%async_computation | async-start | bytes 4423680 | tf_op jit(solution)/shard_map/all_gather | solution.py:201
  9.3 32.1 %collective-permute-start = (f32[5,6,3,1024]{3,2,1,0:T(4,128)}, f32[5,6,3,1024]{3,2,1,0:T(4,128)}, u32[]{:S(2)}, u32[]{:S(2)}) collective-permute-start(f32[5,6,3,1024]{3,2,1,0:T(4,128)} %get-tuple-element.140), channel_id=1, source_target_pairs={{0,1},{1,2},{2,3},{4,5},{5,6},{6,7},{8,9},{9,10},{10,11},{12,13},{... | collective-permute-start | bytes 1105928 | tf_op jit(solution)/shard_map/ppermute | solution.py:21
  13.9 28.8 %collective-permute-start.1 = (f32[5,6,3,1024]{3,2,1,0:T(4,128)}, f32[5,6,3,1024]{3,2,1,0:T(4,128)}, u32[]{:S(2)}, u32[]{:S(2)}) collective-permute-start(f32[5,6,3,1024]{3,2,1,0:T(4,128)} %get-tuple-element.141), channel_id=1, source_target_pairs={{1,0},{2,1},{3,2},{5,4},{6,5},{7,6},{9,8},{10,9},{11,10},{13,12},{... | collective-permute-start | bytes 1105928 | tf_op jit(solution)/shard_map/ppermute | solution.py:23
  17.4 96.1 %all-gather.7.cloned.1.call-start = ((), (), s32[]{:S(2)}) async-start(), calls=%async_computation.1 | async-start | bytes 2457600 | tf_op jit(solution)/shard_map/all_gather | solution.py:211
  21.2 18.7 %collective-permute-start.2 = (f32[5,6,8,3]{3,2,1,0:T(8,128)}, f32[5,6,8,3]{3,2,1,0:T(8,128)}, u32[]{:S(2)}, u32[]{:S(2)}) collective-permute-start(f32[5,6,8,3]{3,2,1,0:T(8,128)} %get-tuple-element.133), channel_id=1, source_target_pairs={{0,4},{4,8},{8,12},{12,16},{16,20},{20,24},{24,28},{28,32},{32,36}... | collective-permute-start | bytes 8648 | tf_op jit(solution)/shard_map/ppermute | solution.py:21
  22.2 17.7 %collective-permute-start.3 = (f32[5,6,8,3]{3,2,1,0:T(8,128)}, f32[5,6,8,3]{3,2,1,0:T(8,128)}, u32[]{:S(2)}, u32[]{:S(2)}) collective-permute-start(f32[5,6,8,3]{3,2,1,0:T(8,128)} %get-tuple-element.132), channel_id=1, source_target_pairs={{4,0},{8,4},{12,8},{16,12},{20,16},{24,20},{28,24},{32,28},{36,32}... | collective-permute-start | bytes 8648 | tf_op jit(solution)/shard_map/ppermute | solution.py:23
  74.3 1.3 copy-start.1
  79.2 2.0 %copy-start.4 = (f32[5,3,8,1024]{3,2,1,0:T(8,128)}, f32[5,3,8,1024]{3,2,1,0:T(8,128)S(1)}, u32[]{:S(2)}) copy-start(f32[5,3,8,1024]{3,2,1,0:T(8,128)S(1)} %rev.2) | copy-start | bytes 1474564
  83.1 1.2 copy-start.3
  98.0 1.8 %copy-start.6 = (f32[5,6,8,1024]{3,2,1,0:T(8,128)S(1)}, f32[5,6,8,1024]{3,2,1,0:T(8,128)}, u32[]{:S(2)}) copy-start(f32[5,6,8,1024]{3,2,1,0:T(8,128)} %param.11) | copy-start | bytes 2949124
  99.5 1.6 copy-start.2
  101.9 19.7 %copy-start.8 = (f32[5,1,8,1024]{3,2,1,0:T(8,128)S(1)}, f32[5,1,8,1024]{3,2,1,0:T(8,128)}, u32[]{:S(2)}) copy-start(f32[5,1,8,1024]{3,2,1,0:T(8,128)} %get-tuple-element.130) | copy-start | bytes 491524
  101.9 19.7 %copy-start.9 = (f32[5,1,8,1024]{3,2,1,0:T(8,128)S(1)}, f32[5,1,8,1024]{3,2,1,0:T(8,128)}, u32[]{:S(2)}) copy-start(f32[5,1,8,1024]{3,2,1,0:T(8,128)} %get-tuple-element.131) | copy-start | bytes 491524
  114.6 18.4 %collective-permute-start.4 = (f32[5,3,8,1024]{3,2,1,0:T(8,128)S(1)}, f32[5,3,8,1024]{3,2,1,0:T(8,128)S(1)}, u32[]{:S(2)}, u32[]{:S(2)}) collective-permute-start(f32[5,3,8,1024]{3,2,1,0:T(8,128)S(1)} %fusion.238), channel_id=1, source_target_pairs={{0,132},{4,136},{8,140},{12,144},{16,148},{20,152},{24,156},{28,16... | collective-permute-start | bytes 1474568 | tf_op jit(solution)/shard_map/ppermute | solution.py:227
  118.4 24.7 %collective-permute-start.5 = (f32[5,3,8,1024]{3,2,1,0:T(8,128)S(1)}, f32[5,3,8,1024]{3,2,1,0:T(8,128)}, u32[]{:S(2)}, u32[]{:S(2)}) collective-permute-start(f32[5,3,8,1024]{3,2,1,0:T(8,128)S(1)} %fusion.238), channel_id=1, source_target_pairs={{0,128},{4,132},{8,136},{12,140},{16,144},{20,148},{24,152},{28,15... | collective-permute-start | bytes 1474568 | tf_op jit(solution)/shard_map/ppermute | solution.py:227
  131.1 1.6 copy-start.7
  132.7 12.1 %copy-start.5 = (f32[5,6,8,1024]{3,2,1,0:T(8,128)}, f32[5,6,8,1024]{3,2,1,0:T(8,128)S(1)}, u32[]{:S(2)}) copy-start(f32[5,6,8,1024]{3,2,1,0:T(8,128)S(1)} %maximum_select_fusion.1.partial_ref) | copy-start | bytes 2949124
Sparse Core Ops, SparseCore 0:
  17.6 54.3 all-gather.4
  83.1 30.3 all-gather.6

commit v10 on v8

--- a/solution.py
+++ b/solution.py
@@ -284,7 +284,7 @@
 
 def mortar_planes_of(section_state, ghost, edge, partial):
     components, planes, bands, width = section_state.shape
-    lanes = 256
+    lanes = 512
     flag = lax.axis_index("blk").astype(jnp.int32).reshape(1)
     late = lambda i, flag_ref: (0, 1 - flag_ref[0], 0, i)
     return pl.pallas_call(

time: 154 us -> 154 us (level)
  no operation moved by 1% of the time
where the time goes in v10:
time: 154 us; the launch traced here: 153 us
  other arithmetic  57.9 us (38%)
  waiting for transfers between devices  23.5 us (15%)
  local copies, waits for them, and re-layouts  20.1 us (13%)
  between operations  19.9 us (13%)
  starting transfers between devices  18.5 us (12%)
  Pallas kernels  13.5 us (9%)
    unnamed x8, other arithmetic  43 us
    all_gather x1, waiting for transfers between devices, pick_row(): gathered = lax.all_gather(slab, 'tx')  10.3 us
    ppermute x1, waiting for transfers between devices, cross_blocks(): lax.ppermute(slab, axes, this_route)  10.1 us
    ppermute x2, starting transfers between devices, padded_2(): lax.ppermute(head, axis, [((i + 1) % count, i) for i in range(ends)])  8.89 us
    pallas_call x1, Pallas kernels, axial_faces(): pl.pallas_call(axial_kernel, grid=(width // lanes,), in_specs=[pl.BlockSp...  7.06 us
    pallas_call x1, Pallas kernels, mortar_planes_of(): pl.pallas_call(mortar_kernel, grid_spec=pltpu.PrefetchScalarGridSpec(num_...  6.4 us
    ppermute x2, starting transfers between devices, padded_2(): lax.ppermute(tail, axis, [(i, (i + 1) % count) for i in range(ends)])  5.55 us
    slice x8, local copies, waits for them, and re-layouts, flip_radial(): return jnp.concatenate([turned[:3], -turned[3:4], turned[4:]], axis=0)  4.88 us
  transfers between devices with their start and end apart: 8, of which 3 were waited for; matrix products, arithmetic and copies ran while one was open for 42% of the time, Pallas kernels for 5%

profile of v10, /device:TPU:1, one launch (start us, length us, event | category | flops | bytes accessed | tf_op | source)
XLA Modules:
  0.0 153.4 jit_solution(10033810697891817817)
XLA Ops:
  6.5 2.6 %fusion.236 = (f32[5,6,3,1024]{3,2,1,0:T(4,128)}, f32[5,6,3,1024]{3,2,1,0:T(4,128)S(1)}) fusion(f32[5,6,8,1024]{3,2,1,0:T(8,128)} %section_ref.1), kind=kLoop, calls=%fused_computation.449 | loop fusion | bytes 1474560 | tf_op jit(solution)/shard_map/slice | solution.py:18
  9.1 4.6 %collective-permute-start = (f32[5,6,3,1024]{3,2,1,0:T(4,128)}, f32[5,6,3,1024]{3,2,1,0:T(4,128)}, u32[]{:S(2)}, u32[]{:S(2)}) collective-permute-start(f32[5,6,3,1024]{3,2,1,0:T(4,128)} %get-tuple-element.140), channel_id=1, source_target_pairs={{0,1},{1,2},{2,3},{4,5},{5,6},{6,7},{8,9},{9,10},{10,11},{12,13},{... | collective-permute-start | bytes 1105928 | tf_op jit(solution)/shard_map/ppermute | solution.py:21
  13.7 2.7 %collective-permute-start.1 = (f32[5,6,3,1024]{3,2,1,0:T(4,128)S(1)}, f32[5,6,3,1024]{3,2,1,0:T(4,128)}, u32[]{:S(2)}, u32[]{:S(2)}) collective-permute-start(f32[5,6,3,1024]{3,2,1,0:T(4,128)S(1)} %get-tuple-element.141), channel_id=1, source_target_pairs={{1,0},{2,1},{3,2},{5,4},{6,5},{7,6},{9,8},{10,9},{11,10},{13,12},{... | collective-permute-start | bytes 1105928 | tf_op jit(solution)/shard_map/ppermute | solution.py:23
  16.4 0.8 slice_select_fusion
  17.4 1.0 collective-permute-start.2
  18.4 6.2 %collective-permute-start.3 = (f32[5,6,8,3]{3,2,1,0:T(8,128)S(1)}, f32[5,6,8,3]{3,2,1,0:T(8,128)}, u32[]{:S(2)}, u32[]{:S(2)}) collective-permute-start(f32[5,6,8,3]{3,2,1,0:T(8,128)S(1)} %get-tuple-element.132), channel_id=1, source_target_pairs={{4,0},{8,4},{12,8},{16,12},{20,16},{24,20},{28,24},{32,28},{36,32}... | collective-permute-start | bytes 8648 | tf_op jit(solution)/shard_map/ppermute | solution.py:23
  24.6 0.1 fusion.234
  24.8 0.8 fusion.232
  26.4 0.3 slice.901
  26.7 2.6 %slice.903 = f32[1,6,3,1024]{3,2,1,0:T(4,128)} reverse(f32[1,6,3,1024]{3,2,1,0:T(4,128)S(1)} %get-tuple-element.139), dimensions={2} | reverse | bytes 147456 | tf_op jit(solution)/shard_map/slice | solution.py:175
  29.3 0.5 slice.899
  29.9 0.3 slice.909
  30.2 0.3 slice.911
  30.6 0.5 slice.907
  31.2 1.5 %concatenate.53 = f32[5,6,8,1030]{3,2,1,0:T(8,128)S(1)} concatenate(f32[5,6,8,3]{3,2,1,0:T(8,128)} %collective-permute-done.2, f32[5,6,8,1024]{3,2,1,0:T(8,128)S(1)} %copy-done, f32[5,6,8,3]{3,2,1,0:T(8,128)} %collective-permute-done.3), dimensions={3} | concatenate | bytes 1977600 | tf_op jit(solution)/shard_map/concatenate | solution.py:19
  32.8 1.2 maximum_select_fusion.2
  34.0 1.2 maximum_select_fusion.3
  35.2 0.4 pad_maximum_fusion
  35.6 0.4 fusion.2
  36.1 0.4 broadcast_multiply_fusion
  36.6 0.2 slice_add_fusion.2
  36.8 0.1 slice_add_fusion.1
  36.9 12.4 %constant_dynamic-update-slice_fusion = (f32[5,6,9,1024]{3,2,1,0:T(8,128)S(1)}, f32[1,6,9,1024]{3,2,1,0:T(8,128)S(1)}, f32[1,6,9,1024]{3,2,1,0:T(8,128)S(1)}, f3...) fusion(f32[1,6,14,1024]{3,2,1,0:T(8,128)S(1)} %get-tuple-elemen, ...), kind=kLoop, calls=%fused_computation.412 | loop fusion | flops 42190848 | bytes 22044672
  49.3 2.8 %add_dynamic-update-slice_fusion.3 = (f32[5,6,9,1024]{3,2,1,0:T(8,128)S(1)}, f32[1,6,9,1024]{3,2,1,0:T(8,128)S(1)}) fusion(f32[5,6,9,1024]{3,2,1,0:T(8,128)S(1)} %get-tuple-element.93, f32[1,6,9,1024]{3,2,1,0:T(8,128)S(1)} %get-tuple-element.110, f32[1,6,9,1024]{3,2,1,0:T(8,128)S(1)} %get-tuple-element.94, f32[1,6,9,1024]{3,2,1,0:T(8,128)S(1)} %get-tuple-element.120, ...), kind=kLoop, calls=%fused_computation.172 | loop fusion | flops 9897984 | bytes 11010048
  52.2 2.8 %add_dynamic-update-slice_fusion.2 = (f32[5,6,9,1024]{3,2,1,0:T(8,128)S(1)}, f32[1,6,9,1024]{3,2,1,0:T(8,128)S(1)}) fusion(f32[5,6,9,1024]{3,2,1,0:T(8,128)S(1)} %get-tuple-element.91, f32[1,6,9,1024]{3,2,1,0:T(8,128)S(1)} %get-tuple-element.111, f32[1,6,9,1024]{3,2,1,0:T(8,128)S(1)} %get-tuple-element.94, f32[1,6,9,1024]{3,2,1,0:T(8,128)S(1)} %get-tuple-element.120, ...), kind=kLoop, calls=%fused_computation.164 | loop fusion | flops 9897984 | bytes 11010048
  55.0 9.8 %add_dynamic-update-slice_fusion.1 = (f32[5,6,9,1024]{3,2,1,0:T(8,128)S(1)}, f32[1,6,9,1024]{3,2,1,0:T(8,128)S(1)}, f32[1,6,9,1024]{3,2,1,0:T(8,128)S(1)}, f32[1,6,9,1024]{3,2,1,0:T(8,128)S(1)}) fusion(f32[5,6,9,1024]{3,2,1,0:T(8,128)S(1)} %get-tuple-element.89, f32[1,6,9,1024]{3,2,1,0:T(8,128)S(1)} %get-tuple-element.97, ...), kind=kLoop, calls=%fused_computation.141 | loop fusion | flops 35665920 | bytes 17694720
  64.8 0.5 add_dynamic-update-slice_fusion
  65.4 0.2 slice_subtract_fusion.1
  65.5 0.2 copy.5
  65.7 0.9 copy-done.1
  66.6 0.6 slice.1190
  68.6 3.1 %all-gather.5.cloned.1.call-done = f32[40,3,8,1024]{3,2,1,0:T(8,128)} async-done(((f32[5,3,8,1024]{3,2,1,0:T(8,128)}), f32[40,3,8,1024]{3,2,1,0:T(8,128)}) %all-gather.5.cloned.1.call-update) | async-done | bytes 3932176 | tf_op jit(solution)/shard_map/all_gather | solution.py:201
  71.7 1.1 dynamic-slice_bitcast_fusion
  72.8 0.7 rev.2
  73.6 0.6 slice.1191
  75.5 1.6 %fusion.5 = f32[5,6,8,1025]{3,2,1,0:T(8,128)} fusion(f32[5,6,8,1030]{3,2,1,0:T(8,128)S(1)} %broadcast_select_fusion), kind=kLoop, calls=%fused_computation.68 | loop fusion | flops 492000 | bytes 2952000 | tf_op jit(solution)/shard_map/mul | solution.py:89
  77.4 1.1 copy-done.3
  78.5 6.4 %constant_dynamic-update-slice_fusion.1 = (f32[5,6,8,1025]{3,2,1,0:T(8,128)S(1)}, f32[1,6,8,1025]{3,2,1,0:T(8,128)S(1)}, f32[1,6,8,1025]{3,2,1,0:T(8,128)S(1)}, ...) fusion(f32[5,6,8,1030]{3,2,1,0:T(8,128)S(1)} %broadcast_select_, ...), kind=kLoop, calls=%fused_computation.413 | loop fusion | flops 35768400 | bytes 17215680
  84.9 1.5 %add_dynamic-update-slice_fusion.7 = (f32[5,6,8,1025]{3,2,1,0:T(8,128)S(1)}, f32[1,6,8,1025]{3,2,1,0:T(8,128)S(1)}) fusion(f32[5,6,8,1025]{3,2,1,0:T(8,128)S(1)} %get-tuple-element.63, f32[1,6,8,1025]{3,2,1,0:T(8,128)S(1)} %get-tuple-element.80, f32[1,6,8,1025]{3,2,1,0:T(8,128)S(1)} %get-tuple-element.64, f32[1,6,8,1025]{3,2,1,0:T(8,128)S(1)} %get-tuple-element.82, ...), kind=kLoop, calls=%fused_computation.317 | loop fusion | flops 8511600 | bytes 6414336
  86.4 5.7 %add_dynamic-update-slice_fusion.6 = (f32[5,6,8,1025]{3,2,1,0:T(8,128)S(1)}, f32[1,6,8,1025]{3,2,1,0:T(8,128)S(1)}, f32[1,6,8,1025]{3,2,1,0:T(8,128)S(1)}, f32[1,6,8,1025]{3,2,1,0:T(8,128)S(1)}) fusion(f32[5,6,8,1025]{3,2,1,0:T(8,128)S(1)} %get-tuple-element.61, f32[1,6,8,1025]{3,2,1,0:T(8,128)S(1)} %get-tuple-element.67, ...), kind=kLoop, calls=%fused_computation.294 | loop fusion | flops 31734000 | bytes 9953280
  92.1 1.5 add_dynamic-update-slice_fusion.5
  93.6 0.3 add_dynamic-update-slice_fusion.4
  93.9 1.3 copy-done.2
  95.2 0.6 multiply_add_fusion
  95.8 0.2 copy.7
  96.0 0.5 slice.1268
  97.9 10.3 %all-gather.7.cloned.1.call-done = f32[20,3,8,1024]{3,2,1,0:T(8,128)} async-done(((f32[5,3,8,1024]{3,2,1,0:T(8,128)}), f32[20,3,8,1024]{3,2,1,0:T(8,128)}) %all-gather.7.cloned.1.call-update) | async-done | bytes 1966096 | tf_op jit(solution)/shard_map/all_gather | solution.py:211
  108.2 1.1 fusion.238
  109.2 3.8 %collective-permute-start.4 = (f32[5,3,8,1024]{3,2,1,0:T(8,128)S(1)}, f32[5,3,8,1024]{3,2,1,0:T(8,128)S(1)}, u32[]{:S(2)}, u32[]{:S(2)}) collective-permute-start(f32[5,3,8,1024]{3,2,1,0:T(8,128)S(1)} %fusion.238), channel_id=1, source_target_pairs={{0,132},{4,136},{8,140},{12,144},{16,148},{20,152},{24,156},{28,16... | collective-permute-start | bytes 1474568 | tf_op jit(solution)/shard_map/ppermute | solution.py:227
  113.0 0.2 collective-permute-start.5
  113.3 1.1 constant_dynamic-slice_fusion
  114.4 0.5 slice.1271
  116.3 1.4 fusion.4.padded_ref
  117.6 7.1 %shard_map.37 = f32[5,4,8,1024]{3,2,1,0:T(8,128)} custom-call(f32[5,9,8,1024]{3,2,1,0:T(8,128)} %fusion.4.padded_ref), custom_call_target="tpu_custom_call" | custom-call | tf_op jit(solution)/shard_map/pallas_call | solution.py:254
  124.7 1.0 slice_select_fusion.1.edge_ref
  125.7 0.1 slice_reduce_fusion
  125.9 1.3 fusion.231
  127.2 0.1 maximum_select_fusion.1.partial_ref
  127.4 0.2 fusion.186
  127.7 10.1 %collective-permute-done.5 = f32[5,3,8,1024]{3,2,1,0:T(8,128)} collective-permute-done((f32[5,3,8,1024]{3,2,1,0:T(8,128)S(1)}, f32[5,3,8,1024]{3,2,1,0:T(8,128)}, u32[]{:S(2)}, u32[]{:S(2)}) %collective-permute-start.5) | collective-permute-done | bytes 491552 | tf_op jit(solution)/shard_map/ppermute | solution.py:227
  137.8 1.4 fusion.6
  139.1 0.2 fusion.7
  139.4 0.8 pad_maximum_fusion.1.ghost_ref
  140.2 6.4 %shard_map.38 = f32[5,6,8,1024]{3,2,1,0:T(8,128)} custom-call(s32[1]{0:T(128)} %bitcast.flag_ref, f32[5,6,8,1024]{3,2,1,0:T(8,128)} %section_ref.1, f32[5,3,8,1024]{3,2,1,0:T(8,128)} %pad_maximum_fusion.1.ghost_ref, f32[5,1,8,1024]{3,2,1,0:T(8,128)} %copy-done.7, f32[5,6,8,1024]{3,2,1,0:T(8,128)} %copy-done.5), custom_call_target="tpu_custom_call", output_to_operand_aliasing={{}: (4, {})} | custom-call | tf_op jit(solution)/shard_map/pallas_call | solution.py:290
  (41 shorter events, 1.0 us)
Async XLA Ops:
  6.5 9.9 %copy-start = (f32[5,6,8,1024]{3,2,1,0:T(8,128)S(1)}, f32[5,6,8,1024]{3,2,1,0:T(8,128)}, u32[]{:S(2)}) copy-start(f32[5,6,8,1024]{3,2,1,0:T(8,128)} %section_ref.1) | copy-start | bytes 2949124
  6.5 65.2 %all-gather.5.cloned.1.call-start = ((), (), s32[]{:S(2)}) async-start(), calls=%async_computation | async-start | bytes 4423680 | tf_op jit(solution)/shard_map/all_gather | solution.py:201
  9.1 23.6 %collective-permute-start = (f32[5,6,3,1024]{3,2,1,0:T(4,128)}, f32[5,6,3,1024]{3,2,1,0:T(4,128)}, u32[]{:S(2)}, u32[]{:S(2)}) collective-permute-start(f32[5,6,3,1024]{3,2,1,0:T(4,128)} %get-tuple-element.140), channel_id=1, source_target_pairs={{0,1},{1,2},{2,3},{4,5},{5,6},{6,7},{8,9},{9,10},{10,11},{12,13},{... | collective-permute-start | bytes 1105928 | tf_op jit(solution)/shard_map/ppermute | solution.py:21
  13.7 20.3 %collective-permute-start.1 = (f32[5,6,3,1024]{3,2,1,0:T(4,128)S(1)}, f32[5,6,3,1024]{3,2,1,0:T(4,128)}, u32[]{:S(2)}, u32[]{:S(2)}) collective-permute-start(f32[5,6,3,1024]{3,2,1,0:T(4,128)S(1)} %get-tuple-element.141), channel_id=1, source_target_pairs={{1,0},{2,1},{3,2},{5,4},{6,5},{7,6},{9,8},{10,9},{11,10},{13,12},{... | collective-permute-start | bytes 1105928 | tf_op jit(solution)/shard_map/ppermute | solution.py:23
  17.3 90.9 %all-gather.7.cloned.1.call-start = ((), (), s32[]{:S(2)}) async-start(), calls=%async_computation.1 | async-start | bytes 2457600 | tf_op jit(solution)/shard_map/all_gather | solution.py:211
  17.4 13.8 %collective-permute-start.2 = (f32[5,6,8,3]{3,2,1,0:T(8,128)S(1)}, f32[5,6,8,3]{3,2,1,0:T(8,128)}, u32[]{:S(2)}, u32[]{:S(2)}) collective-permute-start(f32[5,6,8,3]{3,2,1,0:T(8,128)S(1)} %get-tuple-element.133), channel_id=1, source_target_pairs={{0,4},{4,8},{8,12},{12,16},{16,20},{20,24},{24,28},{28,32},{32,36}... | collective-permute-start | bytes 8648 | tf_op jit(solution)/shard_map/ppermute | solution.py:21
  18.4 12.8 %collective-permute-start.3 = (f32[5,6,8,3]{3,2,1,0:T(8,128)S(1)}, f32[5,6,8,3]{3,2,1,0:T(8,128)}, u32[]{:S(2)}, u32[]{:S(2)}) collective-permute-start(f32[5,6,8,3]{3,2,1,0:T(8,128)S(1)} %get-tuple-element.132), channel_id=1, source_target_pairs={{4,0},{8,4},{12,8},{16,12},{20,16},{24,20},{28,24},{32,28},{36,32}... | collective-permute-start | bytes 8648 | tf_op jit(solution)/shard_map/ppermute | solution.py:23
  65.3 1.3 copy-start.1
  73.5 1.8 %copy-start.4 = (f32[5,3,8,1024]{3,2,1,0:T(8,128)}, f32[5,3,8,1024]{3,2,1,0:T(8,128)S(1)}, u32[]{:S(2)}) copy-start(f32[5,3,8,1024]{3,2,1,0:T(8,128)S(1)} %rev.2) | copy-start | bytes 1474564
  77.2 1.2 copy-start.3
  92.1 1.8 %copy-start.6 = (f32[5,6,8,1024]{3,2,1,0:T(8,128)S(1)}, f32[5,6,8,1024]{3,2,1,0:T(8,128)}, u32[]{:S(2)}) copy-start(f32[5,6,8,1024]{3,2,1,0:T(8,128)} %param.11) | copy-start | bytes 2949124
  93.6 1.6 %copy-start.2 = (f32[5,6,9,1024]{3,2,1,0:T(8,128)S(1)}, f32[5,6,9,1024]{3,2,1,0:T(8,128)}, u32[]{:S(2)}) copy-start(f32[5,6,9,1024]{3,2,1,0:T(8,128)} %copy-done.1) | copy-start | bytes 3317764
  96.0 20.2 %copy-start.8 = (f32[5,1,8,1024]{3,2,1,0:T(8,128)S(1)}, f32[5,1,8,1024]{3,2,1,0:T(8,128)}, u32[]{:S(2)}) copy-start(f32[5,1,8,1024]{3,2,1,0:T(8,128)} %get-tuple-element.130) | copy-start | bytes 491524
  96.0 20.2 %copy-start.9 = (f32[5,1,8,1024]{3,2,1,0:T(8,128)S(1)}, f32[5,1,8,1024]{3,2,1,0:T(8,128)}, u32[]{:S(2)}) copy-start(f32[5,1,8,1024]{3,2,1,0:T(8,128)} %get-tuple-element.131) | copy-start | bytes 491524
  109.2 18.4 %collective-permute-start.4 = (f32[5,3,8,1024]{3,2,1,0:T(8,128)S(1)}, f32[5,3,8,1024]{3,2,1,0:T(8,128)S(1)}, u32[]{:S(2)}, u32[]{:S(2)}) collective-permute-start(f32[5,3,8,1024]{3,2,1,0:T(8,128)S(1)} %fusion.238), channel_id=1, source_target_pairs={{0,132},{4,136},{8,140},{12,144},{16,148},{20,152},{24,156},{28,16... | collective-permute-start | bytes 1474568 | tf_op jit(solution)/shard_map/ppermute | solution.py:227
  113.0 24.7 %collective-permute-start.5 = (f32[5,3,8,1024]{3,2,1,0:T(8,128)S(1)}, f32[5,3,8,1024]{3,2,1,0:T(8,128)}, u32[]{:S(2)}, u32[]{:S(2)}) collective-permute-start(f32[5,3,8,1024]{3,2,1,0:T(8,128)S(1)} %fusion.238), channel_id=1, source_target_pairs={{0,128},{4,132},{8,136},{12,140},{16,144},{20,148},{24,152},{28,15... | collective-permute-start | bytes 1474568 | tf_op jit(solution)/shard_map/ppermute | solution.py:227
  125.7 1.6 %copy-start.7 = (f32[5,1,8,1024]{3,2,1,0:T(8,128)}, f32[5,1,8,1024]{3,2,1,0:T(8,128)S(1)}, u32[]{:S(2)}) copy-start(f32[5,1,8,1024]{3,2,1,0:T(8,128)S(1)} %slice_select_fusion.1.edge_ref) | copy-start | bytes 491524
  127.4 12.0 %copy-start.5 = (f32[5,6,8,1024]{3,2,1,0:T(8,128)}, f32[5,6,8,1024]{3,2,1,0:T(8,128)S(1)}, u32[]{:S(2)}) copy-start(f32[5,6,8,1024]{3,2,1,0:T(8,128)S(1)} %maximum_select_fusion.1.partial_ref) | copy-start | bytes 2949124
Sparse Core Ops, SparseCore 0:
  17.4 54.2 all-gather.4
  77.2 30.8 all-gather.6
